TPU v7x, 256 devices: a whole 4x4x8 slice. The times are simulated.
256 devices in a mesh: lon: 16 (over z, core), lat: 16 (over x, y).
Axes of the slice: x: 4, y: 4, z: 8, core: 2. Of those that a mesh axis runs over, the one named last changes fastest.
Arguments:
- zonal_current: float32 [10, 1024, 2048], P(None, 'lat', 'lon'), may hold values from -6 to 6
- meridional_current: float32 [10, 1024, 2048], P(None, 'lat', 'lon'), may hold values from -6 to 6
- thermal_anomaly: float32 [10, 1024, 2048], P(None, 'lat', 'lon'), may hold values from -6 to 6
- saltiness_anomaly: float32 [10, 1024, 2048], P(None, 'lat', 'lon'), may hold values from -6 to 6
- water_indicator: int32 [10, 1024, 2048], P(None, 'lat', 'lon'), may hold values 0 or 1
- bottom_layer_index: int32 [1024, 2048], P('lat', 'lon'), may hold values from 1 to 10
- water_elevation: float32 [1024, 2048], P('lat', 'lon'), may hold values from -6 to 6
- zonal_barotropic_flow: float32 [1024, 2048], P('lat', 'lon'), may hold values from -6 to 6
- meridional_barotropic_flow: float32 [1024, 2048], P('lat', 'lon'), may hold values from -6 to 6
- planetary_spin_factor: float32 [1024, 2048], P('lat', 'lon'), may hold values from -1.5 to 1.5
Outputs:
- u_next: float32 [10, 1024, 2048], P(None, 'lat', 'lon')
- v_next: float32 [10, 1024, 2048], P(None, 'lat', 'lon')
- temperature_next: float32 [10, 1024, 2048], P(None, 'lat', 'lon')
- salinity_next: float32 [10, 1024, 2048], P(None, 'lat', 'lon')
- surface_next: float32 [1024, 2048], P('lat', 'lon')
- u_bar_next: float32 [1024, 2048], P('lat', 'lon')
- v_bar_next: float32 [1024, 2048], P('lat', 'lon')
All inputs are finite; a program needn't handle non-finite values. No bound on the sum of `water_indicator` on one device may be relied on, other than what follows from the above.
Results may differ from a plain program's by a relative error of at most 0.00002.
Values sent between devices are 32-bit elements; how exact they have to be, the bound alone decides.
No kernel may reach another device: no remote copies, remote signals or barrier semaphores. Data moves between devices by JAX's collectives and lax.ppermute only.
A program may use at most 64 MiB of HBM per device.

v0:
```python
import jax
import jax.numpy as jnp
from jax import lax
from jax.sharding import PartitionSpec as P

SUBSTEPS = 4


advect_scale = 0.25
viscous_scale = 0.02
pressure_scale = 0.5
rotation_scale = 0.3
thermal_scale = 0.2
haline_scale = 0.8
surface_depth = 0.25
gravity_scale = 0.3
divergence_scale = 0.3


def padded(cells, sides, width, closed):
    for axis, dim in sides:
        count = lax.axis_size(axis)
        ends = count if closed else count - 1
        head = lax.slice_in_dim(cells, 0, width, axis=dim)
        tail = lax.slice_in_dim(cells, cells.shape[dim] - width, cells.shape[dim], axis=dim)
        cells = jnp.concatenate(
            [
                lax.ppermute(tail, axis, [(i, (i + 1) % count) for i in range(ends)]),
                cells,
                lax.ppermute(head, axis, [((i + 1) % count, i) for i in range(ends)]),
            ],
            axis=dim,
        )
    return cells


def swapped(block, axis, bit):
    count = lax.axis_size(axis)
    route = []
    for low in range(count):
        high = low | 1 << bit
        if high != low and high < count:
            route += [(low, high), (high, low)]
    return lax.ppermute(block, axis, route)


def east_west(field):
    return 0.5 * (field[..., 1:-1, 2:] - field[..., 1:-1, :-2])


def north_south(field):
    return 0.5 * (field[..., 2:, 1:-1] - field[..., :-2, 1:-1])


def laplace(field):
    return (
        field[..., 1:-1, 2:]
        + field[..., 1:-1, :-2]
        + field[..., 2:, 1:-1]
        + field[..., :-2, 1:-1]
        - 4.0 * field[..., 1:-1, 1:-1]
    )


def extend_block(fields_in, rim_width, parity):
    sign_table = jnp.array(parity, dtype=jnp.float32).reshape(-1, 1, 1, 1)
    row_count = fields_in.shape[2]
    extended = padded(fields_in, (("lat", 2),), rim_width, False)
    top_rows = jnp.flip(fields_in[:, :, row_count - rim_width :, :], axis=(2, 3)) * sign_table
    lon_count = lax.axis_size("lon")
    mirrored = top_rows
    for bit_number in range(lon_count.bit_length() - 1):
        mirrored = swapped(mirrored, "lon", bit_number)
    is_top = lax.axis_index("lat") == lax.axis_size("lat") - 1
    upper_rows = extended[:, :, row_count + rim_width :, :] + jnp.where(is_top, mirrored, 0.0)
    extended = jnp.concatenate([extended[:, :, : row_count + rim_width, :], upper_rows], axis=2)
    return padded(extended, (("lon", 3),), rim_width, True)


def march_marine_state(
    zonal_current,
    meridional_current,
    thermal_anomaly,
    saltiness_anomaly,
    water_indicator,
    bottom_layer_index,
    water_elevation,
    zonal_barotropic_flow,
    meridional_barotropic_flow,
    planetary_spin_factor,
    extend,
):
    levels = zonal_current.shape[0]
    level_index = jnp.arange(levels, dtype=jnp.int32)[:, None, None]
    water_point_total = water_indicator.astype(jnp.float32) * (
        level_index < bottom_layer_index[None]
    ).astype(jnp.float32)
    state_arrays = (
        jnp.stack([zonal_current, meridional_current, thermal_anomaly, saltiness_anomaly])
        * water_point_total[None]
    )
    extended = extend(state_arrays, 2, (-1.0, -1.0, 1.0, 1.0))
    inner_cycle = extended[:, :, 1:-1, 1:-1]
    smooth = laplace(laplace(extended))
    advect = east_west(inner_cycle[0][None] * inner_cycle[2:4]) + north_south(
        inner_cycle[1][None] * inner_cycle[2:4]
    )
    thickness = ((jnp.arange(levels, dtype=jnp.float32) + 1.0) * (2.0 / (levels * (levels + 1))))[
        :, None, None
    ]
    density = haline_scale * inner_cycle[3] - thermal_scale * inner_cycle[2]
    weight = density * thickness
    pressure = jnp.cumsum(weight, axis=0) - 0.5 * weight
    u_old = state_arrays[0]
    v_old = state_arrays[1]
    u_star = (
        u_old
        + rotation_scale * planetary_spin_factor * v_old
        - pressure_scale * east_west(pressure)
        - viscous_scale * smooth[0]
    ) * water_point_total
    v_star = (
        v_old
        - rotation_scale * planetary_spin_factor * u_old
        - pressure_scale * north_south(pressure)
        - viscous_scale * smooth[1]
    ) * water_point_total
    tracers = (
        state_arrays[2:4] - advect_scale * advect - viscous_scale * smooth[2:4]
    ) * water_point_total[None]
    layer_weight = thickness * water_point_total
    column = surface_depth + jnp.sum(layer_weight, axis=0)

    def depth_mean(field):
        return jnp.sum(layer_weight * field, axis=0) / column

    mean_u = depth_mean(u_star)
    mean_v = depth_mean(v_star)
    force_u = (mean_u - depth_mean(u_old)) / SUBSTEPS
    force_v = (mean_v - depth_mean(v_old)) / SUBSTEPS
    wet_column = jnp.max(water_point_total, axis=0)
    surface = water_elevation
    u_bar = zonal_barotropic_flow
    v_bar = meridional_barotropic_flow
    for substep in range(SUBSTEPS):
        surface_ext = extend(surface[None, None], 1, (1.0,))[0, 0]
        u_new = (
            u_bar
            - gravity_scale * east_west(surface_ext)
            + rotation_scale * planetary_spin_factor * v_bar
            + force_u
        ) * wet_column
        v_new = (
            v_bar
            - gravity_scale * north_south(surface_ext)
            - rotation_scale * planetary_spin_factor * u_bar
            + force_v
        ) * wet_column
        u_bar = u_new
        v_bar = v_new
        transport = extend(jnp.stack([column * u_bar, column * v_bar])[:, None], 1, (-1.0, -1.0))[
            :, 0
        ]
        surface = (
            surface - divergence_scale * (east_west(transport[0]) + north_south(transport[1]))
        ) * wet_column
    u_next = (u_star - mean_u + u_bar) * water_point_total
    v_next = (v_star - mean_v + v_bar) * water_point_total
    return (u_next, v_next, tracers[0], tracers[1], surface, u_bar, v_bar)


def local(
    zonal_current,
    meridional_current,
    thermal_anomaly,
    saltiness_anomaly,
    water_indicator,
    bottom_layer_index,
    water_elevation,
    zonal_barotropic_flow,
    meridional_barotropic_flow,
    planetary_spin_factor,
):
    return march_marine_state(
        zonal_current,
        meridional_current,
        thermal_anomaly,
        saltiness_anomaly,
        water_indicator,
        bottom_layer_index,
        water_elevation,
        zonal_barotropic_flow,
        meridional_barotropic_flow,
        planetary_spin_factor,
        extend_block,
    )


def solution(mesh):
    return jax.shard_map(
        local,
        mesh=mesh,
        in_specs=(
            P(None, "lat", "lon"),
            P(None, "lat", "lon"),
            P(None, "lat", "lon"),
            P(None, "lat", "lon"),
            P(None, "lat", "lon"),
            P("lat", "lon"),
            P("lat", "lon"),
            P("lat", "lon"),
            P("lat", "lon"),
            P("lat", "lon"),
        ),
        out_specs=(
            P(None, "lat", "lon"),
            P(None, "lat", "lon"),
            P(None, "lat", "lon"),
            P(None, "lat", "lon"),
            P("lat", "lon"),
            P("lat", "lon"),
            P("lat", "lon"),
        ),
        check_vma=False,
    )
```

profile of v0, /device:TPU:3, one launch (start us, length us, event | category | flops | bytes accessed | tf_op | source)
XLA Modules:
  0.0 321.6 jit_solution(8847340028898352134)
XLA Ops:
  1.6 3.2 collective-permute-start.8
  5.9 4.2 %collective-permute-start.9 = (f32[1,1,1,128]{2,3,1,0:T(8,128)S(1)}, f32[1,1,1,128]{2,3,1,0:T(8,128)S(1)}, u32[]{:S(2)}, u32[]{:S(2)}) collective-permute-start(f32[1,1,1,128]{2,3,1,0:T(8,128)S(1)} %get-tuple-element.110), channel_id=1, source_target_pairs={{1,0},{2,1},{3,2},{4,3},{5,4},{6,5},{7,6},{8,7},{9,8},{10,9},{11,1... | collective-permute-start | bytes 1544 | tf_op jit(solution)/shard_map/ppermute | solution.py:30
  25.2 5.6 %collective-permute-start.13 = (f32[1,1,1,128]{2,3,1,0:T(8,128)S(1)}, f32[1,1,1,128]{2,3,1,0:T(8,128)S(1)}, u32[]{:S(2)}, u32[]{:S(2)}) collective-permute-start(f32[1,1,1,128]{2,3,1,0:T(8,128)S(1)} %collective-permute-done.12), channel_id=1, source_target_pairs={{0,128},{128,0},{16,144},{144,16},{32,160},{160,32},{48,176},{176,... | collective-permute-start | bytes 1544 | tf_op jit(solution)/shard_map/ppermute | solution.py:44
  31.5 5.1 %collective-permute-start.1 = (f32[4,10,2,128]{3,0,2,1:T(4,128)S(1)}, f32[4,10,2,128]{3,0,2,1:T(4,128)S(1)}, u32[]{:S(2)}, u32[]{:S(2)}) collective-permute-start(f32[4,10,2,128]{3,0,2,1:T(4,128)S(1)} %copy.100), channel_id=1, source_target_pairs={{1,0},{2,1},{3,2},{4,3},{5,4},{6,5},{7,6},{8,7},{9,8},{10,9},{11,1... | collective-permute-start | bytes 122888 | tf_op jit(solution)/shard_map/ppermute | solution.py:30
  37.3 3.4 %collective-permute-done.4 = f32[4,10,2,128]{3,0,2,1:T(4,128)S(1)} collective-permute-done((f32[4,10,2,128]{3,0,2,1:T(4,128)S(1)}, f32[4,10,2,128]{3,0,2,1:T(4,128)S(1)}, u32[]{:S(2)}, u32[]{:S(2)}) %collective-permute-start.4) | collective-permute-done | bytes 40992 | tf_op jit(solution)/shard_map/ppermute | solution.py:44
  41.3 4.1 %collective-permute-start.14 = (f32[1,1,66,1]{2,3,1,0:T(1,128)S(1)}, f32[1,1,66,1]{2,3,1,0:T(1,128)S(1)}, u32[]{:S(2)}, u32[]{:S(2)}) collective-permute-start(f32[1,1,66,1]{2,3,1,0:T(1,128)S(1)} %get-tuple-element.91), channel_id=1, source_target_pairs={{0,16},{16,32},{32,48},{48,64},{64,80},{80,96},{96,112},{112,128},... | collective-permute-start | bytes 800 | tf_op jit(solution)/shard_map/ppermute | solution.py:28
  52.4 6.1 %collective-permute-start.7 = (f32[4,10,68,2]{2,0,3,1:T(4,128)S(1)}, f32[4,10,68,2]{2,0,3,1:T(4,128)S(1)}, u32[]{:S(2)}, u32[]{:S(2)}) collective-permute-start(f32[4,10,68,2]{2,0,3,1:T(4,128)S(1)} %copy.106), channel_id=1, source_target_pairs={{16,0},{32,16},{48,32},{64,48},{80,64},{96,80},{112,96},{128,112},... | collective-permute-start | bytes 65288 | tf_op jit(solution)/shard_map/ppermute | solution.py:30
  63.1 3.7 %pad_maximum_fusion.6 = f32[4,10,68,132]{3,2,1,0:T(8,128)S(1)} fusion(f32[4,10,68,2]{3,2,1,0:T(8,128)} %copy.108, f32[4,10,2,128]{3,2,1,0:T(2,128)S(1)} %copy_add_fusion, f32[4,10,64,128]{3,2,1,0:T(8,128)} %copy-done, f32[4,10,2,128]{3,2,1,0:T(2,128)S(1)} %copy.104, f32[4,10,68,2]{3,2,1,0:T(8,128)} %copy.107), kind=kLoop, calls=%fused_computation.11 | loop fusion | flops 1436160 | bytes 2872320 | tf_op jit(solution)/shard_map/concatenate | solution.py:26
  66.9 3.7 %fusion = f32[4,10,66,130]{3,2,1,0:T(8,128)S(1)} fusion(f32[4,10,68,132]{3,2,1,0:T(8,128)S(1)} %pad_maximum_fusion.6, f32[4,10,68,2]{3,2,1,0:T(8,128)S(1)} %copy-done.3, f32[4,10,2,128]{3,2,1,0:T(2,128)S(1)} %copy_add_fusion, f32[4,10,64,128]{3,2,1,0:T(8,128)S(1)} %copy-done.1, f32[4,10,2,128]{3,2,1,0:T(2,128)S(1)} %copy.104, f32[4,10,68,2]{3,2,1,0:T(8,128)S(1)} %copy-done.4), kind=kLoop, calls=%fused_computation.1 | loop fusion | flops 3775200 | bytes 6927360 | tf_op jit(solution)/shard_map/sub | solution.py:57
  87.5 3.5 %collective-permute-start.18 = (f32[2,1,1,128]{2,3,0,1:T(8,128)S(1)}, f32[2,1,1,128]{2,3,0,1:T(8,128)S(1)}, u32[]{:S(2)}, u32[]{:S(2)}) collective-permute-start(f32[2,1,1,128]{2,3,0,1:T(8,128)S(1)} %broadcast_multiply_fusion.3), channel_id=1, source_target_pairs={{0,16},{16,0},{32,48},{48,32},{64,80},{80,64},{96,112},{112,96},{1... | collective-permute-start | bytes 3080 | tf_op jit(solution)/shard_map/ppermute | solution.py:44
  92.0 4.7 %collective-permute-done.19 = f32[2,1,1,128]{2,3,0,1:T(8,128)S(1)} collective-permute-done((f32[2,1,1,128]{2,3,0,1:T(8,128)S(1)}, f32[2,1,1,128]{2,3,0,1:T(8,128)S(1)}, u32[]{:S(2)}, u32[]{:S(2)}) %collective-permute-start.19) | collective-permute-done | bytes 1056 | tf_op jit(solution)/shard_map/ppermute | solution.py:44
  98.6 7.2 %collective-permute-done.20 = f32[2,1,1,128]{2,3,0,1:T(8,128)S(1)} collective-permute-done((f32[2,1,1,128]{2,3,0,1:T(8,128)S(1)}, f32[2,1,1,128]{2,3,0,1:T(8,128)S(1)}, u32[]{:S(2)}, u32[]{:S(2)}) %collective-permute-start.20) | collective-permute-done | bytes 1056 | tf_op jit(solution)/shard_map/ppermute | solution.py:44
  109.2 7.1 %collective-permute-done.21 = f32[2,1,1,128]{2,3,0,1:T(8,128)S(1)} collective-permute-done((f32[2,1,1,128]{2,3,0,1:T(8,128)S(1)}, f32[2,1,1,128]{2,3,0,1:T(8,128)S(1)}, u32[]{:S(2)}, u32[]{:S(2)}) %collective-permute-start.21) | collective-permute-done | bytes 1056 | tf_op jit(solution)/shard_map/ppermute | solution.py:44
  123.9 3.1 collective-permute-done.27
  127.0 3.9 %collective-permute-start.28 = (f32[1,1,1,128]{2,3,1,0:T(8,128)S(1)}, f32[1,1,1,128]{2,3,1,0:T(8,128)S(1)}, u32[]{:S(2)}, u32[]{:S(2)}) collective-permute-start(f32[1,1,1,128]{2,3,1,0:T(8,128)S(1)} %collective-permute-done.27), channel_id=1, source_target_pairs={{0,64},{64,0},{16,80},{80,16},{32,96},{96,32},{48,112},{112,48},{1... | collective-permute-start | bytes 1544 | tf_op jit(solution)/shard_map/ppermute | solution.py:44
  157.0 4.7 %collective-permute-done.35 = f32[2,1,1,128]{2,3,0,1:T(8,128)S(1)} collective-permute-done((f32[2,1,1,128]{2,3,0,1:T(8,128)S(1)}, f32[2,1,1,128]{2,3,0,1:T(8,128)S(1)}, u32[]{:S(2)}, u32[]{:S(2)}) %collective-permute-start.35) | collective-permute-done | bytes 1056 | tf_op jit(solution)/shard_map/ppermute | solution.py:44
  166.4 3.9 %collective-permute-done.36 = f32[2,1,1,128]{2,3,0,1:T(8,128)S(1)} collective-permute-done((f32[2,1,1,128]{2,3,0,1:T(8,128)S(1)}, f32[2,1,1,128]{2,3,0,1:T(8,128)S(1)}, u32[]{:S(2)}, u32[]{:S(2)}) %collective-permute-start.36) | collective-permute-done | bytes 1056 | tf_op jit(solution)/shard_map/ppermute | solution.py:44
  170.4 3.1 collective-permute-start.37
  175.4 6.7 %collective-permute-done.37 = f32[2,1,1,128]{2,3,0,1:T(8,128)S(1)} collective-permute-done((f32[2,1,1,128]{2,3,0,1:T(8,128)S(1)}, f32[2,1,1,128]{2,3,0,1:T(8,128)S(1)}, u32[]{:S(2)}, u32[]{:S(2)}) %collective-permute-start.37) | collective-permute-done | bytes 1056 | tf_op jit(solution)/shard_map/ppermute | solution.py:44
  190.5 3.1 collective-permute-done.43
  198.1 4.0 %collective-permute-start.45 = (f32[1,1,1,128]{2,3,1,0:T(8,128)S(1)}, f32[1,1,1,128]{2,3,1,0:T(8,128)S(1)}, u32[]{:S(2)}, u32[]{:S(2)}) collective-permute-start(f32[1,1,1,128]{2,3,1,0:T(8,128)S(1)} %collective-permute-done.44), channel_id=1, source_target_pairs={{0,128},{128,0},{16,144},{144,16},{32,160},{160,32},{48,176},{176,... | collective-permute-start | bytes 1544 | tf_op jit(solution)/shard_map/ppermute | solution.py:44
  205.3 3.8 %collective-permute-done.40 = f32[1,1,1,128]{2,3,1,0:T(8,128)S(1)} collective-permute-done((f32[1,1,1,128]{2,3,1,0:T(8,128)S(1)}, f32[1,1,1,128]{2,3,1,0:T(8,128)S(1)}, u32[]{:S(2)}, u32[]{:S(2)}) %collective-permute-start.40) | collective-permute-done | bytes 544 | tf_op jit(solution)/shard_map/ppermute | solution.py:28
  209.2 3.2 %collective-permute-start.46 = (f32[1,1,66,1]{2,3,1,0:T(1,128)S(1)}, f32[1,1,66,1]{2,3,1,0:T(1,128)S(1)}, u32[]{:S(2)}, u32[]{:S(2)}) collective-permute-start(f32[1,1,66,1]{2,3,1,0:T(1,128)S(1)} %get-tuple-element.87), channel_id=1, source_target_pairs={{0,16},{16,32},{32,48},{48,64},{64,80},{80,96},{96,112},{112,128},... | collective-permute-start | bytes 800 | tf_op jit(solution)/shard_map/ppermute | solution.py:28
  224.0 3.6 %collective-permute-done.51 = f32[2,1,1,128]{2,3,0,1:T(8,128)S(1)} collective-permute-done((f32[2,1,1,128]{2,3,0,1:T(8,128)S(1)}, f32[2,1,1,128]{2,3,0,1:T(8,128)S(1)}, u32[]{:S(2)}, u32[]{:S(2)}) %collective-permute-start.51) | collective-permute-done | bytes 1056 | tf_op jit(solution)/shard_map/ppermute | solution.py:44
  232.0 3.9 %collective-permute-done.52 = f32[2,1,1,128]{2,3,0,1:T(8,128)S(1)} collective-permute-done((f32[2,1,1,128]{2,3,0,1:T(8,128)S(1)}, f32[2,1,1,128]{2,3,0,1:T(8,128)S(1)}, u32[]{:S(2)}, u32[]{:S(2)}) %collective-permute-start.52) | collective-permute-done | bytes 1056 | tf_op jit(solution)/shard_map/ppermute | solution.py:44
  240.3 6.3 %collective-permute-done.53 = f32[2,1,1,128]{2,3,0,1:T(8,128)S(1)} collective-permute-done((f32[2,1,1,128]{2,3,0,1:T(8,128)S(1)}, f32[2,1,1,128]{2,3,0,1:T(8,128)S(1)}, u32[]{:S(2)}, u32[]{:S(2)}) %collective-permute-start.53) | collective-permute-done | bytes 1056 | tf_op jit(solution)/shard_map/ppermute | solution.py:44
  246.8 3.2 collective-permute-start.54
  256.7 3.1 collective-permute-done.59
  259.8 3.1 collective-permute-start.60
  290.7 3.1 collective-permute-done.67
  308.1 5.2 %collective-permute-done.69 = f32[2,1,1,128]{2,3,0,1:T(8,128)S(1)} collective-permute-done((f32[2,1,1,128]{2,3,0,1:T(8,128)S(1)}, f32[2,1,1,128]{2,3,0,1:T(8,128)S(1)}, u32[]{:S(2)}, u32[]{:S(2)}) %collective-permute-start.69) | collective-permute-done | bytes 1056 | tf_op jit(solution)/shard_map/ppermute | solution.py:44
  314.1 3.1 collective-permute-start.70
  (290 shorter events, 184.2 us)
Async XLA Ops:
  1.6 39.6 %collective-permute-start.8 = (f32[1,1,1,128]{2,3,1,0:T(8,128)S(1)}, f32[1,1,1,128]{2,3,1,0:T(8,128)S(1)}, u32[]{:S(2)}, u32[]{:S(2)}) collective-permute-start(f32[1,1,1,128]{2,3,1,0:T(8,128)S(1)} %get-tuple-element.109), channel_id=1, source_target_pairs={{0,1},{1,2},{2,3},{3,4},{4,5},{5,6},{6,7},{7,8},{8,9},{9,10},{10,1... | collective-permute-start | bytes 1544 | tf_op jit(solution)/shard_map/ppermute | solution.py:28
  4.9 10.7 %collective-permute-start.10 = (f32[1,1,1,128]{2,3,1,0:T(8,128)S(1)}, f32[1,1,1,128]{2,3,1,0:T(8,128)S(1)}, u32[]{:S(2)}, u32[]{:S(2)}) collective-permute-start(f32[1,1,1,128]{2,3,1,0:T(8,128)S(1)} %rev.31), channel_id=1, source_target_pairs={{0,16},{16,0},{32,48},{48,32},{64,80},{80,64},{96,112},{112,96},{1... | collective-permute-start | bytes 1544 | tf_op jit(solution)/shard_map/ppermute | solution.py:44
  5.9 25.6 %collective-permute-start.9 = (f32[1,1,1,128]{2,3,1,0:T(8,128)S(1)}, f32[1,1,1,128]{2,3,1,0:T(8,128)S(1)}, u32[]{:S(2)}, u32[]{:S(2)}) collective-permute-start(f32[1,1,1,128]{2,3,1,0:T(8,128)S(1)} %get-tuple-element.110), channel_id=1, source_target_pairs={{1,0},{2,1},{3,2},{4,3},{5,4},{6,5},{7,6},{8,7},{9,8},{10,9},{11,1... | collective-permute-start | bytes 1544 | tf_op jit(solution)/shard_map/ppermute | solution.py:30
  13.1 9.3 %collective-permute-start.2 = (f32[4,10,2,128]{3,0,2,1:T(4,128)S(1)}, f32[4,10,2,128]{3,0,2,1:T(4,128)S(1)}, u32[]{:S(2)}, u32[]{:S(2)}) collective-permute-start(f32[4,10,2,128]{3,0,2,1:T(4,128)S(1)} %copy.101), channel_id=1, source_target_pairs={{0,16},{16,0},{32,48},{48,32},{64,80},{80,64},{96,112},{112,96},{1... | collective-permute-start | bytes 122888 | tf_op jit(solution)/shard_map/ppermute | solution.py:44
  13.5 32.3 %collective-permute-start = (f32[4,10,2,128]{3,0,2,1:T(4,128)S(1)}, f32[4,10,2,128]{3,0,2,1:T(4,128)S(1)}, u32[]{:S(2)}, u32[]{:S(2)}) collective-permute-start(f32[4,10,2,128]{3,0,2,1:T(4,128)S(1)} %copy.99), channel_id=1, source_target_pairs={{0,1},{1,2},{2,3},{3,4},{4,5},{5,6},{6,7},{7,8},{8,9},{9,10},{10,1... | collective-permute-start | bytes 122888 | tf_op jit(solution)/shard_map/ppermute | solution.py:28
  22.5 14.2 %collective-permute-start.3 = (f32[4,10,2,128]{3,0,2,1:T(4,128)S(1)}, f32[4,10,2,128]{3,0,2,1:T(4,128)S(1)}, u32[]{:S(2)}, u32[]{:S(2)}) collective-permute-start(f32[4,10,2,128]{3,0,2,1:T(4,128)S(1)} %collective-permute-done.2), channel_id=1, source_target_pairs={{0,32},{32,0},{16,48},{48,16},{64,96},{96,64},{80,112},{112,80},{1... | collective-permute-start | bytes 122888 | tf_op jit(solution)/shard_map/ppermute | solution.py:44
  25.2 12.2 %collective-permute-start.13 = (f32[1,1,1,128]{2,3,1,0:T(8,128)S(1)}, f32[1,1,1,128]{2,3,1,0:T(8,128)S(1)}, u32[]{:S(2)}, u32[]{:S(2)}) collective-permute-start(f32[1,1,1,128]{2,3,1,0:T(8,128)S(1)} %collective-permute-done.12), channel_id=1, source_target_pairs={{0,128},{128,0},{16,144},{144,16},{32,160},{160,32},{48,176},{176,... | collective-permute-start | bytes 1544 | tf_op jit(solution)/shard_map/ppermute | solution.py:44
  31.5 14.3 %collective-permute-start.1 = (f32[4,10,2,128]{3,0,2,1:T(4,128)S(1)}, f32[4,10,2,128]{3,0,2,1:T(4,128)S(1)}, u32[]{:S(2)}, u32[]{:S(2)}) collective-permute-start(f32[4,10,2,128]{3,0,2,1:T(4,128)S(1)} %copy.100), channel_id=1, source_target_pairs={{1,0},{2,1},{3,2},{4,3},{5,4},{6,5},{7,6},{8,7},{9,8},{10,9},{11,1... | collective-permute-start | bytes 122888 | tf_op jit(solution)/shard_map/ppermute | solution.py:30
  41.3 17.2 %collective-permute-start.14 = (f32[1,1,66,1]{2,3,1,0:T(1,128)S(1)}, f32[1,1,66,1]{2,3,1,0:T(1,128)S(1)}, u32[]{:S(2)}, u32[]{:S(2)}) collective-permute-start(f32[1,1,66,1]{2,3,1,0:T(1,128)S(1)} %get-tuple-element.91), channel_id=1, source_target_pairs={{0,16},{16,32},{32,48},{48,64},{64,80},{80,96},{96,112},{112,128},... | collective-permute-start | bytes 800 | tf_op jit(solution)/shard_map/ppermute | solution.py:28
  45.3 13.2 %collective-permute-start.15 = (f32[1,1,66,1]{2,3,1,0:T(1,128)S(1)}, f32[1,1,66,1]{2,3,1,0:T(1,128)S(1)}, u32[]{:S(2)}, u32[]{:S(2)}) collective-permute-start(f32[1,1,66,1]{2,3,1,0:T(1,128)S(1)} %get-tuple-element.92), channel_id=1, source_target_pairs={{16,0},{32,16},{48,32},{64,48},{80,64},{96,80},{112,96},{128,112},... | collective-permute-start | bytes 800 | tf_op jit(solution)/shard_map/ppermute | solution.py:30
  52.4 9.0 %collective-permute-start.7 = (f32[4,10,68,2]{2,0,3,1:T(4,128)S(1)}, f32[4,10,68,2]{2,0,3,1:T(4,128)S(1)}, u32[]{:S(2)}, u32[]{:S(2)}) collective-permute-start(f32[4,10,68,2]{2,0,3,1:T(4,128)S(1)} %copy.106), channel_id=1, source_target_pairs={{16,0},{32,16},{48,32},{64,48},{80,64},{96,80},{112,96},{128,112},... | collective-permute-start | bytes 65288 | tf_op jit(solution)/shard_map/ppermute | solution.py:30
  96.7 9.1 %collective-permute-start.20 = (f32[2,1,1,128]{2,3,0,1:T(8,128)S(1)}, f32[2,1,1,128]{2,3,0,1:T(8,128)S(1)}, u32[]{:S(2)}, u32[]{:S(2)}) collective-permute-start(f32[2,1,1,128]{2,3,0,1:T(8,128)S(1)} %collective-permute-done.19), channel_id=1, source_target_pairs={{0,64},{64,0},{16,80},{80,16},{32,96},{96,32},{48,112},{112,48},{1... | collective-permute-start | bytes 3080 | tf_op jit(solution)/shard_map/ppermute | solution.py:44
  96.7 12.5 %collective-permute-start.17 = (f32[2,1,1,128]{2,3,0,1:T(8,128)}, f32[2,1,1,128]{2,3,0,1:T(8,128)S(1)}, u32[]{:S(2)}, u32[]{:S(2)}) collective-permute-start(f32[2,1,1,128]{2,3,0,1:T(8,128)} %get-tuple-element.102), channel_id=1, source_target_pairs={{1,0},{2,1},{3,2},{4,3},{5,4},{6,5},{7,6},{8,7},{9,8},{10,9},{11,1... | collective-permute-start | bytes 3080 | tf_op jit(solution)/shard_map/ppermute | solution.py:30
  105.8 10.5 %collective-permute-start.21 = (f32[2,1,1,128]{2,3,0,1:T(8,128)S(1)}, f32[2,1,1,128]{2,3,0,1:T(8,128)S(1)}, u32[]{:S(2)}, u32[]{:S(2)}) collective-permute-start(f32[2,1,1,128]{2,3,0,1:T(8,128)S(1)} %collective-permute-done.20), channel_id=1, source_target_pairs={{0,128},{128,0},{16,144},{144,16},{32,160},{160,32},{48,176},{176,... | collective-permute-start | bytes 3080 | tf_op jit(solution)/shard_map/ppermute | solution.py:44
  107.3 9.1 %collective-permute-start.16 = (f32[2,1,1,128]{2,3,0,1:T(8,128)}, f32[2,1,1,128]{2,3,0,1:T(8,128)S(1)}, u32[]{:S(2)}, u32[]{:S(2)}) collective-permute-start(f32[2,1,1,128]{2,3,0,1:T(8,128)} %get-tuple-element.101), channel_id=1, source_target_pairs={{0,1},{1,2},{2,3},{3,4},{4,5},{5,6},{6,7},{7,8},{8,9},{9,10},{10,1... | collective-permute-start | bytes 3080 | tf_op jit(solution)/shard_map/ppermute | solution.py:28
  132.8 7.2 %collective-permute-start.29 = (f32[1,1,1,128]{2,3,1,0:T(8,128)S(1)}, f32[1,1,1,128]{2,3,1,0:T(8,128)S(1)}, u32[]{:S(2)}, u32[]{:S(2)}) collective-permute-start(f32[1,1,1,128]{2,3,1,0:T(8,128)S(1)} %collective-permute-done.28), channel_id=1, source_target_pairs={{0,128},{128,0},{16,144},{144,16},{32,160},{160,32},{48,176},{176,... | collective-permute-start | bytes 1544 | tf_op jit(solution)/shard_map/ppermute | solution.py:44
  135.6 7.4 %collective-permute-start.24 = (f32[1,1,1,128]{2,3,1,0:T(8,128)S(1)}, f32[1,1,1,128]{2,3,1,0:T(8,128)S(1)}, u32[]{:S(2)}, u32[]{:S(2)}) collective-permute-start(f32[1,1,1,128]{2,3,1,0:T(8,128)S(1)} %get-tuple-element.107), channel_id=1, source_target_pairs={{0,1},{1,2},{2,3},{3,4},{4,5},{5,6},{6,7},{7,8},{8,9},{9,10},{10,1... | collective-permute-start | bytes 1544 | tf_op jit(solution)/shard_map/ppermute | solution.py:28
  161.7 8.7 %collective-permute-start.36 = (f32[2,1,1,128]{2,3,0,1:T(8,128)S(1)}, f32[2,1,1,128]{2,3,0,1:T(8,128)S(1)}, u32[]{:S(2)}, u32[]{:S(2)}) collective-permute-start(f32[2,1,1,128]{2,3,0,1:T(8,128)S(1)} %collective-permute-done.35), channel_id=1, source_target_pairs={{0,64},{64,0},{16,80},{80,16},{32,96},{96,32},{48,112},{112,48},{1... | collective-permute-start | bytes 3080 | tf_op jit(solution)/shard_map/ppermute | solution.py:44
  164.5 10.9 %collective-permute-start.33 = (f32[2,1,1,128]{2,3,0,1:T(8,128)}, f32[2,1,1,128]{2,3,0,1:T(8,128)S(1)}, u32[]{:S(2)}, u32[]{:S(2)}) collective-permute-start(f32[2,1,1,128]{2,3,0,1:T(8,128)} %get-tuple-element.100), channel_id=1, source_target_pairs={{1,0},{2,1},{3,2},{4,3},{5,4},{6,5},{7,6},{8,7},{9,8},{10,9},{11,1... | collective-permute-start | bytes 3080 | tf_op jit(solution)/shard_map/ppermute | solution.py:30
  170.4 11.8 %collective-permute-start.37 = (f32[2,1,1,128]{2,3,0,1:T(8,128)S(1)}, f32[2,1,1,128]{2,3,0,1:T(8,128)S(1)}, u32[]{:S(2)}, u32[]{:S(2)}) collective-permute-start(f32[2,1,1,128]{2,3,0,1:T(8,128)S(1)} %collective-permute-done.36), channel_id=1, source_target_pairs={{0,128},{128,0},{16,144},{144,16},{32,160},{160,32},{48,176},{176,... | collective-permute-start | bytes 3080 | tf_op jit(solution)/shard_map/ppermute | solution.py:44
  173.5 8.7 %collective-permute-start.32 = (f32[2,1,1,128]{2,3,0,1:T(8,128)}, f32[2,1,1,128]{2,3,0,1:T(8,128)S(1)}, u32[]{:S(2)}, u32[]{:S(2)}) collective-permute-start(f32[2,1,1,128]{2,3,0,1:T(8,128)} %get-tuple-element.99), channel_id=1, source_target_pairs={{0,1},{1,2},{2,3},{3,4},{4,5},{5,6},{6,7},{7,8},{8,9},{9,10},{10,1... | collective-permute-start | bytes 3080 | tf_op jit(solution)/shard_map/ppermute | solution.py:28
  196.1 8.5 %collective-permute-start.41 = (f32[1,1,1,128]{2,3,1,0:T(8,128)}, f32[1,1,1,128]{2,3,1,0:T(8,128)S(1)}, u32[]{:S(2)}, u32[]{:S(2)}) collective-permute-start(f32[1,1,1,128]{2,3,1,0:T(8,128)} %get-tuple-element.106), channel_id=1, source_target_pairs={{1,0},{2,1},{3,2},{4,3},{5,4},{6,5},{7,6},{8,7},{9,8},{10,9},{11,1... | collective-permute-start | bytes 1544 | tf_op jit(solution)/shard_map/ppermute | solution.py:30
  198.1 7.2 %collective-permute-start.45 = (f32[1,1,1,128]{2,3,1,0:T(8,128)S(1)}, f32[1,1,1,128]{2,3,1,0:T(8,128)S(1)}, u32[]{:S(2)}, u32[]{:S(2)}) collective-permute-start(f32[1,1,1,128]{2,3,1,0:T(8,128)S(1)} %collective-permute-done.44), channel_id=1, source_target_pairs={{0,128},{128,0},{16,144},{144,16},{32,160},{160,32},{48,176},{176,... | collective-permute-start | bytes 1544 | tf_op jit(solution)/shard_map/ppermute | solution.py:44
  227.6 8.3 %collective-permute-start.52 = (f32[2,1,1,128]{2,3,0,1:T(8,128)S(1)}, f32[2,1,1,128]{2,3,0,1:T(8,128)S(1)}, u32[]{:S(2)}, u32[]{:S(2)}) collective-permute-start(f32[2,1,1,128]{2,3,0,1:T(8,128)S(1)} %collective-permute-done.51), channel_id=1, source_target_pairs={{0,64},{64,0},{16,80},{80,16},{32,96},{96,32},{48,112},{112,48},{1... | collective-permute-start | bytes 3080 | tf_op jit(solution)/shard_map/ppermute | solution.py:44
  230.1 10.2 %collective-permute-start.49 = (f32[2,1,1,128]{2,3,0,1:T(8,128)}, f32[2,1,1,128]{2,3,0,1:T(8,128)S(1)}, u32[]{:S(2)}, u32[]{:S(2)}) collective-permute-start(f32[2,1,1,128]{2,3,0,1:T(8,128)} %get-tuple-element.98), channel_id=1, source_target_pairs={{1,0},{2,1},{3,2},{4,3},{5,4},{6,5},{7,6},{8,7},{9,8},{10,9},{11,1... | collective-permute-start | bytes 3080 | tf_op jit(solution)/shard_map/ppermute | solution.py:30
  235.9 10.7 %collective-permute-start.53 = (f32[2,1,1,128]{2,3,0,1:T(8,128)S(1)}, f32[2,1,1,128]{2,3,0,1:T(8,128)S(1)}, u32[]{:S(2)}, u32[]{:S(2)}) collective-permute-start(f32[2,1,1,128]{2,3,0,1:T(8,128)S(1)} %collective-permute-done.52), channel_id=1, source_target_pairs={{0,128},{128,0},{16,144},{144,16},{32,160},{160,32},{48,176},{176,... | collective-permute-start | bytes 3080 | tf_op jit(solution)/shard_map/ppermute | solution.py:44
  238.4 8.3 %collective-permute-start.48 = (f32[2,1,1,128]{2,3,0,1:T(8,128)}, f32[2,1,1,128]{2,3,0,1:T(8,128)S(1)}, u32[]{:S(2)}, u32[]{:S(2)}) collective-permute-start(f32[2,1,1,128]{2,3,0,1:T(8,128)} %get-tuple-element.97), channel_id=1, source_target_pairs={{0,1},{1,2},{2,3},{3,4},{4,5},{5,6},{6,7},{7,8},{8,9},{9,10},{10,1... | collective-permute-start | bytes 3080 | tf_op jit(solution)/shard_map/ppermute | solution.py:28
  262.9 8.3 %collective-permute-start.57 = (f32[1,1,1,128]{2,3,1,0:T(8,128)}, f32[1,1,1,128]{2,3,1,0:T(8,128)S(1)}, u32[]{:S(2)}, u32[]{:S(2)}) collective-permute-start(f32[1,1,1,128]{2,3,1,0:T(8,128)} %get-tuple-element.104), channel_id=1, source_target_pairs={{1,0},{2,1},{3,2},{4,3},{5,4},{6,5},{7,6},{8,7},{9,8},{10,9},{11,1... | collective-permute-start | bytes 1544 | tf_op jit(solution)/shard_map/ppermute | solution.py:30
  293.8 8.1 %collective-permute-start.68 = (f32[2,1,1,128]{2,3,0,1:T(8,128)S(1)}, f32[2,1,1,128]{2,3,0,1:T(8,128)S(1)}, u32[]{:S(2)}, u32[]{:S(2)}) collective-permute-start(f32[2,1,1,128]{2,3,0,1:T(8,128)S(1)} %collective-permute-done.67), channel_id=1, source_target_pairs={{0,64},{64,0},{16,80},{80,16},{32,96},{96,32},{48,112},{112,48},{1... | collective-permute-start | bytes 3080 | tf_op jit(solution)/shard_map/ppermute | solution.py:44
  297.1 10.9 %collective-permute-start.65 = (f32[2,1,1,128]{2,3,0,1:T(8,128)S(1)}, f32[2,1,1,128]{2,3,0,1:T(8,128)S(1)}, u32[]{:S(2)}, u32[]{:S(2)}) collective-permute-start(f32[2,1,1,128]{2,3,0,1:T(8,128)S(1)} %copy-done.28), channel_id=1, source_target_pairs={{1,0},{2,1},{3,2},{4,3},{5,4},{6,5},{7,6},{8,7},{9,8},{10,9},{11,1... | collective-permute-start | bytes 3080 | tf_op jit(solution)/shard_map/ppermute | solution.py:30
  302.0 11.3 %collective-permute-start.69 = (f32[2,1,1,128]{2,3,0,1:T(8,128)S(1)}, f32[2,1,1,128]{2,3,0,1:T(8,128)S(1)}, u32[]{:S(2)}, u32[]{:S(2)}) collective-permute-start(f32[2,1,1,128]{2,3,0,1:T(8,128)S(1)} %collective-permute-done.68), channel_id=1, source_target_pairs={{0,128},{128,0},{16,144},{144,16},{32,160},{160,32},{48,176},{176,... | collective-permute-start | bytes 3080 | tf_op jit(solution)/shard_map/ppermute | solution.py:44
  305.9 8.1 %collective-permute-start.64 = (f32[2,1,1,128]{2,3,0,1:T(8,128)S(1)}, f32[2,1,1,128]{2,3,0,1:T(8,128)S(1)}, u32[]{:S(2)}, u32[]{:S(2)}) collective-permute-start(f32[2,1,1,128]{2,3,0,1:T(8,128)S(1)} %copy-done.18), channel_id=1, source_target_pairs={{0,1},{1,2},{2,3},{3,4},{4,5},{5,6},{6,7},{7,8},{8,9},{9,10},{10,1... | collective-permute-start | bytes 3080 | tf_op jit(solution)/shard_map/ppermute | solution.py:28
  (73 other events, 578.0 us)
where the time goes:
time: 323 us; the launch traced here: 322 us
  starting transfers between devices  138 us (43%)
  waiting for transfers between devices  117 us (36%)
  local copies, waits for them, and re-layouts  33.2 us (10%)
  other arithmetic  31.9 us (10%)
    ppermute x36, waiting for transfers between devices, swapped(): return lax.ppermute(block, axis, route)  87.1 us
    ppermute x36, starting transfers between devices, swapped(): return lax.ppermute(block, axis, route)  65 us
    ppermute x18, starting transfers between devices, padded(): lax.ppermute(tail, axis, [(i, (i + 1) % count) for i in range(ends)])  41.5 us
    ppermute x18, starting transfers between devices, padded(): lax.ppermute(head, axis, [((i + 1) % count, i) for i in range(ends)])  31.3 us
    ppermute x18, waiting for transfers between devices, padded(): lax.ppermute(head, axis, [((i + 1) % count, i) for i in range(ends)])  15 us
    ppermute x18, waiting for transfers between devices, padded(): lax.ppermute(tail, axis, [(i, (i + 1) % count) for i in range(ends)])  14.9 us
    unnamed x77, local copies, waits for them, and re-layouts  10.7 us
    slice x12, local copies, waits for them, and re-layouts, padded(): lax.slice_in_dim(cells, cells.shape[dim] - width, cells.shape[dim], axis=...  9.14 us
  transfers between devices with their start and end apart: 72, of which 48 were waited for; matrix products, arithmetic and copies ran while one was open for 5% of the time, Pallas kernels for 0%

commit v1 on v0

v1 whole, which is shorter than its diff:
```python
import functools

import jax
import jax.numpy as jnp
from jax import lax
from jax.experimental import pallas as pl
from jax.experimental.pallas import tpu as pltpu
from jax.sharding import PartitionSpec as P

SUBSTEPS = 4
LEVELS = 10
ROWS = 64
COLS = 128
RIM = 9
PLANES = 54
PER_SLAB = 14
SLABS = 4
TAIL = PLANES * 8
ROW_SLAB = TAIL + 24
SLAB_ROWS = 88
TOP = 16
HIGH = 96

advect_scale = 0.25
viscous_scale = 0.02
pressure_scale = 0.5
rotation_scale = 0.3
thermal_scale = 0.2
haline_scale = 0.8
surface_depth = 0.25
gravity_scale = 0.3
divergence_scale = 0.3

F32 = jnp.float32
SIGNS = [-1.0] * 20 + [1.0] * 30 + [1.0, -1.0, -1.0, 1.0]
THICK = [(k + 1.0) * (2.0 / (LEVELS * (LEVELS + 1))) for k in range(LEVELS)]


def whole(shape):
    return pl.BlockSpec(shape, lambda i: (0,) * len(shape))


def call(kernel, name, out, scratch, flops, *args, in_specs=None):
    return pl.pallas_call(
        kernel,
        grid=(1,),
        out_shape=[jax.ShapeDtypeStruct(s, F32) for s in out],
        in_specs=in_specs or [whole(a.shape) for a in args],
        out_specs=[whole(s) for s in out],
        scratch_shapes=scratch,
        name=name,
        cost_estimate=pl.CostEstimate(flops=flops, bytes_accessed=2_000_000, transcendentals=0),
        compiler_params=pltpu.CompilerParams(vmem_limit_bytes=48 * 1024 * 1024),
    )(*args)


def lane_iota(rows=8):
    return lax.broadcasted_iota(jnp.int32, (rows, COLS), 1)


def sub_iota():
    return lax.broadcasted_iota(jnp.int32, (8, COLS), 0)


def flip_lanes(x):
    return jnp.take_along_axis(x, COLS - 1 - lax.broadcasted_iota(jnp.int32, x.shape, 1), axis=1, mode="promise_in_bounds")


def flip_rows(x):
    return jnp.take_along_axis(x, 7 - lax.broadcasted_iota(jnp.int32, x.shape, 0), axis=0, mode="promise_in_bounds")


def lat_place():
    index = lax.axis_index("lat")
    return index % 2 == 0, index == lax.axis_size("lat") - 1


def pack_rows(u0, u1, v0, v1, t0, t1, s0, s1, w0, w1, bottom, eta, ub, vb, cor, a_ref, b_ref, low9, high9):
    even, top = lat_place()
    low9[...] = jnp.zeros((24, COLS), F32)
    high9[...] = jnp.zeros((24, COLS), F32)
    b0 = bottom[0:16, :]
    b1 = bottom[ROWS - 16 : ROWS, :]

    def put(p, down, up):
        fold = SIGNS[p] * flip_rows(flip_lanes(up))
        a_ref[8 * p : 8 * p + 8, :] = jnp.where(even, up, down)
        b_ref[8 * p : 8 * p + 8, :] = jnp.where(even, down, jnp.where(top, fold, up))

    for k in range(LEVELS):
        wl = jnp.where(k < b0, w0[k].astype(F32), 0.0)
        wh = jnp.where(k < b1, w1[k].astype(F32), 0.0)
        for f, (lo, hi) in enumerate(((u0, u1), (v0, v1), (t0, t1), (s0, s1))):
            p = 10 * f + k
            low = lo[k] * wl
            high = hi[k] * wh
            put(p, low[0:8], high[8:16])
            if f < 2:
                low9[p : p + 1, :] = low[8:9]
                high9[p : p + 1, :] = high[7:8]
        put(40 + k, wl[0:8], wh[8:16])
    for j, ref in enumerate((eta, ub, vb, cor)):
        put(50 + j, ref[0:8, :], ref[ROWS - 8 : ROWS, :])
    for r in range(0, 24, 8):
        down = low9[r : r + 8, :]
        up = high9[r : r + 8, :]
        fold = -flip_lanes(up)
        a_ref[TAIL + r : TAIL + r + 8, :] = jnp.where(even, up, down)
        b_ref[TAIL + r : TAIL + r + 8, :] = jnp.where(even, down, jnp.where(top, fold, up))


def put_columns(val, p, lane, east, west):
    q, j = divmod(p, PER_SLAB)
    here = (lane >= RIM * j) & (lane < RIM * j + RIM)
    east[q] = jnp.where(here, pltpu.roll(val, RIM * j, 1), east[q])
    west[q] = jnp.where(here, pltpu.roll(val, (RIM * j + RIM) % COLS, 1), west[q])


def pack_centre(u, v, t, s, w, bottom, eta, ub, vb, cor, x_ref, east_ref, west_ref):
    lane = lane_iota()

    def tile(i, carry):
        rows = pl.ds(pl.multiple_of(8 * i, 8), 8)
        deep = bottom[rows, :]
        zero = jnp.zeros((8, COLS), F32)
        east = [zero] * SLABS
        west = [zero] * SLABS
        for k in range(LEVELS):
            wet = jnp.where(k < deep, w[k, rows, :].astype(F32), 0.0)
            for f, ref in enumerate((u, v, t, s)):
                val = ref[k, rows, :] * wet
                x_ref[10 * f + k, rows, :] = val
                put_columns(val, 10 * f + k, lane, east, west)
            x_ref[40 + k, rows, :] = wet
            put_columns(wet, 40 + k, lane, east, west)
        for j, ref in enumerate((eta, ub, vb, cor)):
            val = ref[rows, :]
            x_ref[50 + j, rows, :] = val
            put_columns(val, 50 + j, lane, east, west)
        for q in range(SLABS):
            east_ref[q, rows, :] = east[q]
            west_ref[q, rows, :] = west[q]
        return carry

    lax.fori_loop(0, ROWS // 8, tile, 0)


def pack_rims(a_ref, b_ref, ec, wc, e_ref, w_ref):
    even, _ = lat_place()
    lane = lane_iota()
    sub = sub_iota()
    zero = jnp.zeros((8, COLS), F32)
    for q in range(SLABS):
        e_ref[q, 16 : 16 + ROWS, :] = ec[q]
        w_ref[q, 16 : 16 + ROWS, :] = wc[q]

    def both(r, n):
        a = a_ref[r : r + n, :]
        b = b_ref[r : r + n, :]
        return jnp.where(even, b, a), jnp.where(even, a, b)

    packs = [([zero] * SLABS, [zero] * SLABS) for _ in range(3)]
    for p in range(PLANES):
        south, north = both(8 * p, 8)
        put_columns(south, p, lane, *packs[1])
        put_columns(north, p, lane, *packs[2])
        if p < 20:
            south, north = both(TAIL + p, 1)
            put_columns(jnp.where(sub == 0, south, north), p, lane, *packs[0])
    for at, (east, west) in zip((0, 8, 16 + ROWS), packs):
        for q in range(SLABS):
            e_ref[q, at : at + 8, :] = east[q]
            w_ref[q, at : at + 8, :] = west[q]


class Wide:
    def __init__(self, own, rim):
        self.own, self.rim = own, rim

    def with_other(self, other, op):
        if isinstance(other, Wide):
            return Wide(op(self.own, other.own), op(self.rim, other.rim))
        return Wide(op(self.own, other), op(self.rim, other))

    def __add__(self, other):
        return self.with_other(other, lambda a, b: a + b)

    def __sub__(self, other):
        return self.with_other(other, lambda a, b: a - b)

    def __mul__(self, other):
        return self.with_other(other, lambda a, b: a * b)

    __rmul__ = __mul__

    def __truediv__(self, other):
        return self.with_other(other, lambda a, b: a / b)


def east_of(x):
    last = lane_iota() == COLS - 1
    own = pltpu.roll(x.own, COLS - 1, 1)
    rim = pltpu.roll(x.rim, COLS - 1, 1)
    return Wide(jnp.where(last, rim, own), jnp.where(last, own, rim))


def west_of(x):
    first = lane_iota() == 0
    own = pltpu.roll(x.own, 1, 1)
    rim = pltpu.roll(x.rim, 1, 1)
    return Wide(jnp.where(first, rim, own), jnp.where(first, own, rim))


def sides(x):
    return east_of(x) + west_of(x)


def slope(x):
    return east_of(x) - west_of(x)


def step(x_ref, a_ref, b_ref, es, ws, u_out, v_out, t_out, s_out, eta_out, ub_out, vb_out,
         own, rim, us, vs, fu, fv, mu, mv, col, tu, tv):
    even, _ = lat_place()
    lane = lane_iota()

    def place(p, carry):
        own[p, TOP : TOP + ROWS, :] = x_ref[p]
        row = pl.multiple_of(8 * p, 8)
        a = a_ref[pl.ds(row, 8), :]
        b = b_ref[pl.ds(row, 8), :]
        own[p, 8:16, :] = jnp.where(even, b, a)
        own[p, TOP + ROWS : TOP + ROWS + 8, :] = jnp.where(even, a, b)
        return carry

    lax.fori_loop(0, PLANES, place, 0)
    for p in range(20):
        a = a_ref[TAIL + p : TAIL + p + 1, :]
        b = b_ref[TAIL + p : TAIL + p + 1, :]
        own[p, 7:8, :] = jnp.where(even, b, a)
        own[p, TOP + ROWS + 8 : TOP + ROWS + 9, :] = jnp.where(even, a, b)

    def unpack(j, carry):
        shift = RIM * j
        for q in range(SLABS):
            for r in range(0, SLAB_ROWS, 8):
                east = pltpu.roll(es[q, r : r + 8, :], lax.rem(COLS - shift, COLS), 1)
                west = pltpu.roll(ws[q, r : r + 8, :], lax.rem(2 * COLS - RIM - shift, COLS), 1)
                val = jnp.where(lane < RIM, east, jnp.where(lane >= COLS - RIM, west, 0.0))
                if r == 0:
                    rim[PER_SLAB * q + j, 7:8, :] = val[0:1]
                    rim[PER_SLAB * q + j, TOP + ROWS + 8 : TOP + ROWS + 9, :] = val[1:2]
                else:
                    rim[PER_SLAB * q + j, r : r + 8, :] = val
        return carry

    lax.fori_loop(0, PER_SLAB, unpack, 0)

    def wide(ref, at):
        return Wide(ref[0, at, :], ref[1, at, :])

    def keep(ref, at, x):
        ref[0, at, :] = x.own
        ref[1, at, :] = x.rim

    def momentum(i, carry):
        r0 = 8 * i + 8

        def at(p, d):
            rows = pl.ds(r0 + d, 8)
            return Wide(own[p, rows, :], rim[p, rows, :])

        spin = rotation_scale * at(53, 0)
        none = jnp.zeros((8, COLS), F32)
        zero = Wide(none, none)
        acc = acc_ns = sum_u = sum_v = diff_u = diff_v = depth = zero
        for k in range(LEVELS):
            wet = at(40 + k, 0)
            u = at(k, 0)
            v = at(10 + k, 0)
            smooth = []
            for p, c in ((k, u), (10 + k, v)):
                ns = at(p, 1) + at(p, -1)
                smooth.append(sides(sides(c) + 2.0 * ns - 8.0 * c) + (at(p, 2) + at(p, -2) - 8.0 * ns + 18.0 * c))
            half = (0.5 * THICK[k]) * (haline_scale * at(30 + k, 0) - thermal_scale * at(20 + k, 0))
            half_ns = (0.5 * THICK[k]) * (
                haline_scale * (at(30 + k, 1) - at(30 + k, -1)) - thermal_scale * (at(20 + k, 1) - at(20 + k, -1))
            )
            pressure = acc + half
            pressure_ns = acc_ns + half_ns
            acc = pressure + half
            acc_ns = pressure_ns + half_ns
            u_star = wet * (u + spin * v - (0.5 * pressure_scale) * slope(pressure) - viscous_scale * smooth[0])
            v_star = wet * (v - spin * u - (0.5 * pressure_scale) * pressure_ns - viscous_scale * smooth[1])
            us[k, pl.ds(pl.multiple_of(8 * i, 8), 8), :] = u_star.own
            vs[k, pl.ds(pl.multiple_of(8 * i, 8), 8), :] = v_star.own
            sum_u = sum_u + THICK[k] * u_star
            sum_v = sum_v + THICK[k] * v_star
            diff_u = diff_u + THICK[k] * (u_star - u)
            diff_v = diff_v + THICK[k] * (v_star - v)
            depth = depth + THICK[k] * wet
        column = depth + surface_depth
        here = pl.ds(pl.multiple_of(r0, 8), 8)
        keep(fu, here, diff_u / column * (1.0 / SUBSTEPS))
        keep(fv, here, diff_v / column * (1.0 / SUBSTEPS))
        mu[here, :] = sum_u.own / column.own
        mv[here, :] = sum_v.own / column.own
        keep(col, here, column)
        own[53, here, :] = spin.own
        rim[53, here, :] = spin.rim
        return carry

    lax.fori_loop(0, 10, momentum, 0)

    def flat(p, r):
        return Wide(own[p, r : r + 8, :], rim[p, r : r + 8, :])

    def wet_of(column):
        return Wide(jnp.where(column.own > surface_depth, 1.0, 0.0), jnp.where(column.rim > surface_depth, 1.0, 0.0))

    def substep(n, carry):
        for r in range(8, 88, 8):
            here = slice(r, r + 8)
            column = wide(col, here)
            wet = wet_of(column)
            u = flat(51, r)
            v = flat(52, r)
            spin = flat(53, r)
            un = wet * (u - (0.5 * gravity_scale) * slope(flat(50, r)) + spin * v + wide(fu, here))
            vn = wet * (v - (0.5 * gravity_scale) * (flat(50, r + 1) - flat(50, r - 1)) - spin * u + wide(fv, here))
            for p, x in ((51, un), (52, vn)):
                own[p, here, :] = x.own
                rim[p, here, :] = x.rim
            keep(tu, here, column * un)
            keep(tv, here, column * vn)
        for r in range(8, 88, 8):
            here = slice(r, r + 8)
            wet = wet_of(wide(col, here))
            flow = slope(wide(tu, here)) + (wide(tv, slice(r + 1, r + 9)) - wide(tv, slice(r - 1, r + 7)))
            eta = wet * (flat(50, r) - (0.5 * divergence_scale) * flow)
            own[50, here, :] = eta.own
            rim[50, here, :] = eta.rim
        return carry

    lax.fori_loop(0, SUBSTEPS, substep, 0)
    eta_out[...] = own[50, TOP : TOP + ROWS, :]
    ub_out[...] = own[51, TOP : TOP + ROWS, :]
    vb_out[...] = own[52, TOP : TOP + ROWS, :]

    def finish(i, carry):
        r0 = 8 * i + TOP
        here = pl.ds(pl.multiple_of(r0, 8), 8)
        rows = pl.ds(pl.multiple_of(8 * i, 8), 8)
        star = pl.ds(pl.multiple_of(8 * i + 8, 8), 8)

        def at(p, d):
            return Wide(own[p, pl.ds(r0 + d, 8), :], rim[p, pl.ds(r0 + d, 8), :])

        gain_u = own[51, here, :] - mu[here, :]
        gain_v = own[52, here, :] - mv[here, :]
        for k in range(LEVELS):
            wet = own[40 + k, here, :]
            u_out[k, rows, :] = us[k, star, :] + wet * gain_u
            v_out[k, rows, :] = vs[k, star, :] + wet * gain_v
            u = at(k, 0)
            vn = own[10 + k, pl.ds(r0 + 1, 8), :]
            vsouth = own[10 + k, pl.ds(r0 - 1, 8), :]
            for p, out in ((20 + k, t_out), (30 + k, s_out)):
                c = at(p, 0)
                n = at(p, 1)
                s = at(p, -1)
                far = own[p, pl.ds(r0 + 2, 8), :] + own[p, pl.ds(r0 - 2, 8), :]
                ns = n + s
                inner = sides(c) + 2.0 * ns - 8.0 * c
                smooth = sides(inner).own + (far - 8.0 * ns.own + 18.0 * c.own)
                advect = slope(u * c).own + (vn * n.own - vsouth * s.own)
                out[k, rows, :] = wet * (c.own - (0.5 * advect_scale) * advect - viscous_scale * smooth)
        return carry

    lax.fori_loop(0, ROWS // 8, finish, 0)


def colour(parity, lats, lons):
    pairs = []
    for lat in range(lats):
        for lon in range(lons):
            if (lat + parity) % 2 == 0:
                to = (lon, lat + 1) if lat + 1 < lats else (lons - 1 - lon, lat)
            elif lat > 0:
                to = (lon, lat - 1)
            else:
                continue
            pairs.append((lon * lats + lat, to[0] * lats + to[1]))
    return pairs


def local(u, v, t, s, w, bottom, eta, ub, vb, cor):
    lats = lax.axis_size("lat")
    lons = lax.axis_size("lon")
    ends = []
    for _ in range(5):
        ends.append(pl.BlockSpec((LEVELS, 16, COLS), lambda i: (0, 0, 0)))
        ends.append(pl.BlockSpec((LEVELS, 16, COLS), lambda i: (0, ROWS // 16 - 1, 0)))
    flat = whole((ROWS, COLS))
    a, b = call(
        pack_rows, "pack_rows", [(ROW_SLAB, COLS)] * 2, [pltpu.VMEM((24, COLS), F32)] * 2, 1_000_000,
        u, u, v, v, t, t, s, s, w, w, bottom, eta, ub, vb, cor, in_specs=ends + [flat] * 5,
    )
    a = lax.ppermute(a, ("lon", "lat"), colour(0, lats, lons))
    b = lax.ppermute(b, ("lon", "lat"), colour(1, lats, lons))
    x, ec, wc = call(
        pack_centre, "pack_centre", [(PLANES, ROWS, COLS)] + [(SLABS, ROWS, COLS)] * 2, [], 10_000_000,
        u, v, t, s, w, bottom, eta, ub, vb, cor,
    )
    e, west = call(pack_rims, "pack_rims", [(SLABS, SLAB_ROWS, COLS)] * 2, [], 1_000_000, a, b, ec, wc)
    e = lax.ppermute(e, "lon", [((i + 1) % lons, i) for i in range(lons)])
    west = lax.ppermute(west, "lon", [(i, (i + 1) % lons) for i in range(lons)])
    cube = (LEVELS, ROWS, COLS)
    plane = (ROWS, COLS)
    wide = pltpu.VMEM((2, HIGH, COLS), F32)
    thin = pltpu.VMEM((HIGH, COLS), F32)
    star = pltpu.VMEM((LEVELS, 80, COLS), F32)
    planes = pltpu.VMEM((SLABS * PER_SLAB, HIGH, COLS), F32)
    return tuple(
        call(
            step, "step", [cube] * 4 + [plane] * 3,
            [planes, planes, star, star, wide, wide, thin, thin, wide, wide, wide],
            50_000_000, x, a, b, e, west,
        )
    )


def solution(mesh):
    deep = P(None, "lat", "lon")
    flat = P("lat", "lon")
    return jax.shard_map(
        local,
        mesh=mesh,
        in_specs=(deep,) * 5 + (flat,) * 5,
        out_specs=(deep,) * 4 + (flat,) * 3,
        check_vma=False,
    )
```

time: 323 us -> 57.1 us (0.18)
  the two profiles are of different devices: /device:TPU:3 before, /device:TPU:30 now
where the time goes in v1:
time: 57.1 us; the launch traced here: 56.5 us
  Pallas kernels  20.7 us (36%)
  waiting for transfers between devices  15.3 us (27%)
  starting transfers between devices  11.2 us (20%)
  local copies, waits for them, and re-layouts  8.64 us (15%)
  between operations  0.69 us (1%)
    pallas_call x4, Pallas kernels, call(): pl.pallas_call(kernel, grid=(1,), out_shape=[jax.ShapeDtypeStruct(s, F32)...  20.7 us
    ppermute x1, waiting for transfers between devices, local(): b = lax.ppermute(b, ('lon', 'lat'), colour(1, lats, lons))  9.17 us
    unnamed x20, local copies, waits for them, and re-layouts  8.64 us
    ppermute x1, starting transfers between devices, local(): b = lax.ppermute(b, ('lon', 'lat'), colour(1, lats, lons))  6.91 us
    ppermute x1, starting transfers between devices, local(): e = lax.ppermute(e, 'lon', [((i + 1) % lons, i) for i in range(lons)])  3.42 us
    ppermute x1, waiting for transfers between devices, local(): west = lax.ppermute(west, 'lon', [(i, (i + 1) % lons) for i in range(lons)])  3.12 us
    ppermute x1, waiting for transfers between devices, local(): e = lax.ppermute(e, 'lon', [((i + 1) % lons, i) for i in range(lons)])  3.01 us
  transfers between devices with their start and end apart: 4, of which 3 were waited for; matrix products, arithmetic and copies ran while one was open for 0% of the time, Pallas kernels for 3%

profile of v1, /device:TPU:30, one launch (start us, length us, event | category | flops | bytes accessed | tf_op | source)
XLA Modules:
  0.0 56.5 jit_solution(9069052194290098002)
XLA Ops:
  0.6 0.0 copy-start
  0.6 1.0 %copy-done = f32[10,64,128]{2,1,0:T(8,128)S(1)} copy-done((f32[10,64,128]{2,1,0:T(8,128)S(1)}, f32[10,64,128]{2,1,0:T(8,128)}, u32[]{:S(2)}) %copy-start) | copy-done | bytes 327704
  1.6 0.0 copy-start.1
  1.6 1.0 %copy-done.1 = f32[10,64,128]{2,1,0:T(8,128)S(1)} copy-done((f32[10,64,128]{2,1,0:T(8,128)S(1)}, f32[10,64,128]{2,1,0:T(8,128)}, u32[]{:S(2)}) %copy-start.1) | copy-done | bytes 327704
  2.6 0.0 copy-start.2
  2.6 1.0 %copy-done.2 = f32[10,64,128]{2,1,0:T(8,128)S(1)} copy-done((f32[10,64,128]{2,1,0:T(8,128)S(1)}, f32[10,64,128]{2,1,0:T(8,128)}, u32[]{:S(2)}) %copy-start.2) | copy-done | bytes 327704
  3.6 0.0 copy-start.3
  3.6 1.0 %copy-done.3 = f32[10,64,128]{2,1,0:T(8,128)S(1)} copy-done((f32[10,64,128]{2,1,0:T(8,128)S(1)}, f32[10,64,128]{2,1,0:T(8,128)}, u32[]{:S(2)}) %copy-start.3) | copy-done | bytes 327704
  4.5 0.0 copy-start.4
  4.5 1.0 %copy-done.4 = s32[10,64,128]{2,1,0:T(8,128)S(1)} copy-done((s32[10,64,128]{2,1,0:T(8,128)S(1)}, s32[10,64,128]{2,1,0:T(8,128)}, u32[]{:S(2)}) %copy-start.4) | copy-done | bytes 327704
  5.5 0.0 copy-start.5
  5.5 0.8 %copy-done.5 = s32[64,128]{1,0:T(8,128)S(1)} copy-done((s32[64,128]{1,0:T(8,128)S(1)}, s32[64,128]{1,0:T(8,128)}, u32[]{:S(2)}) %copy-start.5) | copy-done | bytes 32792
  6.3 0.0 copy-start.6
  6.3 0.8 %copy-done.6 = f32[64,128]{1,0:T(8,128)S(1)} copy-done((f32[64,128]{1,0:T(8,128)S(1)}, f32[64,128]{1,0:T(8,128)}, u32[]{:S(2)}) %copy-start.6) | copy-done | bytes 32792
  7.0 0.0 copy-start.7
  7.0 0.8 %copy-done.7 = f32[64,128]{1,0:T(8,128)S(1)} copy-done((f32[64,128]{1,0:T(8,128)S(1)}, f32[64,128]{1,0:T(8,128)}, u32[]{:S(2)}) %copy-start.7) | copy-done | bytes 32792
  7.8 0.0 copy-start.8
  7.8 0.8 %copy-done.8 = f32[64,128]{1,0:T(8,128)S(1)} copy-done((f32[64,128]{1,0:T(8,128)S(1)}, f32[64,128]{1,0:T(8,128)}, u32[]{:S(2)}) %copy-start.8) | copy-done | bytes 32792
  8.5 0.0 copy-start.9
  8.5 0.8 %copy-done.9 = f32[64,128]{1,0:T(8,128)S(1)} copy-done((f32[64,128]{1,0:T(8,128)S(1)}, f32[64,128]{1,0:T(8,128)}, u32[]{:S(2)}) %copy-start.9) | copy-done | bytes 32792
  9.3 0.1 pack_rows.1
  9.4 0.8 %collective-permute-start = (f32[456,128]{1,0:T(8,128)S(1)}, f32[456,128]{1,0:T(8,128)S(1)}, u32[]{:S(2)}, u32[]{:S(2)}) collective-permute-start(f32[456,128]{1,0:T(8,128)S(1)} %get-tuple-element.15), channel_id=1, source_target_pairs={{0,1},{16,17},{32,33},{48,49},{64,65},{80,81},{96,97},{112,113},{1... | collective-permute-start | bytes 700424 | tf_op jit(solution)/shard_map/ppermute | solution.py:409
  10.3 6.9 %collective-permute-start.1 = (f32[456,128]{1,0:T(8,128)S(1)}, f32[456,128]{1,0:T(8,128)S(1)}, u32[]{:S(2)}, u32[]{:S(2)}) collective-permute-start(f32[456,128]{1,0:T(8,128)S(1)} %get-tuple-element.16), channel_id=1, source_target_pairs={{1,2},{17,18},{33,34},{49,50},{65,66},{81,82},{97,98},{113,114},{1... | collective-permute-start | bytes 700424 | tf_op jit(solution)/shard_map/ppermute | solution.py:410
  17.2 1.6 %pack_centre.1 = (f32[54,64,128]{2,1,0:T(8,128)S(1)}, f32[4,64,128]{2,1,0:T(8,128)S(1)}, f32[4,64,128]{2,1,0:T(8,128)S(1)}) custom-call(f32[10,64,128]{2,1,0:T(8,128)S(1)} %copy-done, f32[10,64,128]{2,1,0:T(8,128)S(1)} %copy-done.1, f32[10,64,128]{2,1,0:T(8,128)S(1)} %copy-done.2, f32[10,64,128]{2,1,0:T(8,128)S(1)} %copy-done.3, ...), custom_call_target="tpu_custom_call" | custom-call | flops 10000000 | bytes 2000000 | tf_op jit(solution)/shard_map/pack_centre/pallas_call | solution.py:44
  18.8 0.0 collective-permute-done.a_ref
  18.8 9.2 %collective-permute-done.1.b_ref = f32[456,128]{1,0:T(8,128)S(1)} collective-permute-done((f32[456,128]{1,0:T(8,128)S(1)}, f32[456,128]{1,0:T(8,128)S(1)}, u32[]{:S(2)}, u32[]{:S(2)}) %collective-permute-start.1) | collective-permute-done | bytes 233504 | tf_op jit(solution)/shard_map/ppermute | solution.py:410
  28.0 0.3 pack_rims.1
  28.3 3.4 %collective-permute-start.2 = (f32[4,88,128]{2,1,0:T(8,128)S(1)}, f32[4,88,128]{2,1,0:T(8,128)S(1)}, u32[]{:S(2)}, u32[]{:S(2)}) collective-permute-start(f32[4,88,128]{2,1,0:T(8,128)S(1)} %get-tuple-element.19), channel_id=1, source_target_pairs={{16,0},{32,16},{48,32},{64,48},{80,64},{96,80},{112,96},{128,112},... | collective-permute-start | bytes 540680 | tf_op jit(solution)/shard_map/ppermute | solution.py:416
  31.8 0.0 collective-permute-start.3
  31.8 3.0 %collective-permute-done.2.es = f32[4,88,128]{2,1,0:T(8,128)S(1)} collective-permute-done((f32[4,88,128]{2,1,0:T(8,128)S(1)}, f32[4,88,128]{2,1,0:T(8,128)S(1)}, u32[]{:S(2)}, u32[]{:S(2)}) %collective-permute-start.2) | collective-permute-done | bytes 180256 | tf_op jit(solution)/shard_map/ppermute | solution.py:416
  34.8 3.1 %collective-permute-done.3.ws = f32[4,88,128]{2,1,0:T(8,128)S(1)} collective-permute-done((f32[4,88,128]{2,1,0:T(8,128)S(1)}, f32[4,88,128]{2,1,0:T(8,128)S(1)}, u32[]{:S(2)}, u32[]{:S(2)}) %collective-permute-start.3) | collective-permute-done | bytes 180256 | tf_op jit(solution)/shard_map/ppermute | solution.py:417
  37.9 18.6 %step.1 = (f32[10,64,128]{2,1,0:T(8,128)}, f32[10,64,128]{2,1,0:T(8,128)}, f32[10,64,128]{2,1,0:T(8,128)}, f32[10,64,128]{2,1,0:T(8,128)}, f32[64,128]{1,0:T(8,1...) custom-call(f32[54,64,128]{2,1,0:T(8,128)S(1)} %get-tuple-element.14.x_ref, f32[456,128]{1,0:T(8,128)S(1)} %collective-permute-done.a_ref, ...), custom_call_target="tpu_custom_call" | custom-call | flops 50000000 | bytes 2000000 | tf_op jit(solution)/shard_map/step/pallas_call | solution.py:44
Async XLA Ops:
  0.6 1.0 %copy-start = (f32[10,64,128]{2,1,0:T(8,128)S(1)}, f32[10,64,128]{2,1,0:T(8,128)}, u32[]{:S(2)}) copy-start(f32[10,64,128]{2,1,0:T(8,128)} %u1_.1) | copy-start | bytes 983044
  1.6 1.0 %copy-start.1 = (f32[10,64,128]{2,1,0:T(8,128)S(1)}, f32[10,64,128]{2,1,0:T(8,128)}, u32[]{:S(2)}) copy-start(f32[10,64,128]{2,1,0:T(8,128)} %v1.1) | copy-start | bytes 983044
  2.6 1.0 %copy-start.2 = (f32[10,64,128]{2,1,0:T(8,128)S(1)}, f32[10,64,128]{2,1,0:T(8,128)}, u32[]{:S(2)}) copy-start(f32[10,64,128]{2,1,0:T(8,128)} %t1.1) | copy-start | bytes 983044
  3.6 1.0 %copy-start.3 = (f32[10,64,128]{2,1,0:T(8,128)S(1)}, f32[10,64,128]{2,1,0:T(8,128)}, u32[]{:S(2)}) copy-start(f32[10,64,128]{2,1,0:T(8,128)} %s1_.1) | copy-start | bytes 983044
  4.5 1.0 %copy-start.4 = (s32[10,64,128]{2,1,0:T(8,128)S(1)}, s32[10,64,128]{2,1,0:T(8,128)}, u32[]{:S(2)}) copy-start(s32[10,64,128]{2,1,0:T(8,128)} %w1.1) | copy-start | bytes 983044
  5.5 0.8 %copy-start.5 = (s32[64,128]{1,0:T(8,128)S(1)}, s32[64,128]{1,0:T(8,128)}, u32[]{:S(2)}) copy-start(s32[64,128]{1,0:T(8,128)} %bottom.3) | copy-start | bytes 98308
  6.3 0.8 %copy-start.6 = (f32[64,128]{1,0:T(8,128)S(1)}, f32[64,128]{1,0:T(8,128)}, u32[]{:S(2)}) copy-start(f32[64,128]{1,0:T(8,128)} %eta.3) | copy-start | bytes 98308
  7.0 0.8 %copy-start.7 = (f32[64,128]{1,0:T(8,128)S(1)}, f32[64,128]{1,0:T(8,128)}, u32[]{:S(2)}) copy-start(f32[64,128]{1,0:T(8,128)} %ub.3) | copy-start | bytes 98308
  7.8 0.8 %copy-start.8 = (f32[64,128]{1,0:T(8,128)S(1)}, f32[64,128]{1,0:T(8,128)}, u32[]{:S(2)}) copy-start(f32[64,128]{1,0:T(8,128)} %vb.3) | copy-start | bytes 98308
  8.5 0.8 %copy-start.9 = (f32[64,128]{1,0:T(8,128)S(1)}, f32[64,128]{1,0:T(8,128)}, u32[]{:S(2)}) copy-start(f32[64,128]{1,0:T(8,128)} %cor.3) | copy-start | bytes 98308
  9.4 9.4 %collective-permute-start = (f32[456,128]{1,0:T(8,128)S(1)}, f32[456,128]{1,0:T(8,128)S(1)}, u32[]{:S(2)}, u32[]{:S(2)}) collective-permute-start(f32[456,128]{1,0:T(8,128)S(1)} %get-tuple-element.15), channel_id=1, source_target_pairs={{0,1},{16,17},{32,33},{48,49},{64,65},{80,81},{96,97},{112,113},{1... | collective-permute-start | bytes 700424 | tf_op jit(solution)/shard_map/ppermute | solution.py:409
  10.3 17.7 %collective-permute-start.1 = (f32[456,128]{1,0:T(8,128)S(1)}, f32[456,128]{1,0:T(8,128)S(1)}, u32[]{:S(2)}, u32[]{:S(2)}) collective-permute-start(f32[456,128]{1,0:T(8,128)S(1)} %get-tuple-element.16), channel_id=1, source_target_pairs={{1,2},{17,18},{33,34},{49,50},{65,66},{81,82},{97,98},{113,114},{1... | collective-permute-start | bytes 700424 | tf_op jit(solution)/shard_map/ppermute | solution.py:410
  28.3 6.4 %collective-permute-start.2 = (f32[4,88,128]{2,1,0:T(8,128)S(1)}, f32[4,88,128]{2,1,0:T(8,128)S(1)}, u32[]{:S(2)}, u32[]{:S(2)}) collective-permute-start(f32[4,88,128]{2,1,0:T(8,128)S(1)} %get-tuple-element.19), channel_id=1, source_target_pairs={{16,0},{32,16},{48,32},{64,48},{80,64},{96,80},{112,96},{128,112},... | collective-permute-start | bytes 540680 | tf_op jit(solution)/shard_map/ppermute | solution.py:416
  31.8 6.1 %collective-permute-start.3 = (f32[4,88,128]{2,1,0:T(8,128)S(1)}, f32[4,88,128]{2,1,0:T(8,128)S(1)}, u32[]{:S(2)}, u32[]{:S(2)}) collective-permute-start(f32[4,88,128]{2,1,0:T(8,128)S(1)} %get-tuple-element.20), channel_id=1, source_target_pairs={{0,16},{16,32},{32,48},{48,64},{64,80},{80,96},{96,112},{112,128},... | collective-permute-start | bytes 540680 | tf_op jit(solution)/shard_map/ppermute | solution.py:417

commit v2 on v1

v2 whole, which is shorter than its diff:
```python
import functools

import jax
import jax.numpy as jnp
from jax import lax
from jax.experimental import pallas as pl
from jax.experimental.pallas import tpu as pltpu
from jax.sharding import PartitionSpec as P

SUBSTEPS = 4
LEVELS = 10
ROWS = 64
COLS = 128
U, V, D, WET, T, S, FLAT = 0, 10, 20, 30, 40, 50, 60
PLANES = 64
BLOCKS = 44
NINTH = 8 * BLOCKS
PAIRS = NINTH + 24
ROW_SLAB = PAIRS + 4 * LEVELS
STRIDE = 11
SLABS = 4
SLAB_ROWS = 88
TOP = 16
HIGH = 96
BAND = 40

advect_scale = 0.25
viscous_scale = 0.02
pressure_scale = 0.5
rotation_scale = 0.3
thermal_scale = 0.2
haline_scale = 0.8
surface_depth = 0.25
gravity_scale = 0.3
divergence_scale = 0.3

F32 = jnp.float32
SIGNS = [-1.0] * 20 + [1.0] * 20 + [1.0, -1.0, -1.0, 1.0]
THICK = [(k + 1.0) * (2.0 / (LEVELS * (LEVELS + 1))) for k in range(LEVELS)]
HBM = pl.BlockSpec(memory_space=pltpu.HBM)
VMEM = pl.BlockSpec(memory_space=pltpu.VMEM)
CUBE = (LEVELS, ROWS, COLS)
PLANE = (ROWS, COLS)


def call(kernel, name, out, scratch, flops, *args, ins=None, outs=None):
    return pl.pallas_call(
        kernel,
        out_shape=[jax.ShapeDtypeStruct(s, F32) for s in out],
        in_specs=ins or [VMEM] * len(args),
        out_specs=outs or [VMEM] * len(out),
        scratch_shapes=scratch,
        name=name,
        cost_estimate=pl.CostEstimate(flops=flops, bytes_accessed=2_000_000, transcendentals=0),
        compiler_params=pltpu.CompilerParams(vmem_limit_bytes=LIMIT),
    )(*args)


LIMIT = 40 * 1024 * 1024


def lanes(rows=8):
    return lax.broadcasted_iota(jnp.int32, (rows, COLS), 1)


def flip_lanes(x):
    return jnp.take_along_axis(x, COLS - 1 - lax.broadcasted_iota(jnp.int32, x.shape, 1), axis=1, mode="promise_in_bounds")


def flip_rows(x):
    return jnp.take_along_axis(x, 7 - lax.broadcasted_iota(jnp.int32, x.shape, 0), axis=0, mode="promise_in_bounds")


def turn(x, shift):
    return pltpu.roll(x, shift % COLS, 1)


def lat_place():
    index = lax.axis_index("lat")
    return index % 2 == 0, index == lax.axis_size("lat") - 1


def fetch(pairs, sem):
    copies = [pltpu.make_async_copy(src, dst, sem.at[n]) for n, (src, dst) in enumerate(pairs)]
    for copy in copies:
        copy.start()
    return copies


def pack_rows(u, v, t, s, w, bottom, eta, ub, vb, cor, a_ref, b_ref,
              u2, v2, t2, s2, w2, flat, deep, low9, high9, low2, high2, fold2, sem):
    even, top = lat_place()
    moves = []
    for src, dst in ((u, u2), (v, v2), (t, t2), (s, s2), (w, w2)):
        moves.append((src.at[:, 0:16, :], dst.at[0]))
        moves.append((src.at[:, ROWS - 16 : ROWS, :], dst.at[1]))
    for n, src in enumerate((eta, ub, vb, cor)):
        moves.append((src, flat.at[n]))
    moves.append((bottom, deep))
    for copy in fetch(moves, sem):
        copy.wait()
    low9[...] = jnp.zeros((24, COLS), F32)
    high9[...] = jnp.zeros((24, COLS), F32)
    d0 = deep[0:16, :]
    d1 = deep[ROWS - 16 : ROWS, :]

    def send(r, down, up, fold):
        a_ref[r : r + 8, :] = jnp.where(even, up, down)
        b_ref[r : r + 8, :] = jnp.where(even, down, jnp.where(top, fold, up))

    def put(p, down, up):
        send(8 * p, down, up, SIGNS[p] * flip_rows(flip_lanes(up)))

    for k in range(LEVELS):
        wl = jnp.where(k < d0, w2[0, k].astype(F32), 0.0)
        wh = jnp.where(k < d1, w2[1, k].astype(F32), 0.0)
        for f, ref in ((U, u2), (V, v2)):
            low = ref[0, k] * wl
            high = ref[1, k] * wh
            put(f + k, low[0:8], high[8:16])
            low9[f + k : f + k + 1, :] = low[8:9]
            high9[f + k : f + k + 1, :] = high[7:8]
        tl = t2[0, k] * wl
        th = t2[1, k] * wh
        sl = s2[0, k] * wl
        sh = s2[1, k] * wh
        put(D + k, (haline_scale * sl - thermal_scale * tl)[0:8], (haline_scale * sh - thermal_scale * th)[8:16])
        put(WET + k, wl[0:8], wh[8:16])
        for n, (low, high) in enumerate(((tl, th), (sl, sh))):
            r = 4 * k + 2 * n
            low2[r : r + 2, :] = low[0:2]
            high2[r : r + 2, :] = high[14:16]
            fold2[r : r + 1, :] = high[15:16]
            fold2[r + 1 : r + 2, :] = high[14:15]
    for n in range(4):
        put(40 + n, flat[n, 0:8, :], flat[n, ROWS - 8 : ROWS, :])
    for r in range(0, 24, 8):
        up = high9[r : r + 8, :]
        send(NINTH + r, low9[r : r + 8, :], up, -flip_lanes(up))
    for r in range(0, 40, 8):
        send(PAIRS + r, low2[r : r + 8, :], high2[r : r + 8, :], flip_lanes(fold2[r : r + 8, :]))


class Columns:
    def __init__(self, lane):
        self.lane = lane
        zero = jnp.zeros((8, COLS), F32)
        self.east = [zero] * SLABS
        self.west = [zero] * SLABS

    def put_east(self, q, moved, at, count):
        lane = self.lane
        self.east[q] = jnp.where((lane >= at) & (lane < at + count), moved, self.east[q])

    def put_west(self, q, moved, end, count):
        lane = self.lane
        low = (end - count) % COLS
        here = (lane >= low) & (lane < end) if low < end else (lane >= low) | (lane < end)
        self.west[q] = jnp.where(here, moved, self.west[q])

    def put(self, q, val, shift, count):
        moved = turn(val, shift)
        self.put_east(q, moved, shift, count)
        self.put_west(q, moved, shift, count)

    def level(self, q, k, val):
        self.put(q, val, STRIDE * k + 2, 9)

    def tracers(self, k, t, s):
        for q, val in enumerate((t, s)):
            self.put_east(q, turn(val, STRIDE * k), STRIDE * k, 2)
            self.put_west(q, turn(val, STRIDE * k + 4), STRIDE * k + 4, 2)

    def flat(self, n, val):
        if n % 2 == 0:
            self.put(n // 2, val, 112, 9)
        else:
            self.put(n // 2, val, 121, 7)


def shifted(x, d):
    lane = lanes()
    keep = lane < COLS - d if d > 0 else lane >= -d
    return jnp.where(keep, turn(x, -d), 0.0)


def smoothed(at, p, c, shift):
    north, south = at(p, 1), at(p, -1)
    q = (north + south) - 4.0 * c
    both = shift(c, 2) + shift(c, -2) + (at(p, 2) + at(p, -2))
    return both + 2.0 * ((shift(q, 1) + shift(q, -1)) - 4.0 * q) - 12.0 * c, north, south


def own_tile(at, spin, put_u, put_v, put_t, put_s):
    zero = jnp.zeros((8, COLS), F32)
    acc = acc_ns = sum_u = sum_v = old_u = old_v = depth = zero
    for k in range(LEVELS):
        wet = at(WET + k, 0)
        u = at(U + k, 0)
        v = at(V + k, 0)
        smooth_u, _, _ = smoothed(at, U + k, u, shifted)
        smooth_v, v_north, v_south = smoothed(at, V + k, v, shifted)
        half = (0.5 * THICK[k]) * at(D + k, 0)
        half_ns = (0.5 * THICK[k]) * (at(D + k, 1) - at(D + k, -1))
        pressure = acc + half
        pressure_ns = acc_ns + half_ns
        acc = pressure + half
        acc_ns = pressure_ns + half_ns
        slope = shifted(pressure, 1) - shifted(pressure, -1)
        u_star = wet * (u + spin * v - (0.5 * pressure_scale) * slope - viscous_scale * smooth_u)
        v_star = wet * (v - spin * u - (0.5 * pressure_scale) * pressure_ns - viscous_scale * smooth_v)
        sum_u = sum_u + THICK[k] * u_star
        sum_v = sum_v + THICK[k] * v_star
        old_u = old_u + THICK[k] * u
        old_v = old_v + THICK[k] * v
        depth = depth + THICK[k] * wet
        if put_u is None:
            continue
        put_u(k, u_star)
        put_v(k, v_star)
        for p, put in ((T + k, put_t), (S + k, put_s)):
            c = at(p, 0)
            smooth, north, south = smoothed(at, p, c, shifted)
            flux = u * c
            advect = (shifted(flux, 1) - shifted(flux, -1)) + (v_north * north - v_south * south)
            put(k, wet * (c - (0.5 * advect_scale) * advect - viscous_scale * smooth))
    return sum_u, sum_v, sum_u - old_u, sum_v - old_v, depth


def centre(u, v, t, s, w, bottom, eta, ub, vb, cor, x_ref, ec, wc, us, vs, tn, sn, sums,
           u2, v2, t2, s2, w2, deep, sem):
    moves = list(zip((u, v, t, s, w, bottom), (u2, v2, t2, s2, w2, deep)))
    for n, src in enumerate((eta, ub, vb, cor)):
        moves.append((src, x_ref.at[FLAT + n]))
    for copy in fetch(moves, sem):
        copy.wait()
    lane = lanes()

    def pack(i, carry):
        rows = pl.ds(pl.multiple_of(8 * i, 8), 8)
        bed = deep[rows, :]
        columns = Columns(lane)
        for k in range(LEVELS):
            wet = jnp.where(k < bed, w2[k, rows, :].astype(F32), 0.0)
            uk = u2[k, rows, :] * wet
            vk = v2[k, rows, :] * wet
            tk = t2[k, rows, :] * wet
            sk = s2[k, rows, :] * wet
            dk = haline_scale * sk - thermal_scale * tk
            for p, val in ((U, uk), (V, vk), (D, dk), (WET, wet), (T, tk), (S, sk)):
                x_ref[p + k, rows, :] = val
            for q, val in enumerate((uk, vk, dk, wet)):
                columns.level(q, k, val)
            columns.tracers(k, tk, sk)
        for n in range(4):
            columns.flat(n, x_ref[FLAT + n, rows, :])
        for q in range(SLABS):
            ec[q, rows, :] = columns.east[q]
            wc[q, rows, :] = columns.west[q]
        return carry

    lax.fori_loop(0, ROWS // 8, pack, 0)

    def inner(i, carry):
        r0 = 8 * i
        rows = pl.ds(pl.multiple_of(r0, 8), 8)

        def store(ref):
            def put(k, val):
                ref[k, rows, :] = val
            return put

        got = own_tile(
            lambda p, d: x_ref[p, pl.ds(r0 + d, 8), :], rotation_scale * x_ref[FLAT + 3, rows, :],
            store(us), store(vs), store(tn), store(sn),
        )
        for n in range(5):
            sums[n, rows, :] = got[n]
        return carry

    lax.fori_loop(1, ROWS // 8 - 1, inner, 0)


def pack_rims(a_ref, b_ref, ec, wc, e_ref, w_ref):
    even, _ = lat_place()
    lane = lanes()
    sub = lax.broadcasted_iota(jnp.int32, (8, COLS), 0)
    for q in range(SLABS):
        e_ref[q, TOP : TOP + ROWS, :] = ec[q]
        w_ref[q, TOP : TOP + ROWS, :] = wc[q]

    def both(r, n):
        a = a_ref[r : r + n, :]
        b = b_ref[r : r + n, :]
        return jnp.where(even, b, a), jnp.where(even, a, b)

    ninth, south, north = Columns(lane), Columns(lane), Columns(lane)
    for k in range(LEVELS):
        for q in range(4):
            lo, hi = both(8 * (10 * q + k), 8)
            south.level(q, k, lo)
            north.level(q, k, hi)
            if q < 2:
                lo, hi = both(NINTH + 10 * q + k, 1)
                ninth.level(q, k, jnp.where(sub == 0, lo, hi))
        pairs = [both(PAIRS + 4 * k + n, 1) for n in range(4)]
        t_lo, s_lo = (jnp.where(sub == 6, pairs[n][0], pairs[n + 1][0]) for n in (0, 2))
        t_hi, s_hi = (jnp.where(sub == 0, pairs[n][1], pairs[n + 1][1]) for n in (0, 2))
        south.tracers(k, t_lo, s_lo)
        north.tracers(k, t_hi, s_hi)
    for n in range(4):
        lo, hi = both(8 * (40 + n), 8)
        south.flat(n, lo)
        north.flat(n, hi)
    for at, columns in ((0, ninth), (8, south), (TOP + ROWS, north)):
        for q in range(SLABS):
            e_ref[q, at : at + 8, :] = columns.east[q]
            w_ref[q, at : at + 8, :] = columns.west[q]


def edges(x_ref, a_ref, b_ref, us, vs, tn, sn, sums, low, high):
    even, _ = lat_place()

    def both(r, n):
        a = a_ref[pl.ds(r, n), :]
        b = b_ref[pl.ds(r, n), :]
        return jnp.where(even, b, a), jnp.where(even, a, b)

    def place(p, carry):
        low[p, 16:32, :] = x_ref[p, 0:16, :]
        high[p, 0:16, :] = x_ref[p, ROWS - 16 : ROWS, :]
        return carry

    lax.fori_loop(0, FLAT, place, 0)

    def rims(p, carry):
        lo, hi = both(pl.multiple_of(8 * p, 8), 8)
        low[p, 8:16, :] = lo
        high[p, 16:24, :] = hi
        return carry

    lax.fori_loop(0, 40, rims, 0)
    for p in range(20):
        lo, hi = both(NINTH + p, 1)
        low[p, 7:8, :] = lo
        high[p, 24:25, :] = hi
    for k in range(LEVELS):
        for n, p in enumerate((T + k, S + k)):
            lo, hi = both(PAIRS + 4 * k + 2 * n, 2)
            low[p, 14:16, :] = lo
            high[p, 16:18, :] = hi
    spin_low, spin_high = both(8 * 43, 8)
    for n, (ref, r0, spin) in enumerate((
        (low, 16, x_ref[FLAT + 3, 0:8, :]),
        (high, 8, x_ref[FLAT + 3, ROWS - 8 : ROWS, :]),
        (low, 8, spin_low),
        (high, 16, spin_high),
    )):
        def store(out):
            def put(k, val):
                out[k, 8 * n : 8 * n + 8, :] = val
            return put

        puts = [store(out) for out in (us, vs, tn, sn)] if n < 2 else [None] * 4
        got = own_tile(lambda p, d: ref[p, r0 + d : r0 + d + 8, :], rotation_scale * spin, *puts)
        for m in range(5):
            sums[m, 8 * n : 8 * n + 8, :] = got[m]


class Wide:
    def __init__(self, own, rim):
        self.own, self.rim = own, rim

    def with_other(self, other, op):
        if isinstance(other, Wide):
            return Wide(op(self.own, other.own), op(self.rim, other.rim))
        return Wide(op(self.own, other), op(self.rim, other))

    def __add__(self, other):
        return self.with_other(other, lambda a, b: a + b)

    def __sub__(self, other):
        return self.with_other(other, lambda a, b: a - b)

    def __mul__(self, other):
        return self.with_other(other, lambda a, b: a * b)

    __rmul__ = __mul__

    def __truediv__(self, other):
        return self.with_other(other, lambda a, b: a / b)


def slope(x):
    lane = lanes()
    east_own, east_rim = turn(x.own, -1), turn(x.rim, -1)
    west_own, west_rim = turn(x.own, 1), turn(x.rim, 1)
    last, first = lane == COLS - 1, lane == 0
    return Wide(
        jnp.where(last, east_rim, east_own) - jnp.where(first, west_rim, west_own),
        jnp.where(last, east_own, east_rim) - jnp.where(first, west_own, west_rim),
    )


def group_sum(x):
    one = x + turn(x, -STRIDE)
    two = one + turn(one, -2 * STRIDE)
    return two + turn(two, -4 * STRIDE) + turn(one, -8 * STRIDE)


def step(x_ref, a_ref, b_ref, e_mine, w_mine, e_got, w_got, us, vs, tn, sn, sums, us2, vs2, tn2, sn2, sums2,
         u_out, v_out, t_out, s_out, eta_out, ub_out, vb_out,
         es, ws, own, rim, fix, total, col, fu, fv, mu, mv, tu, tv, spins, t_new, s_new, u_new, v_new, flats, sem):
    even, _ = lat_place()
    lane = lanes()
    rest = lane % STRIDE
    inside = lane < LEVELS * STRIDE
    for r in range(0, SLAB_ROWS, 8):
        for q in range(SLABS):
            here = slice(r, r + 8)
            east = jnp.where((rest < 2) & inside, w_mine[q, here, :], e_got[q, here, :])
            west = jnp.where(((rest == 2) | (rest == 3)) & inside, e_mine[q, here, :], w_got[q, here, :])
            for ref, val in ((es, east), (ws, west)):
                if r == 0:
                    ref[q, 7:8, :] = val[0:1]
                    ref[q, TOP + ROWS + 8 : TOP + ROWS + 9, :] = val[1:2]
                else:
                    ref[q, here, :] = val
            if q < 2 and r > 0:
                es[SLABS + q, here, :] = turn(e_got[q, here, :], 2)
                ws[SLABS + q, here, :] = turn(w_got[q, here, :], -2)
    for n in range(4):
        a = a_ref[8 * (40 + n) : 8 * (41 + n), :]
        b = b_ref[8 * (40 + n) : 8 * (41 + n), :]
        own[n, 8:16, :] = jnp.where(even, b, a)
        own[n, TOP : TOP + ROWS, :] = x_ref[FLAT + n]
        own[n, TOP + ROWS : TOP + ROWS + 8, :] = jnp.where(even, a, b)
        q, second = divmod(n, 2)
        for r in range(8, 88, 8):
            at = (121, 7) if second else (112, 16)
            rim[n, r : r + 8, :] = turn(jnp.where(lane >= at[0], es[q, r : r + 8, :], ws[q, r : r + 8, :]), at[1])
    for m in range(5):
        total[m, 8:16, :] = sums2[m, 16:24, :]
        total[m, 16:24, :] = sums2[m, 0:8, :]
        total[m, 24:72, :] = sums[m, 8:56, :]
        total[m, 72:80, :] = sums2[m, 8:16, :]
        total[m, 80:88, :] = sums2[m, 24:32, :]

    short = lane
    lane = lanes(BAND)
    rest = lane % STRIDE
    inside = lane < LEVELS * STRIDE
    level_e = jnp.minimum(lane // STRIDE, LEVELS)
    level_w = jnp.minimum(((lane + 7) % COLS) // STRIDE, LEVELS)
    thick_e = jnp.where(level_e < LEVELS, (level_e + 1).astype(F32) * THICK[0], 0.0)
    thick_w = jnp.where(level_w < LEVELS, (level_w + 1).astype(F32) * THICK[0], 0.0)
    edge = (lane < 2) | (lane >= COLS - 2)
    border = (short < 2) | (short >= COLS - 2)

    def slab_tile(i, carry):
        r0 = BAND * i + 8
        here = pl.ds(pl.multiple_of(r0, 8), BAND)
        parts = []
        for ref, level, thick, ahead in ((es, level_e, thick_e, 1), (ws, level_w, thick_w, -1)):
            def at(q, d):
                return ref[q, pl.ds(r0 + d, BAND), :]

            def stacked(x):
                for n in (1, 2, 4, 8):
                    x = x + jnp.where(level >= n, turn(x, n * STRIDE), 0.0)
                return x

            def around(x, d):
                return turn(x, -d)

            if ahead > 0:
                near, pair = (rest == 2) & inside, ((rest == 2) | (rest == 3)) & inside
            else:
                near, pair = (rest == 1) & inside, (rest < 2) & inside
            wet = at(3, 0)
            u = at(0, 0)
            v = at(1, 0)
            weight = thick * at(2, 0)
            weight_ns = thick * (at(2, 1) - at(2, -1))
            pressure = stacked(weight) - 0.5 * weight
            pressure_ns = stacked(weight_ns) - 0.5 * weight_ns
            smooth_u, un, us_ = smoothed(at, 0, u, around)
            smooth_v, vn, vs_ = smoothed(at, 1, v, around)
            change = pressure_scale * 0.5 * (turn(pressure, -1) - turn(pressure, 1)) + viscous_scale * smooth_u
            change_ns = pressure_scale * 0.5 * pressure_ns + viscous_scale * smooth_v
            parts.append((wet * thick, -change, -change_ns, u, v, wet))

            def beyond(c, ns, extra):
                far = viscous_scale * jnp.where(pair, c, 0.0)
                close = jnp.where(near, (2.0 * viscous_scale) * (ns - 4.0 * c) + extra, 0.0)
                return -(turn(far, -2 * ahead) + turn(close, -ahead))

            push = (0.5 * pressure_scale * ahead) * pressure
            fixes = [beyond(u, un + us_, push), beyond(v, vn + vs_, 0.0)]
            carry_u = (0.5 * advect_scale * ahead) * u
            for q in (SLABS, SLABS + 1):
                c = at(q, 0)
                fixes.append(beyond(c, at(q, 1) + at(q, -1), carry_u * c))
            parts.append(fixes)
        (we, due, dve, ue, ve, wet_e), fix_e, (ww, duw, dvw, uw, vw, wet_w), fix_w = parts
        own_wet = jnp.where(rest < 2, wet_e, wet_w)
        own_thick = jnp.where(rest < 2, thick_e, thick_w)
        fixes = [own_wet * (x + y) for x, y in zip(fix_e, fix_w)]
        for n in range(4):
            fix[n, here, :] = fixes[n]

        def to_rim(e, w):
            return turn(jnp.where((lane >= 2) & (lane <= 10), group_sum(e), group_sum(w)), -2)

        def to_own(x):
            return jnp.where(edge, turn(group_sum(own_thick * x), -2), 0.0)

        spin = Wide(rotation_scale * own[3, here, :], rotation_scale * rim[3, here, :])
        column = Wide(surface_depth + total[4, here, :], surface_depth + to_rim(we, ww))
        rim_u = to_rim(we * due, ww * duw) + spin.rim * to_rim(we * ve, ww * vw)
        rim_v = to_rim(we * dve, ww * dvw) - spin.rim * to_rim(we * ue, ww * uw)
        fix_u = to_own(fixes[0])
        fix_v = to_own(fixes[1])
        part = Wide(1.0 / column.own, 1.0 / column.rim)
        for ref, mean, own_sum, own_diff, rim_diff, x in (
            (fu, mu, total[0, here, :], total[2, here, :], rim_u, fix_u),
            (fv, mv, total[1, here, :], total[3, here, :], rim_v, fix_v),
        ):
            ref[0, here, :] = (own_diff + x) * part.own * (1.0 / SUBSTEPS)
            ref[1, here, :] = rim_diff * part.rim * (1.0 / SUBSTEPS)
            mean[here, :] = (own_sum + x) * part.own
        for ref, x in ((col, column), (spins, spin)):
            ref[0, here, :] = x.own
            ref[1, here, :] = x.rim
        return carry

    lax.fori_loop(0, 80 // BAND, slab_tile, 0)

    def mend(n, k, rows_fix):
        return jnp.where(border, turn(fix[n, rows_fix, :], -(STRIDE * k + 2)), 0.0)

    def tile_of(i):
        return pl.ds(pl.multiple_of(8 * i, 8), 8), pl.ds(pl.multiple_of(8 * i + TOP, 8), 8)

    def tracer_tile(rows, fixed, refs, src):
        for n, (ref, out) in enumerate(zip(refs, (t_new, s_new))):
            for k in range(LEVELS):
                out[k, rows, :] = ref[k, src, :] + mend(2 + n, k, fixed)

    def tracer_loop(i, carry):
        rows, fixed = tile_of(i)
        tracer_tile(rows, fixed, (tn, sn), rows)
        return carry

    lax.fori_loop(1, ROWS // 8 - 1, tracer_loop, 0)
    for n, i in enumerate((0, ROWS // 8 - 1)):
        tracer_tile(slice(8 * i, 8 * i + 8), slice(8 * i + TOP, 8 * i + TOP + 8), (tn2, sn2), slice(8 * n, 8 * n + 8))
    first = [pltpu.make_async_copy(src, dst, sem.at[n]) for n, (src, dst) in enumerate(((t_new, t_out), (s_new, s_out)))]
    for copy in first:
        copy.start()

    def wide(ref, at):
        return Wide(ref[0, at, :], ref[1, at, :])

    def keep(ref, at, x):
        ref[0, at, :] = x.own
        ref[1, at, :] = x.rim

    def flat(p, r):
        return Wide(own[p, r : r + 8, :], rim[p, r : r + 8, :])

    def wet_of(column):
        return Wide(jnp.where(column.own > surface_depth, 1.0, 0.0), jnp.where(column.rim > surface_depth, 1.0, 0.0))

    def substep(n, carry):
        for r in range(8, 88, 8):
            here = slice(r, r + 8)
            column = wide(col, here)
            wet = wet_of(column)
            u = flat(1, r)
            v = flat(2, r)
            spin = wide(spins, here)
            un = wet * (u - (0.5 * gravity_scale) * slope(flat(0, r)) + spin * v + wide(fu, here))
            vn = wet * (v - (0.5 * gravity_scale) * (flat(0, r + 1) - flat(0, r - 1)) - spin * u + wide(fv, here))
            for p, x in ((1, un), (2, vn)):
                own[p, here, :] = x.own
                rim[p, here, :] = x.rim
            keep(tu, here, column * un)
            keep(tv, here, column * vn)
        for r in range(8, 88, 8):
            here = slice(r, r + 8)
            wet = wet_of(wide(col, here))
            flow = slope(wide(tu, here)) + (wide(tv, slice(r + 1, r + 9)) - wide(tv, slice(r - 1, r + 7)))
            eta = wet * (flat(0, r) - (0.5 * divergence_scale) * flow)
            own[0, here, :] = eta.own
            rim[0, here, :] = eta.rim
        return carry

    lax.fori_loop(0, SUBSTEPS, substep, 0)
    second = []
    for n, dst in enumerate((eta_out, ub_out, vb_out)):
        flats[n] = own[n, TOP : TOP + ROWS, :]
        second.append(pltpu.make_async_copy(flats.at[n], dst, sem.at[2 + n]))
        second[-1].start()

    def flow_tile(rows, fixed, refs, src):
        gain = (own[1, fixed, :] - mu[fixed, :], own[2, fixed, :] - mv[fixed, :])
        for k in range(LEVELS):
            wet = x_ref[WET + k, rows, :]
            for n, (ref, out) in enumerate(zip(refs, (u_new, v_new))):
                out[k, rows, :] = ref[k, src, :] + mend(n, k, fixed) + wet * gain[n]

    def flow_loop(i, carry):
        rows, fixed = tile_of(i)
        flow_tile(rows, fixed, (us, vs), rows)
        return carry

    lax.fori_loop(1, ROWS // 8 - 1, flow_loop, 0)
    for n, i in enumerate((0, ROWS // 8 - 1)):
        flow_tile(slice(8 * i, 8 * i + 8), slice(8 * i + TOP, 8 * i + TOP + 8), (us2, vs2), slice(8 * n, 8 * n + 8))
    last = [pltpu.make_async_copy(src, dst, sem.at[5 + n]) for n, (src, dst) in enumerate(((u_new, u_out), (v_new, v_out)))]
    for copy in last:
        copy.start()
    for copy in first + second + last:
        copy.wait()


def colour(parity, lats, lons):
    pairs = []
    for lat in range(lats):
        for lon in range(lons):
            if (lat + parity) % 2 == 0:
                to = (lon, lat + 1) if lat + 1 < lats else (lons - 1 - lon, lat)
            elif lat > 0:
                to = (lon, lat - 1)
            else:
                continue
            pairs.append((lon * lats + lat, to[0] * lats + to[1]))
    return pairs


def local(u, v, t, s, w, bottom, eta, ub, vb, cor):
    lats = lax.axis_size("lat")
    lons = lax.axis_size("lon")
    raw = tuple(pltpu.with_memory_space_constraint(z, pltpu.HBM) for z in (u, v, t, s, w, bottom, eta, ub, vb, cor))
    vmem = pltpu.VMEM
    dma = pltpu.SemaphoreType.DMA
    two = (2, LEVELS, 16, COLS)
    a, b = call(
        pack_rows, "pack_rows", [(ROW_SLAB, COLS)] * 2,
        [vmem(two, F32)] * 4 + [vmem(two, jnp.int32), vmem((4, ROWS, COLS), F32), vmem(PLANE, jnp.int32)]
        + [vmem((24, COLS), F32)] * 2 + [vmem((40, COLS), F32)] * 3 + [dma((15,))],
        1_000_000, *raw, ins=[HBM] * 10,
    )
    b = lax.ppermute(b, ("lon", "lat"), colour(1, lats, lons))
    a = lax.ppermute(a, ("lon", "lat"), colour(0, lats, lons))
    x, ec, wc, us, vs, tn, sn, sums = call(
        centre, "centre", [(PLANES, ROWS, COLS)] + [(SLABS, ROWS, COLS)] * 2 + [CUBE] * 4 + [(5, ROWS, COLS)],
        [vmem(CUBE, F32)] * 4 + [vmem(CUBE, jnp.int32), vmem(PLANE, jnp.int32), dma((10,))],
        20_000_000, *raw, ins=[HBM] * 10,
    )
    e_mine, w_mine = call(pack_rims, "pack_rims", [(SLABS, SLAB_ROWS, COLS)] * 2, [], 1_000_000, a, b, ec, wc)
    e_got = lax.ppermute(e_mine, "lon", [((i + 1) % lons, i) for i in range(lons)])
    w_got = lax.ppermute(w_mine, "lon", [(i, (i + 1) % lons) for i in range(lons)])
    window = vmem((FLAT, 32, COLS), F32)
    us2, vs2, tn2, sn2, sums2 = call(
        edges, "edges", [(LEVELS, 16, COLS)] * 4 + [(5, 32, COLS)], [window] * 2, 10_000_000, x, a, b,
    )
    wide = vmem((2, HIGH, COLS), F32)
    thin = vmem((HIGH, COLS), F32)
    slab = vmem((SLABS + 2, HIGH, COLS), F32)
    four = vmem((4, HIGH, COLS), F32)
    return tuple(
        call(
            step, "step", [CUBE] * 4 + [PLANE] * 3,
            [slab] * 2 + [four] * 3 + [vmem((5, HIGH, COLS), F32)] + [wide] * 3 + [thin] * 2 + [wide] * 3
            + [vmem(CUBE, F32)] * 4 + [vmem((3, ROWS, COLS), F32), dma((7,))],
            50_000_000, x, a, b, e_mine, w_mine, e_got, w_got, us, vs, tn, sn, sums, us2, vs2, tn2, sn2, sums2,
            outs=[HBM] * 7,
        )
    )


def solution(mesh):
    deep = P(None, "lat", "lon")
    flat = P("lat", "lon")
    return jax.shard_map(
        local,
        mesh=mesh,
        in_specs=(deep,) * 5 + (flat,) * 5,
        out_specs=(deep,) * 4 + (flat,) * 3,
        check_vma=False,
    )
```

time: 57.1 us -> 36 us (0.63)
  local copies, waits for them, and re-layouts: 8.64 us -> 0 us
  Pallas kernels: 20.7 us -> 14.1 us
  waiting for transfers between devices: 15.3 us -> 9.92 us
    unnamed x20 -> x0, local copies, waits for them, and re-layouts: 8.64 us -> none
    pallas_call x4 -> x5, Pallas kernels: 20.7 us -> 14.1 us  [call(): pl.pallas_call(kernel, out_shape=[jax.ShapeDtypeStruct(s, F32) for s in o...]
    ppermute x1, waiting for transfers between devices: 9.17 us -> 5.25 us  [local(): b = lax.ppermute(b, ('lon', 'lat'), colour(1, lats, lons))]
    ppermute x2, waiting for transfers between devices: 6.13 us -> 4.67 us  [the longest x1 3.12 us: local(): lax.ppermute(w_mine, 'lon', [(i, (i + 1) % lons) for i in range(lons)])]
  transfers between devices with their start and end apart: 4 -> 4, of which waited for: 3 -> 3; matrix products, arithmetic and copies ran while one was open for 0% -> 0% of each run, Pallas kernels for 3% -> 17%
where the time goes in v2:
time: 36 us; the launch traced here: 35.8 us
  Pallas kernels  14.1 us (39%)
  starting transfers between devices  11.2 us (31%)
  waiting for transfers between devices  9.92 us (28%)
  between operations  0.68 us (2%)
    pallas_call x5, Pallas kernels, call(): pl.pallas_call(kernel, out_shape=[jax.ShapeDtypeStruct(s, F32) for s in o...  14.1 us
    ppermute x1, starting transfers between devices, local(): b = lax.ppermute(b, ('lon', 'lat'), colour(1, lats, lons))  6.91 us
    ppermute x1, waiting for transfers between devices, local(): b = lax.ppermute(b, ('lon', 'lat'), colour(1, lats, lons))  5.25 us
    ppermute x1, starting transfers between devices, local(): lax.ppermute(e_mine, 'lon', [((i + 1) % lons, i) for i in range(lons)])  3.42 us
    ppermute x1, waiting for transfers between devices, local(): lax.ppermute(w_mine, 'lon', [(i, (i + 1) % lons) for i in range(lons)])  3.12 us
    ppermute x1, waiting for transfers between devices, local(): lax.ppermute(e_mine, 'lon', [((i + 1) % lons, i) for i in range(lons)])  1.55 us
    ppermute x1, starting transfers between devices, local(): a = lax.ppermute(a, ('lon', 'lat'), colour(0, lats, lons))  0.83 us
  transfers between devices with their start and end apart: 4, of which 3 were waited for; matrix products, arithmetic and copies ran while one was open for 0% of the time, Pallas kernels for 17%

profile of v2, /device:TPU:30, one launch (start us, length us, event | category | flops | bytes accessed | tf_op | source)
XLA Modules:
  0.0 35.8 jit_solution(11722449993979677748)
XLA Ops:
  0.6 1.5 %pack_rows.1 = (f32[416,128]{1,0:T(8,128)S(1)}, f32[416,128]{1,0:T(8,128)S(1)}) custom-call(f32[10,64,128]{2,1,0:T(8,128)} %u.3, f32[10,64,128]{2,1,0:T(8,128)} %v.3, f32[10,64,128]{2,1,0:T(8,128)} %t.3, f32[10,64,128]{2,1,0:T(8,128)} %s.3, s32[10,64,128]{2,1,0:T(8,128)} %w.3, s32[64,128]{1,0:T(8,128)} %bottom.3, f32[64,128]{1,0:T(8,128)} %eta.3, ...), custom_call_target="tpu_custom_call" | custom-call | flops 1000000 | bytes 2000000 | tf_op jit(solution)/shard_map/pack_rows/pallas_call | solution.py:47
  2.2 0.8 %collective-permute-start = (f32[416,128]{1,0:T(8,128)S(1)}, f32[416,128]{1,0:T(8,128)S(1)}, u32[]{:S(2)}, u32[]{:S(2)}) collective-permute-start(f32[416,128]{1,0:T(8,128)S(1)} %get-tuple-element.25), channel_id=1, source_target_pairs={{0,1},{16,17},{32,33},{48,49},{64,65},{80,81},{96,97},{112,113},{1... | collective-permute-start | bytes 638984 | tf_op jit(solution)/shard_map/ppermute | solution.py:656
  3.0 6.9 %collective-permute-start.1 = (f32[416,128]{1,0:T(8,128)S(1)}, f32[416,128]{1,0:T(8,128)S(1)}, u32[]{:S(2)}, u32[]{:S(2)}) collective-permute-start(f32[416,128]{1,0:T(8,128)S(1)} %get-tuple-element.26), channel_id=1, source_target_pairs={{1,2},{17,18},{33,34},{49,50},{65,66},{81,82},{97,98},{113,114},{1... | collective-permute-start | bytes 638984 | tf_op jit(solution)/shard_map/ppermute | solution.py:655
  9.9 4.6 %centre.1 = (f32[64,64,128]{2,1,0:T(8,128)S(1)}, f32[4,64,128]{2,1,0:T(8,128)S(1)}, f32[4,64,128]{2,1,0:T(8,128)S(1)}, f32[10,64,128]{2,1,0:T(8,128)S(1)}, f32[1...) custom-call(f32[10,64,128]{2,1,0:T(8,128)} %u.3, ...), custom_call_target="tpu_custom_call" | custom-call | flops 20000000 | bytes 2000000 | tf_op jit(solution)/shard_map/centre/pallas_call | solution.py:47
  14.6 0.0 collective-permute-done.a_ref
  14.6 5.3 %collective-permute-done.1.b_ref = f32[416,128]{1,0:T(8,128)S(1)} collective-permute-done((f32[416,128]{1,0:T(8,128)S(1)}, f32[416,128]{1,0:T(8,128)S(1)}, u32[]{:S(2)}, u32[]{:S(2)}) %collective-permute-start.1) | collective-permute-done | bytes 213024 | tf_op jit(solution)/shard_map/ppermute | solution.py:655
  19.8 0.3 pack_rims.1
  20.1 3.4 %collective-permute-start.2 = (f32[4,88,128]{2,1,0:T(8,128)S(1)}, f32[4,88,128]{2,1,0:T(8,128)S(1)}, u32[]{:S(2)}, u32[]{:S(2)}) collective-permute-start(f32[4,88,128]{2,1,0:T(8,128)S(1)} %get-tuple-element.29.e_mine), channel_id=1, source_target_pairs={{16,0},{32,16},{48,32},{64,48},{80,64},{96,80},{112,96},{128,112},... | collective-permute-start | bytes 540680 | tf_op jit(solution)/shard_map/ppermute | solution.py:663
  23.5 0.0 collective-permute-start.3
  23.5 1.5 %edges.1 = (f32[10,16,128]{2,1,0:T(8,128)S(1)}, f32[10,16,128]{2,1,0:T(8,128)S(1)}, f32[10,16,128]{2,1,0:T(8,128)S(1)}, f32[10,16,128]{2,1,0:T(8,128)S(1)}, f32[5,32,128]{2,1,0:T(8,128)S(1)}) custom-call(f32[64,64,128]{2,1,0:T(8,128)S(1)} %get-tuple-element.24.x_ref, f32[416,128]{1,0:T(8,128)S(1)} %collective-permute-done.a_ref, ...), custom_call_target="tpu_custom_call" | custom-call | flops 10000000 | bytes 2000000 | tf_op jit(solution)/shard_map/edges/pallas_call | solution.py:47
  25.0 1.6 %collective-permute-done.2.e_got = f32[4,88,128]{2,1,0:T(8,128)S(1)} collective-permute-done((f32[4,88,128]{2,1,0:T(8,128)S(1)}, f32[4,88,128]{2,1,0:T(8,128)S(1)}, u32[]{:S(2)}, u32[]{:S(2)}) %collective-permute-start.2) | collective-permute-done | bytes 180256 | tf_op jit(solution)/shard_map/ppermute | solution.py:663
  26.5 3.1 %collective-permute-done.3.w_got = f32[4,88,128]{2,1,0:T(8,128)S(1)} collective-permute-done((f32[4,88,128]{2,1,0:T(8,128)S(1)}, f32[4,88,128]{2,1,0:T(8,128)S(1)}, u32[]{:S(2)}, u32[]{:S(2)}) %collective-permute-start.3) | collective-permute-done | bytes 180256 | tf_op jit(solution)/shard_map/ppermute | solution.py:664
  29.7 6.2 %step.1 = (f32[10,64,128]{2,1,0:T(8,128)}, f32[10,64,128]{2,1,0:T(8,128)}, f32[10,64,128]{2,1,0:T(8,128)}, f32[10,64,128]{2,1,0:T(8,128)}, f32[64,128]{1,0:T(8,1...) custom-call(f32[64,64,128]{2,1,0:T(8,128)S(1)} %get-tuple-element.24.x_ref, f32[416,128]{1,0:T(8,128)S(1)} %collective-permute-done.a_ref, ...), custom_call_target="tpu_custom_call" | custom-call | flops 50000000 | bytes 2000000 | tf_op jit(solution)/shard_map/step/pallas_call | solution.py:47
Async XLA Ops:
  2.2 12.4 %collective-permute-start = (f32[416,128]{1,0:T(8,128)S(1)}, f32[416,128]{1,0:T(8,128)S(1)}, u32[]{:S(2)}, u32[]{:S(2)}) collective-permute-start(f32[416,128]{1,0:T(8,128)S(1)} %get-tuple-element.25), channel_id=1, source_target_pairs={{0,1},{16,17},{32,33},{48,49},{64,65},{80,81},{96,97},{112,113},{1... | collective-permute-start | bytes 638984 | tf_op jit(solution)/shard_map/ppermute | solution.py:656
  3.0 16.8 %collective-permute-start.1 = (f32[416,128]{1,0:T(8,128)S(1)}, f32[416,128]{1,0:T(8,128)S(1)}, u32[]{:S(2)}, u32[]{:S(2)}) collective-permute-start(f32[416,128]{1,0:T(8,128)S(1)} %get-tuple-element.26), channel_id=1, source_target_pairs={{1,2},{17,18},{33,34},{49,50},{65,66},{81,82},{97,98},{113,114},{1... | collective-permute-start | bytes 638984 | tf_op jit(solution)/shard_map/ppermute | solution.py:655
  20.1 6.4 %collective-permute-start.2 = (f32[4,88,128]{2,1,0:T(8,128)S(1)}, f32[4,88,128]{2,1,0:T(8,128)S(1)}, u32[]{:S(2)}, u32[]{:S(2)}) collective-permute-start(f32[4,88,128]{2,1,0:T(8,128)S(1)} %get-tuple-element.29.e_mine), channel_id=1, source_target_pairs={{16,0},{32,16},{48,32},{64,48},{80,64},{96,80},{112,96},{128,112},... | collective-permute-start | bytes 540680 | tf_op jit(solution)/shard_map/ppermute | solution.py:663
  23.5 6.1 %collective-permute-start.3 = (f32[4,88,128]{2,1,0:T(8,128)S(1)}, f32[4,88,128]{2,1,0:T(8,128)S(1)}, u32[]{:S(2)}, u32[]{:S(2)}) collective-permute-start(f32[4,88,128]{2,1,0:T(8,128)S(1)} %get-tuple-element.30.w_mine), channel_id=1, source_target_pairs={{0,16},{16,32},{32,48},{48,64},{64,80},{80,96},{96,112},{112,128},... | collective-permute-start | bytes 540680 | tf_op jit(solution)/shard_map/ppermute | solution.py:664

commit v3 on v2

--- a/solution.py
+++ b/solution.py
@@ -1,11 +1,10 @@
-import functools
-
 import jax
 import jax.numpy as jnp
 from jax import lax
 from jax.experimental import pallas as pl
 from jax.experimental.pallas import tpu as pltpu
 from jax.sharding import PartitionSpec as P
+
 
 SUBSTEPS = 4
 LEVELS = 10
@@ -22,7 +21,7 @@
 SLAB_ROWS = 88
 TOP = 16
 HIGH = 96
-BAND = 40
+BAND = 80
 
 advect_scale = 0.25
 viscous_scale = 0.02
@@ -43,14 +42,13 @@
 PLANE = (ROWS, COLS)
 
 
-def call(kernel, name, out, scratch, flops, *args, ins=None, outs=None):
+def call(kernel, out, scratch, flops, *args, ins=None, outs=None):
     return pl.pallas_call(
         kernel,
         out_shape=[jax.ShapeDtypeStruct(s, F32) for s in out],
         in_specs=ins or [VMEM] * len(args),
         out_specs=outs or [VMEM] * len(out),
         scratch_shapes=scratch,
-        name=name,
         cost_estimate=pl.CostEstimate(flops=flops, bytes_accessed=2_000_000, transcendentals=0),
         compiler_params=pltpu.CompilerParams(vmem_limit_bytes=LIMIT),
     )(*args)
@@ -227,12 +225,40 @@
     return sum_u, sum_v, sum_u - old_u, sum_v - old_v, depth
 
 
-def centre(u, v, t, s, w, bottom, eta, ub, vb, cor, x_ref, ec, wc, us, vs, tn, sn, sums,
+def level_sums(mats):
+    i = lax.broadcasted_iota(jnp.int32, (COLS, COLS), 0)
+    j = lax.broadcasted_iota(jnp.int32, (COLS, COLS), 1)
+    for side, offset in enumerate((0, 7)):
+        def place(x):
+            y = (x + offset) & (COLS - 1)
+            return jnp.where(y < STRIDE * LEVELS, y % STRIDE, -1), y // STRIDE
+
+        def above(src, dst):
+            same = (src[0] == dst[0]) & (src[0] >= 0)
+            return jnp.where(same & (src[1] < dst[1]), 1.0, jnp.where(same & (src[1] == dst[1]), 0.5, 0.0))
+
+        src = place(i)
+        mats[2 * side] = above(src, place(j))
+        mats[2 * side + 1] = above(src, place(j + 1)) - above(src, place(j - 1))
+        target = j + 2 if side == 0 else (j + 9) & (COLS - 1)
+        low = 2 if side == 0 else 0
+        mats[4 + side] = jnp.where((target >= low) & (target < low + 9) & (src[0] == target), 1.0, 0.0)
+        if side == 0:
+            mats[6] = jnp.where((src[0] == ((j + 2) & (COLS - 1))) & (((j + 2) & (COLS - 1)) < 4), 1.0, 0.0)
+
+
+def dot(x, mat):
+    return jnp.dot(x, mat, precision=lax.Precision.HIGHEST, preferred_element_type=F32)
+
+
+def centre(u, v, t, s, w, bottom, eta, ub, vb, cor, x_ref, ec, wc, us, vs, tn, sn, sums, mats,
            u2, v2, t2, s2, w2, deep, sem):
     moves = list(zip((u, v, t, s, w, bottom), (u2, v2, t2, s2, w2, deep)))
     for n, src in enumerate((eta, ub, vb, cor)):
         moves.append((src, x_ref.at[FLAT + n]))
-    for copy in fetch(moves, sem):
+    copies = fetch(moves, sem)
+    level_sums(mats)
+    for copy in copies:
         copy.wait()
     lane = lanes()
 
@@ -268,6 +294,7 @@
         def store(ref):
             def put(k, val):
                 ref[k, rows, :] = val
+
             return put
 
         got = own_tile(
@@ -359,6 +386,7 @@
         def store(out):
             def put(k, val):
                 out[k, 8 * n : 8 * n + 8, :] = val
+
             return put
 
         puts = [store(out) for out in (us, vs, tn, sn)] if n < 2 else [None] * 4
@@ -402,13 +430,7 @@
     )
 
 
-def group_sum(x):
-    one = x + turn(x, -STRIDE)
-    two = one + turn(one, -2 * STRIDE)
-    return two + turn(two, -4 * STRIDE) + turn(one, -8 * STRIDE)
-
-
-def step(x_ref, a_ref, b_ref, e_mine, w_mine, e_got, w_got, us, vs, tn, sn, sums, us2, vs2, tn2, sn2, sums2,
+def step(x_ref, a_ref, b_ref, e_mine, w_mine, e_got, w_got, us, vs, tn, sn, sums, us2, vs2, tn2, sn2, sums2, mats,
          u_out, v_out, t_out, s_out, eta_out, ub_out, vb_out,
          es, ws, own, rim, fix, total, col, fu, fv, mu, mv, tu, tv, spins, t_new, s_new, u_new, v_new, flats, sem):
     even, _ = lat_place()
@@ -461,14 +483,9 @@
         r0 = BAND * i + 8
         here = pl.ds(pl.multiple_of(r0, 8), BAND)
         parts = []
-        for ref, level, thick, ahead in ((es, level_e, thick_e, 1), (ws, level_w, thick_w, -1)):
+        for ref, side, thick, ahead in ((es, 0, thick_e, 1), (ws, 1, thick_w, -1)):
             def at(q, d):
                 return ref[q, pl.ds(r0 + d, BAND), :]
-
-            def stacked(x):
-                for n in (1, 2, 4, 8):
-                    x = x + jnp.where(level >= n, turn(x, n * STRIDE), 0.0)
-                return x
 
             def around(x, d):
                 return turn(x, -d)
@@ -482,11 +499,12 @@
             v = at(1, 0)
             weight = thick * at(2, 0)
             weight_ns = thick * (at(2, 1) - at(2, -1))
-            pressure = stacked(weight) - 0.5 * weight
-            pressure_ns = stacked(weight_ns) - 0.5 * weight_ns
+            pressure = dot(weight, mats[2 * side])
+            pressure_slope = dot(weight, mats[2 * side + 1])
+            pressure_ns = dot(weight_ns, mats[2 * side])
             smooth_u, un, us_ = smoothed(at, 0, u, around)
             smooth_v, vn, vs_ = smoothed(at, 1, v, around)
-            change = pressure_scale * 0.5 * (turn(pressure, -1) - turn(pressure, 1)) + viscous_scale * smooth_u
+            change = pressure_scale * 0.5 * pressure_slope + viscous_scale * smooth_u
             change_ns = pressure_scale * 0.5 * pressure_ns + viscous_scale * smooth_v
             parts.append((wet * thick, -change, -change_ns, u, v, wet))
 
@@ -509,22 +527,20 @@
         for n in range(4):
             fix[n, here, :] = fixes[n]
 
-        def to_rim(e, w):
-            return turn(jnp.where((lane >= 2) & (lane <= 10), group_sum(e), group_sum(w)), -2)
-
-        def to_own(x):
-            return jnp.where(edge, turn(group_sum(own_thick * x), -2), 0.0)
-
+        east = jnp.concatenate([we, we * due, we * dve, we * ue, we * ve], axis=0)
+        west = jnp.concatenate([ww, ww * duw, ww * dvw, ww * uw, ww * vw], axis=0)
+        rims = dot(east, mats[4]) + dot(west, mats[5])
+        rim_depth, rim_du, rim_dv, rim_u, rim_v = (rims[BAND * n : BAND * n + BAND] for n in range(5))
+        owns = dot(jnp.concatenate([own_thick * fixes[0], own_thick * fixes[1]], axis=0), mats[6])
         spin = Wide(rotation_scale * own[3, here, :], rotation_scale * rim[3, here, :])
-        column = Wide(surface_depth + total[4, here, :], surface_depth + to_rim(we, ww))
-        rim_u = to_rim(we * due, ww * duw) + spin.rim * to_rim(we * ve, ww * vw)
-        rim_v = to_rim(we * dve, ww * dvw) - spin.rim * to_rim(we * ue, ww * uw)
-        fix_u = to_own(fixes[0])
-        fix_v = to_own(fixes[1])
+        column = Wide(surface_depth + total[4, here, :], surface_depth + rim_depth)
+        diff_u = rim_du + spin.rim * rim_v
+        diff_v = rim_dv - spin.rim * rim_u
+        fix_u, fix_v = owns[0:BAND], owns[BAND : 2 * BAND]
         part = Wide(1.0 / column.own, 1.0 / column.rim)
         for ref, mean, own_sum, own_diff, rim_diff, x in (
-            (fu, mu, total[0, here, :], total[2, here, :], rim_u, fix_u),
-            (fv, mv, total[1, here, :], total[3, here, :], rim_v, fix_v),
+            (fu, mu, total[0, here, :], total[2, here, :], diff_u, fix_u),
+            (fv, mv, total[1, here, :], total[3, here, :], diff_v, fix_v),
         ):
             ref[0, here, :] = (own_diff + x) * part.own * (1.0 / SUBSTEPS)
             ref[1, here, :] = rim_diff * part.rim * (1.0 / SUBSTEPS)
@@ -647,24 +663,24 @@
     dma = pltpu.SemaphoreType.DMA
     two = (2, LEVELS, 16, COLS)
     a, b = call(
-        pack_rows, "pack_rows", [(ROW_SLAB, COLS)] * 2,
+        pack_rows, [(ROW_SLAB, COLS)] * 2,
         [vmem(two, F32)] * 4 + [vmem(two, jnp.int32), vmem((4, ROWS, COLS), F32), vmem(PLANE, jnp.int32)]
         + [vmem((24, COLS), F32)] * 2 + [vmem((40, COLS), F32)] * 3 + [dma((15,))],
         1_000_000, *raw, ins=[HBM] * 10,
     )
     b = lax.ppermute(b, ("lon", "lat"), colour(1, lats, lons))
     a = lax.ppermute(a, ("lon", "lat"), colour(0, lats, lons))
-    x, ec, wc, us, vs, tn, sn, sums = call(
-        centre, "centre", [(PLANES, ROWS, COLS)] + [(SLABS, ROWS, COLS)] * 2 + [CUBE] * 4 + [(5, ROWS, COLS)],
+    x, ec, wc, us, vs, tn, sn, sums, mats = call(
+        centre, [(PLANES, ROWS, COLS)] + [(SLABS, ROWS, COLS)] * 2 + [CUBE] * 4 + [(5, ROWS, COLS), (7, COLS, COLS)],
         [vmem(CUBE, F32)] * 4 + [vmem(CUBE, jnp.int32), vmem(PLANE, jnp.int32), dma((10,))],
         20_000_000, *raw, ins=[HBM] * 10,
     )
-    e_mine, w_mine = call(pack_rims, "pack_rims", [(SLABS, SLAB_ROWS, COLS)] * 2, [], 1_000_000, a, b, ec, wc)
+    e_mine, w_mine = call(pack_rims, [(SLABS, SLAB_ROWS, COLS)] * 2, [], 1_000_000, a, b, ec, wc)
     e_got = lax.ppermute(e_mine, "lon", [((i + 1) % lons, i) for i in range(lons)])
     w_got = lax.ppermute(w_mine, "lon", [(i, (i + 1) % lons) for i in range(lons)])
     window = vmem((FLAT, 32, COLS), F32)
     us2, vs2, tn2, sn2, sums2 = call(
-        edges, "edges", [(LEVELS, 16, COLS)] * 4 + [(5, 32, COLS)], [window] * 2, 10_000_000, x, a, b,
+        edges, [(LEVELS, 16, COLS)] * 4 + [(5, 32, COLS)], [window] * 2, 10_000_000, x, a, b,
     )
     wide = vmem((2, HIGH, COLS), F32)
     thin = vmem((HIGH, COLS), F32)
@@ -672,10 +688,10 @@
     four = vmem((4, HIGH, COLS), F32)
     return tuple(
         call(
-            step, "step", [CUBE] * 4 + [PLANE] * 3,
+            step, [CUBE] * 4 + [PLANE] * 3,
             [slab] * 2 + [four] * 3 + [vmem((5, HIGH, COLS), F32)] + [wide] * 3 + [thin] * 2 + [wide] * 3
             + [vmem(CUBE, F32)] * 4 + [vmem((3, ROWS, COLS), F32), dma((7,))],
-            50_000_000, x, a, b, e_mine, w_mine, e_got, w_got, us, vs, tn, sn, sums, us2, vs2, tn2, sn2, sums2,
+            50_000_000, x, a, b, e_mine, w_mine, e_got, w_got, us, vs, tn, sn, sums, us2, vs2, tn2, sn2, sums2, mats,
             outs=[HBM] * 7,
         )
     )

time: 36 us -> 33.8 us (0.939)
  Pallas kernels: 14.1 us -> 11.8 us
    pallas_call x5, Pallas kernels: 14.1 us -> 11.8 us  [call(): pl.pallas_call(kernel, out_shape=[jax.ShapeDtypeStruct(s, F32) for s in o...]
  transfers between devices with their start and end apart: 4 -> 4, of which waited for: 3 -> 3; matrix products, arithmetic and copies ran while one was open for 0% -> 0% of each run, Pallas kernels for 17% -> 18%
where the time goes in v3:
time: 33.8 us; the launch traced here: 33.6 us
  Pallas kernels  11.8 us (35%)
  starting transfers between devices  11.2 us (33%)
  waiting for transfers between devices  9.92 us (29%)
  between operations  0.68 us (2%)
    pallas_call x5, Pallas kernels, call(): pl.pallas_call(kernel, out_shape=[jax.ShapeDtypeStruct(s, F32) for s in o...  11.8 us
    ppermute x1, starting transfers between devices, local(): b = lax.ppermute(b, ('lon', 'lat'), colour(1, lats, lons))  6.91 us
    ppermute x1, waiting for transfers between devices, local(): b = lax.ppermute(b, ('lon', 'lat'), colour(1, lats, lons))  5.25 us
    ppermute x1, starting transfers between devices, local(): lax.ppermute(e_mine, 'lon', [((i + 1) % lons, i) for i in range(lons)])  3.42 us
    ppermute x1, waiting for transfers between devices, local(): lax.ppermute(w_mine, 'lon', [(i, (i + 1) % lons) for i in range(lons)])  3.12 us
    ppermute x1, waiting for transfers between devices, local(): lax.ppermute(e_mine, 'lon', [((i + 1) % lons, i) for i in range(lons)])  1.55 us
    ppermute x1, starting transfers between devices, local(): a = lax.ppermute(a, ('lon', 'lat'), colour(0, lats, lons))  0.83 us
  transfers between devices with their start and end apart: 4, of which 3 were waited for; matrix products, arithmetic and copies ran while one was open for 0% of the time, Pallas kernels for 18%

profile of v3, /device:TPU:30, one launch (start us, length us, event | category | flops | bytes accessed | tf_op | source)
XLA Modules:
  0.0 33.6 jit_solution(5282349105681830761)
XLA Ops:
  0.6 1.5 %shard_map.154 = (f32[416,128]{1,0:T(8,128)S(1)}, f32[416,128]{1,0:T(8,128)S(1)}) custom-call(f32[10,64,128]{2,1,0:T(8,128)} %u.3, f32[10,64,128]{2,1,0:T(8,128)} %v.3, f32[10,64,128]{2,1,0:T(8,128)} %t.3, f32[10,64,128]{2,1,0:T(8,128)} %s.3, s32[10,64,128]{2,1,0:T(8,128)} %w.3, s32[64,128]{1,0:T(8,128)} %bottom.3, f32[64,128]{1,0:T(8,128)} %eta.3, ...), custom_call_target="tpu_custom_call" | custom-call | flops 1000000 | bytes 2000000 | tf_op jit(solution)/shard_map/pallas_call | solution.py:46
  2.2 0.8 %collective-permute-start = (f32[416,128]{1,0:T(8,128)S(1)}, f32[416,128]{1,0:T(8,128)S(1)}, u32[]{:S(2)}, u32[]{:S(2)}) collective-permute-start(f32[416,128]{1,0:T(8,128)S(1)} %get-tuple-element.26), channel_id=1, source_target_pairs={{0,1},{16,17},{32,33},{48,49},{64,65},{80,81},{96,97},{112,113},{1... | collective-permute-start | bytes 638984 | tf_op jit(solution)/shard_map/ppermute | solution.py:672
  3.0 6.9 %collective-permute-start.1 = (f32[416,128]{1,0:T(8,128)S(1)}, f32[416,128]{1,0:T(8,128)S(1)}, u32[]{:S(2)}, u32[]{:S(2)}) collective-permute-start(f32[416,128]{1,0:T(8,128)S(1)} %get-tuple-element.27), channel_id=1, source_target_pairs={{1,2},{17,18},{33,34},{49,50},{65,66},{81,82},{97,98},{113,114},{1... | collective-permute-start | bytes 638984 | tf_op jit(solution)/shard_map/ppermute | solution.py:671
  9.9 4.7 %shard_map.153 = (f32[64,64,128]{2,1,0:T(8,128)S(1)}, f32[4,64,128]{2,1,0:T(8,128)S(1)}, f32[4,64,128]{2,1,0:T(8,128)S(1)}, f32[10,64,128]{2,1,0:T(8,128)S(1)}, ...) custom-call(f32[10,64,128]{2,1,0:T(8,128)} %u.3, ...), custom_call_target="tpu_custom_call" | custom-call | flops 20000000 | bytes 2000000 | tf_op jit(solution)/shard_map/pallas_call | solution.py:46
  14.6 0.0 collective-permute-done.a_ref
  14.6 5.2 %collective-permute-done.1.b_ref = f32[416,128]{1,0:T(8,128)S(1)} collective-permute-done((f32[416,128]{1,0:T(8,128)S(1)}, f32[416,128]{1,0:T(8,128)S(1)}, u32[]{:S(2)}, u32[]{:S(2)}) %collective-permute-start.1) | collective-permute-done | bytes 213024 | tf_op jit(solution)/shard_map/ppermute | solution.py:671
  19.8 0.3 shard_map.155
  20.1 3.4 %collective-permute-start.2 = (f32[4,88,128]{2,1,0:T(8,128)S(1)}, f32[4,88,128]{2,1,0:T(8,128)S(1)}, u32[]{:S(2)}, u32[]{:S(2)}) collective-permute-start(f32[4,88,128]{2,1,0:T(8,128)S(1)} %get-tuple-element.30.e_mine), channel_id=1, source_target_pairs={{16,0},{32,16},{48,32},{64,48},{80,64},{96,80},{112,96},{128,112},... | collective-permute-start | bytes 540680 | tf_op jit(solution)/shard_map/ppermute | solution.py:679
  23.5 0.0 collective-permute-start.3
  23.5 1.5 %shard_map.156 = (f32[10,16,128]{2,1,0:T(8,128)S(1)}, f32[10,16,128]{2,1,0:T(8,128)S(1)}, f32[10,16,128]{2,1,0:T(8,128)S(1)}, f32[10,16,128]{2,1,0:T(8,128)S(1)}, f32[5,32,128]{2,1,0:T(8,128)S(1)}) custom-call(f32[64,64,128]{2,1,0:T(8,128)S(1)} %get-tuple-element.25.x_ref, f32[416,128]{1,0:T(8,128)S(1)} %collective-permute-done.a_ref, ...), custom_call_target="tpu_custom_call" | custom-call | flops 10000000 | bytes 2000000 | tf_op jit(solution)/shard_map/pallas_call | solution.py:46
  25.0 1.6 %collective-permute-done.2.e_got = f32[4,88,128]{2,1,0:T(8,128)S(1)} collective-permute-done((f32[4,88,128]{2,1,0:T(8,128)S(1)}, f32[4,88,128]{2,1,0:T(8,128)S(1)}, u32[]{:S(2)}, u32[]{:S(2)}) %collective-permute-start.2) | collective-permute-done | bytes 180256 | tf_op jit(solution)/shard_map/ppermute | solution.py:679
  26.5 3.1 %collective-permute-done.3.w_got = f32[4,88,128]{2,1,0:T(8,128)S(1)} collective-permute-done((f32[4,88,128]{2,1,0:T(8,128)S(1)}, f32[4,88,128]{2,1,0:T(8,128)S(1)}, u32[]{:S(2)}, u32[]{:S(2)}) %collective-permute-start.3) | collective-permute-done | bytes 180256 | tf_op jit(solution)/shard_map/ppermute | solution.py:680
  29.7 3.9 %shard_map.157 = (f32[10,64,128]{2,1,0:T(8,128)}, f32[10,64,128]{2,1,0:T(8,128)}, f32[10,64,128]{2,1,0:T(8,128)}, f32[10,64,128]{2,1,0:T(8,128)}, f32[64,128]{1,...) custom-call(f32[64,64,128]{2,1,0:T(8,128)S(1)} %get-tuple-element.25.x_ref, f32[416,128]{1,0:T(8,128)S(1)} %collective-permute-done.a_ref, ...), custom_call_target="tpu_custom_call" | custom-call | flops 50000000 | bytes 2000000 | tf_op jit(solution)/shard_map/pallas_call | solution.py:46
Async XLA Ops:
  2.2 12.4 %collective-permute-start = (f32[416,128]{1,0:T(8,128)S(1)}, f32[416,128]{1,0:T(8,128)S(1)}, u32[]{:S(2)}, u32[]{:S(2)}) collective-permute-start(f32[416,128]{1,0:T(8,128)S(1)} %get-tuple-element.26), channel_id=1, source_target_pairs={{0,1},{16,17},{32,33},{48,49},{64,65},{80,81},{96,97},{112,113},{1... | collective-permute-start | bytes 638984 | tf_op jit(solution)/shard_map/ppermute | solution.py:672
  3.0 16.8 %collective-permute-start.1 = (f32[416,128]{1,0:T(8,128)S(1)}, f32[416,128]{1,0:T(8,128)S(1)}, u32[]{:S(2)}, u32[]{:S(2)}) collective-permute-start(f32[416,128]{1,0:T(8,128)S(1)} %get-tuple-element.27), channel_id=1, source_target_pairs={{1,2},{17,18},{33,34},{49,50},{65,66},{81,82},{97,98},{113,114},{1... | collective-permute-start | bytes 638984 | tf_op jit(solution)/shard_map/ppermute | solution.py:671
  20.1 6.4 %collective-permute-start.2 = (f32[4,88,128]{2,1,0:T(8,128)S(1)}, f32[4,88,128]{2,1,0:T(8,128)S(1)}, u32[]{:S(2)}, u32[]{:S(2)}) collective-permute-start(f32[4,88,128]{2,1,0:T(8,128)S(1)} %get-tuple-element.30.e_mine), channel_id=1, source_target_pairs={{16,0},{32,16},{48,32},{64,48},{80,64},{96,80},{112,96},{128,112},... | collective-permute-start | bytes 540680 | tf_op jit(solution)/shard_map/ppermute | solution.py:679
  23.5 6.1 %collective-permute-start.3 = (f32[4,88,128]{2,1,0:T(8,128)S(1)}, f32[4,88,128]{2,1,0:T(8,128)S(1)}, u32[]{:S(2)}, u32[]{:S(2)}) collective-permute-start(f32[4,88,128]{2,1,0:T(8,128)S(1)} %get-tuple-element.31.w_mine), channel_id=1, source_target_pairs={{0,16},{16,32},{32,48},{48,64},{64,80},{80,96},{96,112},{112,128},... | collective-permute-start | bytes 540680 | tf_op jit(solution)/shard_map/ppermute | solution.py:680

commit v4 on v3

--- a/solution.py
+++ b/solution.py
@@ -12,10 +12,12 @@
 COLS = 128
 U, V, D, WET, T, S, FLAT = 0, 10, 20, 30, 40, 50, 60
 PLANES = 64
-BLOCKS = 44
-NINTH = 8 * BLOCKS
-PAIRS = NINTH + 24
-ROW_SLAB = PAIRS + 4 * LEVELS
+AT_PAIR = 120
+AT_FLAT = AT_PAIR + 64
+AT_SUM = AT_FLAT + 32
+AT_SLAB = AT_SUM + 24
+AT_NINE = AT_SLAB + 64
+ROW_SLAB = AT_NINE + 8
 STRIDE = 11
 SLABS = 4
 SLAB_ROWS = 88
@@ -34,7 +36,6 @@
 divergence_scale = 0.3
 
 F32 = jnp.float32
-SIGNS = [-1.0] * 20 + [1.0] * 20 + [1.0, -1.0, -1.0, 1.0]
 THICK = [(k + 1.0) * (2.0 / (LEVELS * (LEVELS + 1))) for k in range(LEVELS)]
 HBM = pl.BlockSpec(memory_space=pltpu.HBM)
 VMEM = pl.BlockSpec(memory_space=pltpu.VMEM)
@@ -78,65 +79,15 @@
     return index % 2 == 0, index == lax.axis_size("lat") - 1
 
 
+def lon_odd():
+    return lax.axis_index("lon") % 2 == 1
+
+
 def fetch(pairs, sem):
     copies = [pltpu.make_async_copy(src, dst, sem.at[n]) for n, (src, dst) in enumerate(pairs)]
     for copy in copies:
         copy.start()
     return copies
-
-
-def pack_rows(u, v, t, s, w, bottom, eta, ub, vb, cor, a_ref, b_ref,
-              u2, v2, t2, s2, w2, flat, deep, low9, high9, low2, high2, fold2, sem):
-    even, top = lat_place()
-    moves = []
-    for src, dst in ((u, u2), (v, v2), (t, t2), (s, s2), (w, w2)):
-        moves.append((src.at[:, 0:16, :], dst.at[0]))
-        moves.append((src.at[:, ROWS - 16 : ROWS, :], dst.at[1]))
-    for n, src in enumerate((eta, ub, vb, cor)):
-        moves.append((src, flat.at[n]))
-    moves.append((bottom, deep))
-    for copy in fetch(moves, sem):
-        copy.wait()
-    low9[...] = jnp.zeros((24, COLS), F32)
-    high9[...] = jnp.zeros((24, COLS), F32)
-    d0 = deep[0:16, :]
-    d1 = deep[ROWS - 16 : ROWS, :]
-
-    def send(r, down, up, fold):
-        a_ref[r : r + 8, :] = jnp.where(even, up, down)
-        b_ref[r : r + 8, :] = jnp.where(even, down, jnp.where(top, fold, up))
-
-    def put(p, down, up):
-        send(8 * p, down, up, SIGNS[p] * flip_rows(flip_lanes(up)))
-
-    for k in range(LEVELS):
-        wl = jnp.where(k < d0, w2[0, k].astype(F32), 0.0)
-        wh = jnp.where(k < d1, w2[1, k].astype(F32), 0.0)
-        for f, ref in ((U, u2), (V, v2)):
-            low = ref[0, k] * wl
-            high = ref[1, k] * wh
-            put(f + k, low[0:8], high[8:16])
-            low9[f + k : f + k + 1, :] = low[8:9]
-            high9[f + k : f + k + 1, :] = high[7:8]
-        tl = t2[0, k] * wl
-        th = t2[1, k] * wh
-        sl = s2[0, k] * wl
-        sh = s2[1, k] * wh
-        put(D + k, (haline_scale * sl - thermal_scale * tl)[0:8], (haline_scale * sh - thermal_scale * th)[8:16])
-        put(WET + k, wl[0:8], wh[8:16])
-        for n, (low, high) in enumerate(((tl, th), (sl, sh))):
-            r = 4 * k + 2 * n
-            low2[r : r + 2, :] = low[0:2]
-            high2[r : r + 2, :] = high[14:16]
-            fold2[r : r + 1, :] = high[15:16]
-            fold2[r + 1 : r + 2, :] = high[14:15]
-    for n in range(4):
-        put(40 + n, flat[n, 0:8, :], flat[n, ROWS - 8 : ROWS, :])
-    for r in range(0, 24, 8):
-        up = high9[r : r + 8, :]
-        send(NINTH + r, low9[r : r + 8, :], up, -flip_lanes(up))
-    for r in range(0, 40, 8):
-        send(PAIRS + r, low2[r : r + 8, :], high2[r : r + 8, :], flip_lanes(fold2[r : r + 8, :]))
 
 
 class Columns:
@@ -225,6 +176,111 @@
     return sum_u, sum_v, sum_u - old_u, sum_v - old_v, depth
 
 
+def mirrored_lanes(side):
+    lane = lanes()
+    offset = 7 * side
+    y = (lane + offset) & (COLS - 1)
+    level = y // STRIDE
+    col = y % STRIDE
+    group = y < STRIDE * LEVELS
+    second = lane >= (121 if side == 0 else 112)
+    source = jnp.where(group, 2 * STRIDE * level + 3 - lane, jnp.where(second, 241 - lane, 223 - lane)) & (COLS - 1)
+    tracer = (col < 2) if side == 0 else (col >= STRIDE - 2)
+    with_u = jnp.where(group, jnp.where(tracer, 1.0, -1.0), jnp.where(second, -1.0, 1.0))
+    with_v = jnp.where(group, jnp.where(tracer, 1.0, -1.0), jnp.where(second, 1.0, -1.0))
+    return source, (with_u, with_v, 1.0, 1.0)
+
+
+def pick(x, source):
+    return jnp.take_along_axis(x, source, axis=1, mode="promise_in_bounds")
+
+
+def pack_rows(u, v, t, s, w, bottom, eta, ub, vb, cor, a_ref, b_ref,
+              u2, v2, t2, s2, w2, flat, deep, lo, hi, low4, high4, fold4, low2, high2, fold2, low1, high1, fold1, sem):
+    even, top = lat_place()
+    lane = lanes()
+    sub = lax.broadcasted_iota(jnp.int32, (8, COLS), 0)
+    moves = []
+    for src, dst in ((u, u2), (v, v2), (t, t2), (s, s2), (w, w2)):
+        moves.append((src.at[:, 0:16, :], dst.at[0]))
+        moves.append((src.at[:, ROWS - 16 : ROWS, :], dst.at[1]))
+    for n, src in enumerate((eta, ub, vb, cor)):
+        moves.append((src, flat.at[n]))
+    moves.append((bottom, deep))
+    copies = fetch(moves, sem)
+    sources = [mirrored_lanes(side) for side in (0, 1)]
+    for copy in copies:
+        copy.wait()
+    for ref in (low2, high2, fold2):
+        ref[56:64, :] = jnp.zeros((8, COLS), F32)
+    for ref in (low1, high1, fold1):
+        ref[...] = jnp.zeros((8, COLS), F32)
+    d0 = deep[0:16, :]
+    d1 = deep[ROWS - 16 : ROWS, :]
+    south, north, ninth = Columns(lane), Columns(lane), Columns(lane)
+
+    def send(r, down, up, fold):
+        a_ref[r : r + 8, :] = jnp.where(even, up, down)
+        b_ref[r : r + 8, :] = jnp.where(even, down, jnp.where(top, fold, up))
+
+    def turned(x):
+        return flip_rows(flip_lanes(x))
+
+    for k in range(LEVELS):
+        wl = jnp.where(k < d0, w2[0, k].astype(F32), 0.0)
+        wh = jnp.where(k < d1, w2[1, k].astype(F32), 0.0)
+        low = [ref[0, k] * wl for ref in (u2, v2, t2, s2)]
+        high = [ref[1, k] * wh for ref in (u2, v2, t2, s2)]
+        low_d = haline_scale * low[3] - thermal_scale * low[2]
+        high_d = haline_scale * high[3] - thermal_scale * high[2]
+        for p, q, sign, x, y in (
+            (U, 0, -1.0, low[0], high[0]), (V, 1, -1.0, low[1], high[1]), (D, 2, 1.0, low_d, high_d), (WET, 3, 1.0, wl, wh),
+        ):
+            lo[p + k, 8:24, :] = x
+            hi[p + k, 0:16, :] = y
+            south.level(q, k, x[0:8])
+            north.level(q, k, y[8:16])
+            if q < 2:
+                ninth.level(q, k, jnp.where(sub == 0, x[8:9], y[7:8]))
+            if q < 3:
+                r = 4 * (p + k)
+                low4[r : r + 4, :] = x[0:4]
+                high4[r : r + 4, :] = y[12:16]
+                fold4[r : r + 4, :] = sign * turned(y[8:16])[0:4]
+        south.tracers(k, low[2][0:8], low[3][0:8])
+        north.tracers(k, high[2][8:16], high[3][8:16])
+        for n, (x, y) in enumerate(((low[2], high[2]), (low[3], high[3]), (wl, wh))):
+            r = 20 * n + 2 * k
+            low2[r : r + 2, :] = x[0:2]
+            high2[r : r + 2, :] = y[14:16]
+            fold2[r : r + 2, :] = turned(y[8:16])[0:2]
+    for n in range(4):
+        down, up = flat[n, 0:8, :], flat[n, ROWS - 8 : ROWS, :]
+        south.flat(n, down)
+        north.flat(n, up)
+        send(AT_FLAT + 8 * n, down, up, (-1.0 if n in (1, 2) else 1.0) * turned(up))
+    for r in range(0, AT_PAIR, 8):
+        send(r, low4[r : r + 8, :], high4[r : r + 8, :], fold4[r : r + 8, :])
+    for r in range(0, 64, 8):
+        send(AT_PAIR + r, low2[r : r + 8, :], high2[r : r + 8, :], fold2[r : r + 8, :])
+    none = [None] * 4
+    down = own_tile(lambda p, d: lo[p, 8 + d : 16 + d, :], rotation_scale * flat[3, 0:8, :], *none)
+    up = own_tile(lambda p, d: hi[p, 8 + d : 16 + d, :], rotation_scale * flat[3, ROWS - 8 : ROWS, :], *none)
+    for n, sign in enumerate((-1.0, -1.0, 1.0)):
+        send(AT_SUM + 8 * n, down[2 + n], up[2 + n], sign * turned(up[2 + n]))
+    for side, (downs, ups, others) in enumerate(((south.east, north.east, north.west), (south.west, north.west, north.east))):
+        source, signs = sources[side]
+        for q in range(SLABS):
+            send(AT_SLAB + 32 * side + 8 * q, downs[q], ups[q], signs[q] * flip_rows(pick(others[q], source)))
+    for side, (mine, other) in enumerate(((ninth.east, ninth.west), (ninth.west, ninth.east))):
+        for q in range(2):
+            r = 2 * side + q
+            low1[r : r + 1, :] = mine[q][0:1]
+            high1[r : r + 1, :] = mine[q][1:2]
+            fold1[r : r + 1, :] = -pick(other[q], sources[side][0])[1:2]
+    send(AT_NINE, low1[...], high1[...], fold1[...])
+
+
 def level_sums(mats):
     i = lax.broadcasted_iota(jnp.int32, (COLS, COLS), 0)
     j = lax.broadcasted_iota(jnp.int32, (COLS, COLS), 1)
@@ -308,41 +364,32 @@
     lax.fori_loop(1, ROWS // 8 - 1, inner, 0)
 
 
-def pack_rims(a_ref, b_ref, ec, wc, e_ref, w_ref):
+def pack_rims(a_ref, b_ref, ec, wc, far_ref, near_ref):
     even, _ = lat_place()
-    lane = lanes()
+    odd = lon_odd()
     sub = lax.broadcasted_iota(jnp.int32, (8, COLS), 0)
+
+    def send(q, at, east, west):
+        far_ref[q, at, :] = jnp.where(odd, west, east)
+        near_ref[q, at, :] = jnp.where(odd, east, west)
+
     for q in range(SLABS):
-        e_ref[q, TOP : TOP + ROWS, :] = ec[q]
-        w_ref[q, TOP : TOP + ROWS, :] = wc[q]
+        send(q, slice(TOP, TOP + ROWS), ec[q], wc[q])
 
     def both(r, n):
         a = a_ref[r : r + n, :]
         b = b_ref[r : r + n, :]
         return jnp.where(even, b, a), jnp.where(even, a, b)
 
-    ninth, south, north = Columns(lane), Columns(lane), Columns(lane)
-    for k in range(LEVELS):
-        for q in range(4):
-            lo, hi = both(8 * (10 * q + k), 8)
-            south.level(q, k, lo)
-            north.level(q, k, hi)
-            if q < 2:
-                lo, hi = both(NINTH + 10 * q + k, 1)
-                ninth.level(q, k, jnp.where(sub == 0, lo, hi))
-        pairs = [both(PAIRS + 4 * k + n, 1) for n in range(4)]
-        t_lo, s_lo = (jnp.where(sub == 6, pairs[n][0], pairs[n + 1][0]) for n in (0, 2))
-        t_hi, s_hi = (jnp.where(sub == 0, pairs[n][1], pairs[n + 1][1]) for n in (0, 2))
-        south.tracers(k, t_lo, s_lo)
-        north.tracers(k, t_hi, s_hi)
-    for n in range(4):
-        lo, hi = both(8 * (40 + n), 8)
-        south.flat(n, lo)
-        north.flat(n, hi)
-    for at, columns in ((0, ninth), (8, south), (TOP + ROWS, north)):
-        for q in range(SLABS):
-            e_ref[q, at : at + 8, :] = columns.east[q]
-            w_ref[q, at : at + 8, :] = columns.west[q]
+    for q in range(SLABS):
+        (e_lo, e_hi), (w_lo, w_hi) = (both(AT_SLAB + 32 * side + 8 * q, 8) for side in (0, 1))
+        send(q, slice(8, 16), e_lo, w_lo)
+        send(q, slice(TOP + ROWS, SLAB_ROWS), e_hi, w_hi)
+        if q < 2:
+            rows = [both(AT_NINE + 2 * side + q, 1) for side in (0, 1)]
+            send(q, slice(0, 8), *(jnp.where(sub == 0, lo, hi) for lo, hi in rows))
+        else:
+            send(q, slice(0, 8), *[jnp.zeros((8, COLS), F32)] * 2)
 
 
 def edges(x_ref, a_ref, b_ref, us, vs, tn, sn, sums, low, high):
@@ -353,6 +400,8 @@
         b = b_ref[pl.ds(r, n), :]
         return jnp.where(even, b, a), jnp.where(even, a, b)
 
+    sub = lax.broadcasted_iota(jnp.int32, (8, COLS), 0)
+
     def place(p, carry):
         low[p, 16:32, :] = x_ref[p, 0:16, :]
         high[p, 0:16, :] = x_ref[p, ROWS - 16 : ROWS, :]
@@ -360,23 +409,16 @@
 
     lax.fori_loop(0, FLAT, place, 0)
 
-    def rims(p, carry):
-        lo, hi = both(pl.multiple_of(8 * p, 8), 8)
-        low[p, 8:16, :] = lo
-        high[p, 16:24, :] = hi
-        return carry
-
-    lax.fori_loop(0, 40, rims, 0)
-    for p in range(20):
-        lo, hi = both(NINTH + p, 1)
-        low[p, 7:8, :] = lo
-        high[p, 24:25, :] = hi
-    for k in range(LEVELS):
-        for n, p in enumerate((T + k, S + k)):
-            lo, hi = both(PAIRS + 4 * k + 2 * n, 2)
-            low[p, 14:16, :] = lo
-            high[p, 16:18, :] = hi
-    spin_low, spin_high = both(8 * 43, 8)
+    for p in range(30):
+        lo, hi = both(4 * p, 4)
+        low[p, 12:16, :] = lo
+        high[p, 16:20, :] = hi
+    for n, p in enumerate((T, S, WET)):
+        for k in range(LEVELS):
+            lo, hi = both(AT_PAIR + 20 * n + 2 * k, 2)
+            low[p + k, 14:16, :] = lo
+            high[p + k, 16:18, :] = hi
+    spin_low, spin_high = both(AT_FLAT + 24, 8)
     for n, (ref, r0, spin) in enumerate((
         (low, 16, x_ref[FLAT + 3, 0:8, :]),
         (high, 8, x_ref[FLAT + 3, ROWS - 8 : ROWS, :]),
@@ -392,7 +434,11 @@
         puts = [store(out) for out in (us, vs, tn, sn)] if n < 2 else [None] * 4
         got = own_tile(lambda p, d: ref[p, r0 + d : r0 + d + 8, :], rotation_scale * spin, *puts)
         for m in range(5):
-            sums[m, 8 * n : 8 * n + 8, :] = got[m]
+            val = got[m]
+            if n >= 2 and m >= 2:
+                lo, hi = both(AT_SUM + 8 * (m - 2), 8)
+                val = jnp.where(sub >= 6, val, lo) if n == 2 else jnp.where(sub < 2, val, hi)
+            sums[m, 8 * n : 8 * n + 8, :] = val
 
 
 class Wide:
@@ -430,18 +476,23 @@
     )
 
 
-def step(x_ref, a_ref, b_ref, e_mine, w_mine, e_got, w_got, us, vs, tn, sn, sums, us2, vs2, tn2, sn2, sums2, mats,
+def step(x_ref, a_ref, b_ref, far_mine, near_mine, far_got, near_got, us, vs, tn, sn, sums, us2, vs2, tn2, sn2, sums2, mats,
          u_out, v_out, t_out, s_out, eta_out, ub_out, vb_out,
          es, ws, own, rim, fix, total, col, fu, fv, mu, mv, tu, tv, spins, t_new, s_new, u_new, v_new, flats, sem):
     even, _ = lat_place()
     lane = lanes()
     rest = lane % STRIDE
     inside = lane < LEVELS * STRIDE
+    odd = lon_odd()
     for r in range(0, SLAB_ROWS, 8):
         for q in range(SLABS):
             here = slice(r, r + 8)
-            east = jnp.where((rest < 2) & inside, w_mine[q, here, :], e_got[q, here, :])
-            west = jnp.where(((rest == 2) | (rest == 3)) & inside, e_mine[q, here, :], w_got[q, here, :])
+            far_in, near_in = far_got[q, here, :], near_got[q, here, :]
+            far_out, near_out = far_mine[q, here, :], near_mine[q, here, :]
+            e_got, w_got = jnp.where(odd, far_in, near_in), jnp.where(odd, near_in, far_in)
+            e_mine, w_mine = jnp.where(odd, near_out, far_out), jnp.where(odd, far_out, near_out)
+            east = jnp.where((rest < 2) & inside, w_mine, e_got)
+            west = jnp.where(((rest == 2) | (rest == 3)) & inside, e_mine, w_got)
             for ref, val in ((es, east), (ws, west)):
                 if r == 0:
                     ref[q, 7:8, :] = val[0:1]
@@ -449,11 +500,11 @@
                 else:
                     ref[q, here, :] = val
             if q < 2 and r > 0:
-                es[SLABS + q, here, :] = turn(e_got[q, here, :], 2)
-                ws[SLABS + q, here, :] = turn(w_got[q, here, :], -2)
+                es[SLABS + q, here, :] = turn(e_got, 2)
+                ws[SLABS + q, here, :] = turn(w_got, -2)
     for n in range(4):
-        a = a_ref[8 * (40 + n) : 8 * (41 + n), :]
-        b = b_ref[8 * (40 + n) : 8 * (41 + n), :]
+        a = a_ref[AT_FLAT + 8 * n : AT_FLAT + 8 * n + 8, :]
+        b = b_ref[AT_FLAT + 8 * n : AT_FLAT + 8 * n + 8, :]
         own[n, 8:16, :] = jnp.where(even, b, a)
         own[n, TOP : TOP + ROWS, :] = x_ref[FLAT + n]
         own[n, TOP + ROWS : TOP + ROWS + 8, :] = jnp.where(even, a, b)
@@ -655,6 +706,14 @@
     return pairs
 
 
+def partners(first, lons):
+    pairs = []
+    for west in range(first, lons + first, 2):
+        east = (west + 1) % lons
+        pairs += [(west % lons, east), (east, west % lons)]
+    return pairs
+
+
 def local(u, v, t, s, w, bottom, eta, ub, vb, cor):
     lats = lax.axis_size("lat")
     lons = lax.axis_size("lon")
@@ -665,7 +724,8 @@
     a, b = call(
         pack_rows, [(ROW_SLAB, COLS)] * 2,
         [vmem(two, F32)] * 4 + [vmem(two, jnp.int32), vmem((4, ROWS, COLS), F32), vmem(PLANE, jnp.int32)]
-        + [vmem((24, COLS), F32)] * 2 + [vmem((40, COLS), F32)] * 3 + [dma((15,))],
+        + [vmem((40, 24, COLS), F32)] * 2 + [vmem((AT_PAIR, COLS), F32)] * 3 + [vmem((64, COLS), F32)] * 3
+        + [vmem((8, COLS), F32)] * 3 + [dma((15,))],
         1_000_000, *raw, ins=[HBM] * 10,
     )
     b = lax.ppermute(b, ("lon", "lat"), colour(1, lats, lons))
@@ -675,9 +735,9 @@
         [vmem(CUBE, F32)] * 4 + [vmem(CUBE, jnp.int32), vmem(PLANE, jnp.int32), dma((10,))],
         20_000_000, *raw, ins=[HBM] * 10,
     )
-    e_mine, w_mine = call(pack_rims, [(SLABS, SLAB_ROWS, COLS)] * 2, [], 1_000_000, a, b, ec, wc)
-    e_got = lax.ppermute(e_mine, "lon", [((i + 1) % lons, i) for i in range(lons)])
-    w_got = lax.ppermute(w_mine, "lon", [(i, (i + 1) % lons) for i in range(lons)])
+    far, near = call(pack_rims, [(SLABS, SLAB_ROWS, COLS)] * 2, [], 1_000_000, a, b, ec, wc)
+    far_got = lax.ppermute(far, "lon", partners(1, lons))
+    near_got = lax.ppermute(near, "lon", partners(0, lons))
     window = vmem((FLAT, 32, COLS), F32)
     us2, vs2, tn2, sn2, sums2 = call(
         edges, [(LEVELS, 16, COLS)] * 4 + [(5, 32, COLS)], [window] * 2, 10_000_000, x, a, b,
@@ -691,7 +751,7 @@
             step, [CUBE] * 4 + [PLANE] * 3,
             [slab] * 2 + [four] * 3 + [vmem((5, HIGH, COLS), F32)] + [wide] * 3 + [thin] * 2 + [wide] * 3
             + [vmem(CUBE, F32)] * 4 + [vmem((3, ROWS, COLS), F32), dma((7,))],
-            50_000_000, x, a, b, e_mine, w_mine, e_got, w_got, us, vs, tn, sn, sums, us2, vs2, tn2, sn2, sums2, mats,
+            50_000_000, x, a, b, far, near, far_got, near_got, us, vs, tn, sn, sums, us2, vs2, tn2, sn2, sums2, mats,
             outs=[HBM] * 7,
         )
     )

time: 33.8 us -> 29 us (0.86)
  waiting for transfers between devices: 9.92 us -> 4.98 us
    ppermute x2, waiting for transfers between devices: 4.67 us -> 2.01 us  [the longest x1 2.01 us: local(): far_got = lax.ppermute(far, 'lon', partners(1, lons))]
    ppermute x1, waiting for transfers between devices: 5.25 us -> 2.97 us  [local(): b = lax.ppermute(b, ('lon', 'lat'), colour(1, lats, lons))]
  transfers between devices with their start and end apart: 4 -> 4, of which waited for: 3 -> 2; matrix products, arithmetic and copies ran while one was open for 0% -> 0% of each run, Pallas kernels for 18% -> 20%
where the time goes in v4:
time: 29 us; the launch traced here: 28.8 us
  Pallas kernels  11.9 us (41%)
  starting transfers between devices  11.2 us (39%)
  waiting for transfers between devices  4.98 us (17%)
  between operations  0.68 us (2%)
    pallas_call x5, Pallas kernels, call(): pl.pallas_call(kernel, out_shape=[jax.ShapeDtypeStruct(s, F32) for s in o...  11.9 us
    ppermute x1, starting transfers between devices, local(): b = lax.ppermute(b, ('lon', 'lat'), colour(1, lats, lons))  6.91 us
    ppermute x1, starting transfers between devices, local(): far_got = lax.ppermute(far, 'lon', partners(1, lons))  3.5 us
    ppermute x1, waiting for transfers between devices, local(): b = lax.ppermute(b, ('lon', 'lat'), colour(1, lats, lons))  2.97 us
    ppermute x1, waiting for transfers between devices, local(): far_got = lax.ppermute(far, 'lon', partners(1, lons))  2.01 us
    ppermute x1, starting transfers between devices, local(): a = lax.ppermute(a, ('lon', 'lat'), colour(0, lats, lons))  0.83 us
  transfers between devices with their start and end apart: 4, of which 2 were waited for; matrix products, arithmetic and copies ran while one was open for 0% of the time, Pallas kernels for 20%

profile of v4, /device:TPU:30, one launch (start us, length us, event | category | flops | bytes accessed | tf_op | source)
XLA Modules:
  0.0 28.8 jit_solution(15127860700901251249)
XLA Ops:
  0.6 2.1 %shard_map.154 = (f32[312,128]{1,0:T(8,128)S(1)}, f32[312,128]{1,0:T(8,128)S(1)}) custom-call(f32[10,64,128]{2,1,0:T(8,128)} %u.3, f32[10,64,128]{2,1,0:T(8,128)} %v.3, f32[10,64,128]{2,1,0:T(8,128)} %t.3, f32[10,64,128]{2,1,0:T(8,128)} %s.3, s32[10,64,128]{2,1,0:T(8,128)} %w.3, s32[64,128]{1,0:T(8,128)} %bottom.3, f32[64,128]{1,0:T(8,128)} %eta.3, ...), custom_call_target="tpu_custom_call" | custom-call | flops 1000000 | bytes 2000000 | tf_op jit(solution)/shard_map/pallas_call | solution.py:47
  2.7 0.8 %collective-permute-start = (f32[312,128]{1,0:T(8,128)S(1)}, f32[312,128]{1,0:T(8,128)S(1)}, u32[]{:S(2)}, u32[]{:S(2)}) collective-permute-start(f32[312,128]{1,0:T(8,128)S(1)} %get-tuple-element.26), channel_id=1, source_target_pairs={{0,1},{16,17},{32,33},{48,49},{64,65},{80,81},{96,97},{112,113},{1... | collective-permute-start | bytes 479240 | tf_op jit(solution)/shard_map/ppermute | solution.py:732
  3.6 6.9 %collective-permute-start.1 = (f32[312,128]{1,0:T(8,128)S(1)}, f32[312,128]{1,0:T(8,128)S(1)}, u32[]{:S(2)}, u32[]{:S(2)}) collective-permute-start(f32[312,128]{1,0:T(8,128)S(1)} %get-tuple-element.27), channel_id=1, source_target_pairs={{1,2},{17,18},{33,34},{49,50},{65,66},{81,82},{97,98},{113,114},{1... | collective-permute-start | bytes 479240 | tf_op jit(solution)/shard_map/ppermute | solution.py:731
  10.5 4.7 %shard_map.153 = (f32[64,64,128]{2,1,0:T(8,128)S(1)}, f32[4,64,128]{2,1,0:T(8,128)S(1)}, f32[4,64,128]{2,1,0:T(8,128)S(1)}, f32[10,64,128]{2,1,0:T(8,128)S(1)}, ...) custom-call(f32[10,64,128]{2,1,0:T(8,128)} %u.3, ...), custom_call_target="tpu_custom_call" | custom-call | flops 20000000 | bytes 2000000 | tf_op jit(solution)/shard_map/pallas_call | solution.py:47
  15.1 0.0 collective-permute-done.a_ref
  15.1 3.0 %collective-permute-done.1.b_ref = f32[312,128]{1,0:T(8,128)S(1)} collective-permute-done((f32[312,128]{1,0:T(8,128)S(1)}, f32[312,128]{1,0:T(8,128)S(1)}, u32[]{:S(2)}, u32[]{:S(2)}) %collective-permute-start.1) | collective-permute-done | bytes 159776 | tf_op jit(solution)/shard_map/ppermute | solution.py:731
  18.2 3.5 %collective-permute-start.2 = (f32[4,88,128]{2,1,0:T(8,128)S(1)}, f32[4,88,128]{2,1,0:T(8,128)S(1)}, u32[]{:S(2)}, u32[]{:S(2)}) collective-permute-start(f32[4,88,128]{2,1,0:T(8,128)S(1)} %get-tuple-element.30.far_mine), channel_id=1, source_target_pairs={{16,32},{32,16},{48,64},{64,48},{80,96},{96,80},{112,128},{128,112... | collective-permute-start | bytes 540680 | tf_op jit(solution)/shard_map/ppermute | solution.py:739
  21.7 0.0 collective-permute-start.3
  21.7 1.2 %shard_map.156 = (f32[10,16,128]{2,1,0:T(8,128)S(1)}, f32[10,16,128]{2,1,0:T(8,128)S(1)}, f32[10,16,128]{2,1,0:T(8,128)S(1)}, f32[10,16,128]{2,1,0:T(8,128)S(1)}, f32[5,32,128]{2,1,0:T(8,128)S(1)}) custom-call(f32[64,64,128]{2,1,0:T(8,128)S(1)} %get-tuple-element.25.x_ref, f32[312,128]{1,0:T(8,128)S(1)} %collective-permute-done.a_ref, ...), custom_call_target="tpu_custom_call" | custom-call | flops 10000000 | bytes 2000000 | tf_op jit(solution)/shard_map/pallas_call | solution.py:47
  22.8 2.0 %collective-permute-done.2.far_got = f32[4,88,128]{2,1,0:T(8,128)S(1)} collective-permute-done((f32[4,88,128]{2,1,0:T(8,128)S(1)}, f32[4,88,128]{2,1,0:T(8,128)S(1)}, u32[]{:S(2)}, u32[]{:S(2)}) %collective-permute-start.2) | collective-permute-done | bytes 180256 | tf_op jit(solution)/shard_map/ppermute | solution.py:739
  24.8 0.0 collective-permute-done.3.near_got
  24.8 4.0 %shard_map.157 = (f32[10,64,128]{2,1,0:T(8,128)}, f32[10,64,128]{2,1,0:T(8,128)}, f32[10,64,128]{2,1,0:T(8,128)}, f32[10,64,128]{2,1,0:T(8,128)}, f32[64,128]{1,...) custom-call(f32[64,64,128]{2,1,0:T(8,128)S(1)} %get-tuple-element.25.x_ref, f32[312,128]{1,0:T(8,128)S(1)} %collective-permute-done.a_ref, ...), custom_call_target="tpu_custom_call" | custom-call | flops 50000000 | bytes 2000000 | tf_op jit(solution)/shard_map/pallas_call | solution.py:47
  (1 shorter events, 0.0 us)
Async XLA Ops:
  2.7 12.4 %collective-permute-start = (f32[312,128]{1,0:T(8,128)S(1)}, f32[312,128]{1,0:T(8,128)S(1)}, u32[]{:S(2)}, u32[]{:S(2)}) collective-permute-start(f32[312,128]{1,0:T(8,128)S(1)} %get-tuple-element.26), channel_id=1, source_target_pairs={{0,1},{16,17},{32,33},{48,49},{64,65},{80,81},{96,97},{112,113},{1... | collective-permute-start | bytes 479240 | tf_op jit(solution)/shard_map/ppermute | solution.py:732
  3.6 14.6 %collective-permute-start.1 = (f32[312,128]{1,0:T(8,128)S(1)}, f32[312,128]{1,0:T(8,128)S(1)}, u32[]{:S(2)}, u32[]{:S(2)}) collective-permute-start(f32[312,128]{1,0:T(8,128)S(1)} %get-tuple-element.27), channel_id=1, source_target_pairs={{1,2},{17,18},{33,34},{49,50},{65,66},{81,82},{97,98},{113,114},{1... | collective-permute-start | bytes 479240 | tf_op jit(solution)/shard_map/ppermute | solution.py:731
  18.2 6.7 %collective-permute-start.2 = (f32[4,88,128]{2,1,0:T(8,128)S(1)}, f32[4,88,128]{2,1,0:T(8,128)S(1)}, u32[]{:S(2)}, u32[]{:S(2)}) collective-permute-start(f32[4,88,128]{2,1,0:T(8,128)S(1)} %get-tuple-element.30.far_mine), channel_id=1, source_target_pairs={{16,32},{32,16},{48,64},{64,48},{80,96},{96,80},{112,128},{128,112... | collective-permute-start | bytes 540680 | tf_op jit(solution)/shard_map/ppermute | solution.py:739
  21.7 3.2 %collective-permute-start.3 = (f32[4,88,128]{2,1,0:T(8,128)S(1)}, f32[4,88,128]{2,1,0:T(8,128)S(1)}, u32[]{:S(2)}, u32[]{:S(2)}) collective-permute-start(f32[4,88,128]{2,1,0:T(8,128)S(1)} %get-tuple-element.31.near_mine), channel_id=1, source_target_pairs={{0,16},{16,0},{32,48},{48,32},{64,80},{80,64},{96,112},{112,96},{1... | collective-permute-start | bytes 540680 | tf_op jit(solution)/shard_map/ppermute | solution.py:740

commit v5 on v4

--- a/solution.py
+++ b/solution.py
@@ -12,15 +12,18 @@
 COLS = 128
 U, V, D, WET, T, S, FLAT = 0, 10, 20, 30, 40, 50, 60
 PLANES = 64
-AT_PAIR = 120
-AT_FLAT = AT_PAIR + 64
-AT_SUM = AT_FLAT + 32
-AT_SLAB = AT_SUM + 24
+AT_THREE = 80
+AT_PAIR = AT_THREE + 30
+AT_FLAT = AT_PAIR + 60
+AT_SUM = AT_FLAT + 29
+AT_SLAB = AT_SUM + 15
 AT_NINE = AT_SLAB + 64
-ROW_SLAB = AT_NINE + 8
+ROW_SLAB = AT_NINE + 10
+FLAT_ROWS = ((0, 8), (8, 7), (15, 7), (22, 7))
 STRIDE = 11
 SLABS = 4
-SLAB_ROWS = 88
+TALL = 80
+COLUMN_SLAB = SLABS * TALL + 8
 TOP = 16
 HIGH = 96
 BAND = 80
@@ -196,7 +199,7 @@
 
 
 def pack_rows(u, v, t, s, w, bottom, eta, ub, vb, cor, a_ref, b_ref,
-              u2, v2, t2, s2, w2, flat, deep, lo, hi, low4, high4, fold4, low2, high2, fold2, low1, high1, fold1, sem):
+              u2, v2, t2, s2, w2, flat, deep, lo, hi, downs_ref, ups_ref, folds_ref, sem):
     even, top = lat_place()
     lane = lanes()
     sub = lax.broadcasted_iota(jnp.int32, (8, COLS), 0)
@@ -211,17 +214,15 @@
     sources = [mirrored_lanes(side) for side in (0, 1)]
     for copy in copies:
         copy.wait()
-    for ref in (low2, high2, fold2):
-        ref[56:64, :] = jnp.zeros((8, COLS), F32)
-    for ref in (low1, high1, fold1):
-        ref[...] = jnp.zeros((8, COLS), F32)
+    for ref in (downs_ref, ups_ref, folds_ref):
+        ref[ROW_SLAB - 8 : ROW_SLAB, :] = jnp.zeros((8, COLS), F32)
     d0 = deep[0:16, :]
     d1 = deep[ROWS - 16 : ROWS, :]
     south, north, ninth = Columns(lane), Columns(lane), Columns(lane)
 
-    def send(r, down, up, fold):
-        a_ref[r : r + 8, :] = jnp.where(even, up, down)
-        b_ref[r : r + 8, :] = jnp.where(even, down, jnp.where(top, fold, up))
+    def lay(r, down, up, fold):
+        for ref, val in ((downs_ref, down), (ups_ref, up), (folds_ref, fold)):
+            ref[r : r + val.shape[0], :] = val
 
     def turned(x):
         return flip_rows(flip_lanes(x))
@@ -242,43 +243,37 @@
             north.level(q, k, y[8:16])
             if q < 2:
                 ninth.level(q, k, jnp.where(sub == 0, x[8:9], y[7:8]))
-            if q < 3:
-                r = 4 * (p + k)
-                low4[r : r + 4, :] = x[0:4]
-                high4[r : r + 4, :] = y[12:16]
-                fold4[r : r + 4, :] = sign * turned(y[8:16])[0:4]
+            if q < 2:
+                lay(4 * (p + k), x[0:4], y[12:16], sign * turned(y[8:16])[0:4])
+            elif q == 2:
+                lay(AT_THREE + 3 * k, x[0:3], y[13:16], turned(y[8:16])[0:3])
         south.tracers(k, low[2][0:8], low[3][0:8])
         north.tracers(k, high[2][8:16], high[3][8:16])
         for n, (x, y) in enumerate(((low[2], high[2]), (low[3], high[3]), (wl, wh))):
-            r = 20 * n + 2 * k
-            low2[r : r + 2, :] = x[0:2]
-            high2[r : r + 2, :] = y[14:16]
-            fold2[r : r + 2, :] = turned(y[8:16])[0:2]
-    for n in range(4):
+            lay(AT_PAIR + 20 * n + 2 * k, x[0:2], y[14:16], turned(y[8:16])[0:2])
+    for n, (at, count) in enumerate(FLAT_ROWS):
         down, up = flat[n, 0:8, :], flat[n, ROWS - 8 : ROWS, :]
         south.flat(n, down)
         north.flat(n, up)
-        send(AT_FLAT + 8 * n, down, up, (-1.0 if n in (1, 2) else 1.0) * turned(up))
-    for r in range(0, AT_PAIR, 8):
-        send(r, low4[r : r + 8, :], high4[r : r + 8, :], fold4[r : r + 8, :])
-    for r in range(0, 64, 8):
-        send(AT_PAIR + r, low2[r : r + 8, :], high2[r : r + 8, :], fold2[r : r + 8, :])
+        mirrored = (-1.0 if n in (1, 2) else 1.0) * turned(up)
+        lay(AT_FLAT + at, down[0:count], up[8 - count : 8], mirrored[0:count])
     none = [None] * 4
     down = own_tile(lambda p, d: lo[p, 8 + d : 16 + d, :], rotation_scale * flat[3, 0:8, :], *none)
     up = own_tile(lambda p, d: hi[p, 8 + d : 16 + d, :], rotation_scale * flat[3, ROWS - 8 : ROWS, :], *none)
     for n, sign in enumerate((-1.0, -1.0, 1.0)):
-        send(AT_SUM + 8 * n, down[2 + n], up[2 + n], sign * turned(up[2 + n]))
+        lay(AT_SUM + 5 * n, down[2 + n][2:7], up[2 + n][1:6], sign * turned(up[2 + n])[2:7])
     for side, (downs, ups, others) in enumerate(((south.east, north.east, north.west), (south.west, north.west, north.east))):
         source, signs = sources[side]
         for q in range(SLABS):
-            send(AT_SLAB + 32 * side + 8 * q, downs[q], ups[q], signs[q] * flip_rows(pick(others[q], source)))
+            lay(AT_SLAB + 32 * side + 8 * q, downs[q], ups[q], signs[q] * flip_rows(pick(others[q], source)))
     for side, (mine, other) in enumerate(((ninth.east, ninth.west), (ninth.west, ninth.east))):
         for q in range(2):
-            r = 2 * side + q
-            low1[r : r + 1, :] = mine[q][0:1]
-            high1[r : r + 1, :] = mine[q][1:2]
-            fold1[r : r + 1, :] = -pick(other[q], sources[side][0])[1:2]
-    send(AT_NINE, low1[...], high1[...], fold1[...])
+            lay(AT_NINE + 2 * side + q, mine[q][0:1], mine[q][1:2], -pick(other[q], sources[side][0])[1:2])
+    for r in range(0, ROW_SLAB, 8):
+        here = slice(r, r + 8)
+        down, up = downs_ref[here, :], ups_ref[here, :]
+        a_ref[here, :] = jnp.where(even, up, down)
+        b_ref[here, :] = jnp.where(even, down, jnp.where(top, folds_ref[here, :], up))
 
 
 def level_sums(mats):
@@ -367,14 +362,14 @@
 def pack_rims(a_ref, b_ref, ec, wc, far_ref, near_ref):
     even, _ = lat_place()
     odd = lon_odd()
-    sub = lax.broadcasted_iota(jnp.int32, (8, COLS), 0)
-
-    def send(q, at, east, west):
-        far_ref[q, at, :] = jnp.where(odd, west, east)
-        near_ref[q, at, :] = jnp.where(odd, east, west)
+
+    def send(at, east, west):
+        here = slice(at, at + east.shape[0])
+        far_ref[here, :] = jnp.where(odd, west, east)
+        near_ref[here, :] = jnp.where(odd, east, west)
 
     for q in range(SLABS):
-        send(q, slice(TOP, TOP + ROWS), ec[q], wc[q])
+        send(TALL * q + 8, ec[q], wc[q])
 
     def both(r, n):
         a = a_ref[r : r + n, :]
@@ -383,13 +378,13 @@
 
     for q in range(SLABS):
         (e_lo, e_hi), (w_lo, w_hi) = (both(AT_SLAB + 32 * side + 8 * q, 8) for side in (0, 1))
-        send(q, slice(8, 16), e_lo, w_lo)
-        send(q, slice(TOP + ROWS, SLAB_ROWS), e_hi, w_hi)
-        if q < 2:
-            rows = [both(AT_NINE + 2 * side + q, 1) for side in (0, 1)]
-            send(q, slice(0, 8), *(jnp.where(sub == 0, lo, hi) for lo, hi in rows))
-        else:
-            send(q, slice(0, 8), *[jnp.zeros((8, COLS), F32)] * 2)
+        send(TALL * q, e_lo, w_lo)
+        send(TALL * q + 8 + ROWS, e_hi, w_hi)
+    for q in range(2):
+        pairs = [both(AT_NINE + 2 * side + q, 1) for side in (0, 1)]
+        for n in (0, 1):
+            send(SLABS * TALL + 2 * q + n, pairs[0][n], pairs[1][n])
+    send(SLABS * TALL + 4, *[jnp.zeros((4, COLS), F32)] * 2)
 
 
 def edges(x_ref, a_ref, b_ref, us, vs, tn, sn, sums, low, high):
@@ -400,8 +395,6 @@
         b = b_ref[pl.ds(r, n), :]
         return jnp.where(even, b, a), jnp.where(even, a, b)
 
-    sub = lax.broadcasted_iota(jnp.int32, (8, COLS), 0)
-
     def place(p, carry):
         low[p, 16:32, :] = x_ref[p, 0:16, :]
         high[p, 0:16, :] = x_ref[p, ROWS - 16 : ROWS, :]
@@ -409,21 +402,27 @@
 
     lax.fori_loop(0, FLAT, place, 0)
 
-    for p in range(30):
+    for p in range(20):
         lo, hi = both(4 * p, 4)
         low[p, 12:16, :] = lo
         high[p, 16:20, :] = hi
+    for k in range(LEVELS):
+        lo, hi = both(AT_THREE + 3 * k, 3)
+        low[D + k, 13:16, :] = lo
+        high[D + k, 16:19, :] = hi
     for n, p in enumerate((T, S, WET)):
         for k in range(LEVELS):
             lo, hi = both(AT_PAIR + 20 * n + 2 * k, 2)
             low[p + k, 14:16, :] = lo
             high[p + k, 16:18, :] = hi
-    spin_low, spin_high = both(AT_FLAT + 24, 8)
+    lo, hi = both(AT_FLAT + FLAT_ROWS[3][0], 7)
+    low[FLAT, 9:16, :] = lo
+    high[FLAT, 16:23, :] = hi
     for n, (ref, r0, spin) in enumerate((
         (low, 16, x_ref[FLAT + 3, 0:8, :]),
         (high, 8, x_ref[FLAT + 3, ROWS - 8 : ROWS, :]),
-        (low, 8, spin_low),
-        (high, 16, spin_high),
+        (low, 8, low[FLAT, 8:16, :]),
+        (high, 16, high[FLAT, 16:24, :]),
     )):
         def store(out):
             def put(k, val):
@@ -434,11 +433,12 @@
         puts = [store(out) for out in (us, vs, tn, sn)] if n < 2 else [None] * 4
         got = own_tile(lambda p, d: ref[p, r0 + d : r0 + d + 8, :], rotation_scale * spin, *puts)
         for m in range(5):
-            val = got[m]
+            at = 8 * n
+            sums[m, at : at + 8, :] = got[m]
             if n >= 2 and m >= 2:
-                lo, hi = both(AT_SUM + 8 * (m - 2), 8)
-                val = jnp.where(sub >= 6, val, lo) if n == 2 else jnp.where(sub < 2, val, hi)
-            sums[m, 8 * n : 8 * n + 8, :] = val
+                lo, hi = both(AT_SUM + 5 * (m - 2), 5)
+                first = at + 1 if n == 2 else at + 2
+                sums[m, first : first + 5, :] = lo if n == 2 else hi
 
 
 class Wide:
@@ -484,30 +484,30 @@
     rest = lane % STRIDE
     inside = lane < LEVELS * STRIDE
     odd = lon_odd()
-    for r in range(0, SLAB_ROWS, 8):
-        for q in range(SLABS):
-            here = slice(r, r + 8)
-            far_in, near_in = far_got[q, here, :], near_got[q, here, :]
-            far_out, near_out = far_mine[q, here, :], near_mine[q, here, :]
-            e_got, w_got = jnp.where(odd, far_in, near_in), jnp.where(odd, near_in, far_in)
-            e_mine, w_mine = jnp.where(odd, near_out, far_out), jnp.where(odd, far_out, near_out)
-            east = jnp.where((rest < 2) & inside, w_mine, e_got)
-            west = jnp.where(((rest == 2) | (rest == 3)) & inside, e_mine, w_got)
-            for ref, val in ((es, east), (ws, west)):
-                if r == 0:
-                    ref[q, 7:8, :] = val[0:1]
-                    ref[q, TOP + ROWS + 8 : TOP + ROWS + 9, :] = val[1:2]
-                else:
-                    ref[q, here, :] = val
-            if q < 2 and r > 0:
-                es[SLABS + q, here, :] = turn(e_got, 2)
-                ws[SLABS + q, here, :] = turn(w_got, -2)
+    for q, r, count in [(q, r, 8) for r in range(8, 88, 8) for q in range(SLABS)] + [(0, 0, 2), (1, 0, 2)]:
+        at = TALL * q + r - 8 if r else SLABS * TALL + 2 * q
+        got = slice(at, at + count)
+        far_in, near_in = far_got[got, :], near_got[got, :]
+        far_out, near_out = far_mine[got, :], near_mine[got, :]
+        e_got, w_got = jnp.where(odd, far_in, near_in), jnp.where(odd, near_in, far_in)
+        e_mine, w_mine = jnp.where(odd, near_out, far_out), jnp.where(odd, far_out, near_out)
+        own_e, own_w = (m[0:count] for m in ((rest < 2) & inside, ((rest == 2) | (rest == 3)) & inside))
+        for ref, val in ((es, jnp.where(own_e, w_mine, e_got)), (ws, jnp.where(own_w, e_mine, w_got))):
+            if r:
+                ref[q, r : r + 8, :] = val
+            else:
+                ref[q, 7:8, :] = val[0:1]
+                ref[q, TOP + ROWS + 8 : TOP + ROWS + 9, :] = val[1:2]
+        if q < 2 and r:
+            es[SLABS + q, r : r + 8, :] = turn(e_got, 2)
+            ws[SLABS + q, r : r + 8, :] = turn(w_got, -2)
     for n in range(4):
-        a = a_ref[AT_FLAT + 8 * n : AT_FLAT + 8 * n + 8, :]
-        b = b_ref[AT_FLAT + 8 * n : AT_FLAT + 8 * n + 8, :]
-        own[n, 8:16, :] = jnp.where(even, b, a)
+        at, count = FLAT_ROWS[n]
+        a = a_ref[AT_FLAT + at : AT_FLAT + at + count, :]
+        b = b_ref[AT_FLAT + at : AT_FLAT + at + count, :]
+        own[n, TOP - count : TOP, :] = jnp.where(even, b, a)
         own[n, TOP : TOP + ROWS, :] = x_ref[FLAT + n]
-        own[n, TOP + ROWS : TOP + ROWS + 8, :] = jnp.where(even, a, b)
+        own[n, TOP + ROWS : TOP + ROWS + count, :] = jnp.where(even, a, b)
         q, second = divmod(n, 2)
         for r in range(8, 88, 8):
             at = (121, 7) if second else (112, 16)
@@ -724,8 +724,7 @@
     a, b = call(
         pack_rows, [(ROW_SLAB, COLS)] * 2,
         [vmem(two, F32)] * 4 + [vmem(two, jnp.int32), vmem((4, ROWS, COLS), F32), vmem(PLANE, jnp.int32)]
-        + [vmem((40, 24, COLS), F32)] * 2 + [vmem((AT_PAIR, COLS), F32)] * 3 + [vmem((64, COLS), F32)] * 3
-        + [vmem((8, COLS), F32)] * 3 + [dma((15,))],
+        + [vmem((40, 24, COLS), F32)] * 2 + [vmem((ROW_SLAB, COLS), F32)] * 3 + [dma((15,))],
         1_000_000, *raw, ins=[HBM] * 10,
     )
     b = lax.ppermute(b, ("lon", "lat"), colour(1, lats, lons))
@@ -735,10 +734,10 @@
         [vmem(CUBE, F32)] * 4 + [vmem(CUBE, jnp.int32), vmem(PLANE, jnp.int32), dma((10,))],
         20_000_000, *raw, ins=[HBM] * 10,
     )
-    far, near = call(pack_rims, [(SLABS, SLAB_ROWS, COLS)] * 2, [], 1_000_000, a, b, ec, wc)
+    far, near = call(pack_rims, [(COLUMN_SLAB, COLS)] * 2, [], 1_000_000, a, b, ec, wc)
     far_got = lax.ppermute(far, "lon", partners(1, lons))
     near_got = lax.ppermute(near, "lon", partners(0, lons))
-    window = vmem((FLAT, 32, COLS), F32)
+    window = vmem((FLAT + 1, 32, COLS), F32)
     us2, vs2, tn2, sn2, sums2 = call(
         edges, [(LEVELS, 16, COLS)] * 4 + [(5, 32, COLS)], [window] * 2, 10_000_000, x, a, b,
     )

time: 29 us -> 28.3 us (0.976)
  waiting for transfers between devices: 4.98 us -> 4.18 us
    ppermute x1, waiting for transfers between devices: 2.97 us -> 2.3 us  [local(): b = lax.ppermute(b, ('lon', 'lat'), colour(1, lats, lons))]
  transfers between devices with their start and end apart: 4 -> 4, of which waited for: 2 -> 2; matrix products, arithmetic and copies ran while one was open for 0% -> 0% of each run, Pallas kernels for 20% -> 21%
where the time goes in v5:
time: 28.3 us; the launch traced here: 28.2 us
  Pallas kernels  12.1 us (43%)
  starting transfers between devices  11.3 us (40%)
  waiting for transfers between devices  4.18 us (15%)
  between operations  0.67 us (2%)
    pallas_call x5, Pallas kernels, call(): pl.pallas_call(kernel, out_shape=[jax.ShapeDtypeStruct(s, F32) for s in o...  12.1 us
    ppermute x1, starting transfers between devices, local(): b = lax.ppermute(b, ('lon', 'lat'), colour(1, lats, lons))  6.91 us
    ppermute x1, starting transfers between devices, local(): far_got = lax.ppermute(far, 'lon', partners(1, lons))  3.51 us
    ppermute x1, waiting for transfers between devices, local(): b = lax.ppermute(b, ('lon', 'lat'), colour(1, lats, lons))  2.3 us
    ppermute x1, waiting for transfers between devices, local(): far_got = lax.ppermute(far, 'lon', partners(1, lons))  1.88 us
    ppermute x1, starting transfers between devices, local(): a = lax.ppermute(a, ('lon', 'lat'), colour(0, lats, lons))  0.83 us
  transfers between devices with their start and end apart: 4, of which 2 were waited for; matrix products, arithmetic and copies ran while one was open for 0% of the time, Pallas kernels for 21%

profile of v5, /device:TPU:30, one launch (start us, length us, event | category | flops | bytes accessed | tf_op | source)
XLA Modules:
  0.0 28.2 jit_solution(12271696828785445683)
XLA Ops:
  0.6 2.1 %shard_map.154 = (f32[288,128]{1,0:T(8,128)S(1)}, f32[288,128]{1,0:T(8,128)S(1)}) custom-call(f32[10,64,128]{2,1,0:T(8,128)} %u.3, f32[10,64,128]{2,1,0:T(8,128)} %v.3, f32[10,64,128]{2,1,0:T(8,128)} %t.3, f32[10,64,128]{2,1,0:T(8,128)} %s.3, s32[10,64,128]{2,1,0:T(8,128)} %w.3, s32[64,128]{1,0:T(8,128)} %bottom.3, f32[64,128]{1,0:T(8,128)} %eta.3, ...), custom_call_target="tpu_custom_call" | custom-call | flops 1000000 | bytes 2000000 | tf_op jit(solution)/shard_map/pallas_call | solution.py:50
  2.7 0.8 %collective-permute-start = (f32[288,128]{1,0:T(8,128)S(1)}, f32[288,128]{1,0:T(8,128)S(1)}, u32[]{:S(2)}, u32[]{:S(2)}) collective-permute-start(f32[288,128]{1,0:T(8,128)S(1)} %get-tuple-element.26), channel_id=1, source_target_pairs={{0,1},{16,17},{32,33},{48,49},{64,65},{80,81},{96,97},{112,113},{1... | collective-permute-start | bytes 442376 | tf_op jit(solution)/shard_map/ppermute | solution.py:731
  3.6 6.9 %collective-permute-start.1 = (f32[288,128]{1,0:T(8,128)S(1)}, f32[288,128]{1,0:T(8,128)S(1)}, u32[]{:S(2)}, u32[]{:S(2)}) collective-permute-start(f32[288,128]{1,0:T(8,128)S(1)} %get-tuple-element.27), channel_id=1, source_target_pairs={{1,2},{17,18},{33,34},{49,50},{65,66},{81,82},{97,98},{113,114},{1... | collective-permute-start | bytes 442376 | tf_op jit(solution)/shard_map/ppermute | solution.py:730
  10.5 4.8 %shard_map.153 = (f32[64,64,128]{2,1,0:T(8,128)S(1)}, f32[4,64,128]{2,1,0:T(8,128)S(1)}, f32[4,64,128]{2,1,0:T(8,128)S(1)}, f32[10,64,128]{2,1,0:T(8,128)S(1)}, ...) custom-call(f32[10,64,128]{2,1,0:T(8,128)} %u.3, ...), custom_call_target="tpu_custom_call" | custom-call | flops 20000000 | bytes 2000000 | tf_op jit(solution)/shard_map/pallas_call | solution.py:50
  15.3 0.0 collective-permute-done.a_ref
  15.3 2.3 %collective-permute-done.1.b_ref = f32[288,128]{1,0:T(8,128)S(1)} collective-permute-done((f32[288,128]{1,0:T(8,128)S(1)}, f32[288,128]{1,0:T(8,128)S(1)}, u32[]{:S(2)}, u32[]{:S(2)}) %collective-permute-start.1) | collective-permute-done | bytes 147488 | tf_op jit(solution)/shard_map/ppermute | solution.py:730
  17.6 3.5 %collective-permute-start.2 = (f32[328,128]{1,0:T(8,128)S(1)}, f32[328,128]{1,0:T(8,128)S(1)}, u32[]{:S(2)}, u32[]{:S(2)}) collective-permute-start(f32[328,128]{1,0:T(8,128)S(1)} %get-tuple-element.30.far_mine), channel_id=1, source_target_pairs={{16,32},{32,16},{48,64},{64,48},{80,96},{96,80},{112,128},{128,112... | collective-permute-start | bytes 503816 | tf_op jit(solution)/shard_map/ppermute | solution.py:738
  21.1 0.0 collective-permute-start.3
  21.1 1.2 %shard_map.156 = (f32[10,16,128]{2,1,0:T(8,128)S(1)}, f32[10,16,128]{2,1,0:T(8,128)S(1)}, f32[10,16,128]{2,1,0:T(8,128)S(1)}, f32[10,16,128]{2,1,0:T(8,128)S(1)}, f32[5,32,128]{2,1,0:T(8,128)S(1)}) custom-call(f32[64,64,128]{2,1,0:T(8,128)S(1)} %get-tuple-element.25.x_ref, f32[288,128]{1,0:T(8,128)S(1)} %collective-permute-done.a_ref, ...), custom_call_target="tpu_custom_call" | custom-call | flops 10000000 | bytes 2000000 | tf_op jit(solution)/shard_map/pallas_call | solution.py:50
  22.3 1.9 %collective-permute-done.2.far_got = f32[328,128]{1,0:T(8,128)S(1)} collective-permute-done((f32[328,128]{1,0:T(8,128)S(1)}, f32[328,128]{1,0:T(8,128)S(1)}, u32[]{:S(2)}, u32[]{:S(2)}) %collective-permute-start.2) | collective-permute-done | bytes 167968 | tf_op jit(solution)/shard_map/ppermute | solution.py:738
  24.2 0.0 collective-permute-done.3.near_got
  24.2 4.0 %shard_map.157 = (f32[10,64,128]{2,1,0:T(8,128)}, f32[10,64,128]{2,1,0:T(8,128)}, f32[10,64,128]{2,1,0:T(8,128)}, f32[10,64,128]{2,1,0:T(8,128)}, f32[64,128]{1,...) custom-call(f32[64,64,128]{2,1,0:T(8,128)S(1)} %get-tuple-element.25.x_ref, f32[288,128]{1,0:T(8,128)S(1)} %collective-permute-done.a_ref, ...), custom_call_target="tpu_custom_call" | custom-call | flops 50000000 | bytes 2000000 | tf_op jit(solution)/shard_map/pallas_call | solution.py:50
  (1 shorter events, 0.0 us)
Async XLA Ops:
  2.7 12.6 %collective-permute-start = (f32[288,128]{1,0:T(8,128)S(1)}, f32[288,128]{1,0:T(8,128)S(1)}, u32[]{:S(2)}, u32[]{:S(2)}) collective-permute-start(f32[288,128]{1,0:T(8,128)S(1)} %get-tuple-element.26), channel_id=1, source_target_pairs={{0,1},{16,17},{32,33},{48,49},{64,65},{80,81},{96,97},{112,113},{1... | collective-permute-start | bytes 442376 | tf_op jit(solution)/shard_map/ppermute | solution.py:731
  3.6 14.0 %collective-permute-start.1 = (f32[288,128]{1,0:T(8,128)S(1)}, f32[288,128]{1,0:T(8,128)S(1)}, u32[]{:S(2)}, u32[]{:S(2)}) collective-permute-start(f32[288,128]{1,0:T(8,128)S(1)} %get-tuple-element.27), channel_id=1, source_target_pairs={{1,2},{17,18},{33,34},{49,50},{65,66},{81,82},{97,98},{113,114},{1... | collective-permute-start | bytes 442376 | tf_op jit(solution)/shard_map/ppermute | solution.py:730
  17.6 6.6 %collective-permute-start.2 = (f32[328,128]{1,0:T(8,128)S(1)}, f32[328,128]{1,0:T(8,128)S(1)}, u32[]{:S(2)}, u32[]{:S(2)}) collective-permute-start(f32[328,128]{1,0:T(8,128)S(1)} %get-tuple-element.30.far_mine), channel_id=1, source_target_pairs={{16,32},{32,16},{48,64},{64,48},{80,96},{96,80},{112,128},{128,112... | collective-permute-start | bytes 503816 | tf_op jit(solution)/shard_map/ppermute | solution.py:738
  21.1 3.1 %collective-permute-start.3 = (f32[328,128]{1,0:T(8,128)S(1)}, f32[328,128]{1,0:T(8,128)S(1)}, u32[]{:S(2)}, u32[]{:S(2)}) collective-permute-start(f32[328,128]{1,0:T(8,128)S(1)} %get-tuple-element.31.near_mine), channel_id=1, source_target_pairs={{0,16},{16,0},{32,48},{48,32},{64,80},{80,64},{96,112},{112,96},{1... | collective-permute-start | bytes 503816 | tf_op jit(solution)/shard_map/ppermute | solution.py:739

commit v6 on v5

--- a/solution.py
+++ b/solution.py
@@ -12,13 +12,13 @@
 COLS = 128
 U, V, D, WET, T, S, FLAT = 0, 10, 20, 30, 40, 50, 60
 PLANES = 64
-AT_THREE = 80
-AT_PAIR = AT_THREE + 30
+AT_ONE = 40
+AT_PAIR = AT_ONE + 10
 AT_FLAT = AT_PAIR + 60
 AT_SUM = AT_FLAT + 29
-AT_SLAB = AT_SUM + 15
+AT_SLAB = AT_SUM + 21
 AT_NINE = AT_SLAB + 64
-ROW_SLAB = AT_NINE + 10
+ROW_SLAB = AT_NINE + 8
 FLAT_ROWS = ((0, 8), (8, 7), (15, 7), (22, 7))
 STRIDE = 11
 SLABS = 4
@@ -239,14 +239,17 @@
         ):
             lo[p + k, 8:24, :] = x
             hi[p + k, 0:16, :] = y
+            if q < 3:
+                lo[p + k, 0:8, :] = jnp.zeros((8, COLS), F32)
+                hi[p + k, 16:24, :] = jnp.zeros((8, COLS), F32)
             south.level(q, k, x[0:8])
             north.level(q, k, y[8:16])
             if q < 2:
                 ninth.level(q, k, jnp.where(sub == 0, x[8:9], y[7:8]))
             if q < 2:
-                lay(4 * (p + k), x[0:4], y[12:16], sign * turned(y[8:16])[0:4])
+                lay(2 * (p + k), x[0:2], y[14:16], sign * turned(y[8:16])[0:2])
             elif q == 2:
-                lay(AT_THREE + 3 * k, x[0:3], y[13:16], turned(y[8:16])[0:3])
+                lay(AT_ONE + k, x[0:1], y[15:16], turned(y[8:16])[0:1])
         south.tracers(k, low[2][0:8], low[3][0:8])
         north.tracers(k, high[2][8:16], high[3][8:16])
         for n, (x, y) in enumerate(((low[2], high[2]), (low[3], high[3]), (wl, wh))):
@@ -261,7 +264,7 @@
     down = own_tile(lambda p, d: lo[p, 8 + d : 16 + d, :], rotation_scale * flat[3, 0:8, :], *none)
     up = own_tile(lambda p, d: hi[p, 8 + d : 16 + d, :], rotation_scale * flat[3, ROWS - 8 : ROWS, :], *none)
     for n, sign in enumerate((-1.0, -1.0, 1.0)):
-        lay(AT_SUM + 5 * n, down[2 + n][2:7], up[2 + n][1:6], sign * turned(up[2 + n])[2:7])
+        lay(AT_SUM + 7 * n, down[2 + n][0:7], up[2 + n][1:8], sign * turned(up[2 + n])[0:7])
     for side, (downs, ups, others) in enumerate(((south.east, north.east, north.west), (south.west, north.west, north.east))):
         source, signs = sources[side]
         for q in range(SLABS):
@@ -402,43 +405,53 @@
 
     lax.fori_loop(0, FLAT, place, 0)
 
-    for p in range(20):
-        lo, hi = both(4 * p, 4)
-        low[p, 12:16, :] = lo
-        high[p, 16:20, :] = hi
-    for k in range(LEVELS):
-        lo, hi = both(AT_THREE + 3 * k, 3)
-        low[D + k, 13:16, :] = lo
-        high[D + k, 16:19, :] = hi
-    for n, p in enumerate((T, S, WET)):
+    def clear(p, carry):
+        low[p, 8:16, :] = jnp.zeros((8, COLS), F32)
+        high[p, 16:24, :] = jnp.zeros((8, COLS), F32)
+        return carry
+
+    lax.fori_loop(0, 40, clear, 0)
+
+    def pair(n, p):
         for k in range(LEVELS):
             lo, hi = both(AT_PAIR + 20 * n + 2 * k, 2)
             low[p + k, 14:16, :] = lo
             high[p + k, 16:18, :] = hi
-    lo, hi = both(AT_FLAT + FLAT_ROWS[3][0], 7)
-    low[FLAT, 9:16, :] = lo
-    high[FLAT, 16:23, :] = hi
-    for n, (ref, r0, spin) in enumerate((
-        (low, 16, x_ref[FLAT + 3, 0:8, :]),
-        (high, 8, x_ref[FLAT + 3, ROWS - 8 : ROWS, :]),
-        (low, 8, low[FLAT, 8:16, :]),
-        (high, 16, high[FLAT, 16:24, :]),
-    )):
+
+    def tile(n, ref, r0, spin, puts):
+        got = own_tile(lambda p, d: ref[p, r0 + d : r0 + d + 8, :], rotation_scale * spin, *puts)
+        for m in range(5):
+            sums[m, 8 * n : 8 * n + 8, :] = got[m]
+
+    pair(2, WET)
+    none = jnp.zeros((8, COLS), F32)
+    for n, ref, r0 in ((2, low, 8), (3, high, 16)):
+        tile(n, ref, r0, none, [None] * 4)
+    for m in (2, 3, 4):
+        lo, hi = both(AT_SUM + 7 * (m - 2), 7)
+        if m < 4:
+            lo = lo + sums[m, 17:24, :]
+            hi = hi + sums[m, 24:31, :]
+        sums[m, 17:24, :] = lo
+        sums[m, 24:31, :] = hi
+    for p in range(20):
+        lo, hi = both(2 * p, 2)
+        low[p, 14:16, :] = lo
+        high[p, 16:18, :] = hi
+    for k in range(LEVELS):
+        lo, hi = both(AT_ONE + k, 1)
+        low[D + k, 15:16, :] = lo
+        high[D + k, 16:17, :] = hi
+    pair(0, T)
+    pair(1, S)
+    for n, ref, r0, row in ((0, low, 16, 0), (1, high, 8, ROWS - 8)):
         def store(out):
             def put(k, val):
                 out[k, 8 * n : 8 * n + 8, :] = val
 
             return put
 
-        puts = [store(out) for out in (us, vs, tn, sn)] if n < 2 else [None] * 4
-        got = own_tile(lambda p, d: ref[p, r0 + d : r0 + d + 8, :], rotation_scale * spin, *puts)
-        for m in range(5):
-            at = 8 * n
-            sums[m, at : at + 8, :] = got[m]
-            if n >= 2 and m >= 2:
-                lo, hi = both(AT_SUM + 5 * (m - 2), 5)
-                first = at + 1 if n == 2 else at + 2
-                sums[m, first : first + 5, :] = lo if n == 2 else hi
+        tile(n, ref, r0, x_ref[FLAT + 3, row : row + 8, :], [store(out) for out in (us, vs, tn, sn)])
 
 
 class Wide:
@@ -737,7 +750,7 @@
     far, near = call(pack_rims, [(COLUMN_SLAB, COLS)] * 2, [], 1_000_000, a, b, ec, wc)
     far_got = lax.ppermute(far, "lon", partners(1, lons))
     near_got = lax.ppermute(near, "lon", partners(0, lons))
-    window = vmem((FLAT + 1, 32, COLS), F32)
+    window = vmem((FLAT, 32, COLS), F32)
     us2, vs2, tn2, sn2, sums2 = call(
         edges, [(LEVELS, 16, COLS)] * 4 + [(5, 32, COLS)], [window] * 2, 10_000_000, x, a, b,
     )

time: 28.3 us -> 27.1 us (0.958)
  waiting for transfers between devices: 4.18 us -> 2.75 us
    ppermute x1, waiting for transfers between devices: 2.3 us -> 1.1 us  [local(): b = lax.ppermute(b, ('lon', 'lat'), colour(1, lats, lons))]
  transfers between devices with their start and end apart: 4 -> 4, of which waited for: 2 -> 2; matrix products, arithmetic and copies ran while one was open for 0% -> 0% of each run, Pallas kernels for 21% -> 22%
where the time goes in v6:
time: 27.1 us; the launch traced here: 26.9 us
  Pallas kernels  12.2 us (45%)
  starting transfers between devices  11.3 us (42%)
  waiting for transfers between devices  2.75 us (10%)
  between operations  0.68 us (3%)
    pallas_call x5, Pallas kernels, call(): pl.pallas_call(kernel, out_shape=[jax.ShapeDtypeStruct(s, F32) for s in o...  12.2 us
    ppermute x1, starting transfers between devices, local(): b = lax.ppermute(b, ('lon', 'lat'), colour(1, lats, lons))  6.91 us
    ppermute x1, starting transfers between devices, local(): far_got = lax.ppermute(far, 'lon', partners(1, lons))  3.61 us
    ppermute x1, waiting for transfers between devices, local(): far_got = lax.ppermute(far, 'lon', partners(1, lons))  1.64 us
    ppermute x1, waiting for transfers between devices, local(): b = lax.ppermute(b, ('lon', 'lat'), colour(1, lats, lons))  1.1 us
    ppermute x1, starting transfers between devices, local(): a = lax.ppermute(a, ('lon', 'lat'), colour(0, lats, lons))  0.83 us
  transfers between devices with their start and end apart: 4, of which 2 were waited for; matrix products, arithmetic and copies ran while one was open for 0% of the time, Pallas kernels for 22%

profile of v6, /device:TPU:30, one launch (start us, length us, event | category | flops | bytes accessed | tf_op | source)
XLA Modules:
  0.0 26.9 jit_solution(961483247385201391)
XLA Ops:
  0.6 2.1 %shard_map.154 = (f32[232,128]{1,0:T(8,128)S(1)}, f32[232,128]{1,0:T(8,128)S(1)}) custom-call(f32[10,64,128]{2,1,0:T(8,128)} %u.3, f32[10,64,128]{2,1,0:T(8,128)} %v.3, f32[10,64,128]{2,1,0:T(8,128)} %t.3, f32[10,64,128]{2,1,0:T(8,128)} %s.3, s32[10,64,128]{2,1,0:T(8,128)} %w.3, s32[64,128]{1,0:T(8,128)} %bottom.3, f32[64,128]{1,0:T(8,128)} %eta.3, ...), custom_call_target="tpu_custom_call" | custom-call | flops 1000000 | bytes 2000000 | tf_op jit(solution)/shard_map/pallas_call | solution.py:50
  2.7 0.8 %collective-permute-start = (f32[232,128]{1,0:T(8,128)S(1)}, f32[232,128]{1,0:T(8,128)S(1)}, u32[]{:S(2)}, u32[]{:S(2)}) collective-permute-start(f32[232,128]{1,0:T(8,128)S(1)} %get-tuple-element.26), channel_id=1, source_target_pairs={{0,1},{16,17},{32,33},{48,49},{64,65},{80,81},{96,97},{112,113},{1... | collective-permute-start | bytes 356360 | tf_op jit(solution)/shard_map/ppermute | solution.py:744
  3.6 6.9 %collective-permute-start.1 = (f32[232,128]{1,0:T(8,128)S(1)}, f32[232,128]{1,0:T(8,128)S(1)}, u32[]{:S(2)}, u32[]{:S(2)}) collective-permute-start(f32[232,128]{1,0:T(8,128)S(1)} %get-tuple-element.27), channel_id=1, source_target_pairs={{1,2},{17,18},{33,34},{49,50},{65,66},{81,82},{97,98},{113,114},{1... | collective-permute-start | bytes 356360 | tf_op jit(solution)/shard_map/ppermute | solution.py:743
  10.5 4.7 %shard_map.153 = (f32[64,64,128]{2,1,0:T(8,128)S(1)}, f32[4,64,128]{2,1,0:T(8,128)S(1)}, f32[4,64,128]{2,1,0:T(8,128)S(1)}, f32[10,64,128]{2,1,0:T(8,128)S(1)}, ...) custom-call(f32[10,64,128]{2,1,0:T(8,128)} %u.3, ...), custom_call_target="tpu_custom_call" | custom-call | flops 20000000 | bytes 2000000 | tf_op jit(solution)/shard_map/pallas_call | solution.py:50
  15.1 0.0 collective-permute-done.a_ref
  15.1 1.1 %collective-permute-done.1.b_ref = f32[232,128]{1,0:T(8,128)S(1)} collective-permute-done((f32[232,128]{1,0:T(8,128)S(1)}, f32[232,128]{1,0:T(8,128)S(1)}, u32[]{:S(2)}, u32[]{:S(2)}) %collective-permute-start.1) | collective-permute-done | bytes 118816 | tf_op jit(solution)/shard_map/ppermute | solution.py:743
  16.3 3.6 %collective-permute-start.2 = (f32[328,128]{1,0:T(8,128)S(1)}, f32[328,128]{1,0:T(8,128)S(1)}, u32[]{:S(2)}, u32[]{:S(2)}) collective-permute-start(f32[328,128]{1,0:T(8,128)S(1)} %get-tuple-element.30.far_mine), channel_id=1, source_target_pairs={{16,32},{32,16},{48,64},{64,48},{80,96},{96,80},{112,128},{128,112... | collective-permute-start | bytes 503816 | tf_op jit(solution)/shard_map/ppermute | solution.py:751
  19.9 0.0 collective-permute-start.3
  19.9 1.4 %shard_map.156 = (f32[10,16,128]{2,1,0:T(8,128)S(1)}, f32[10,16,128]{2,1,0:T(8,128)S(1)}, f32[10,16,128]{2,1,0:T(8,128)S(1)}, f32[10,16,128]{2,1,0:T(8,128)S(1)}, f32[5,32,128]{2,1,0:T(8,128)S(1)}) custom-call(f32[64,64,128]{2,1,0:T(8,128)S(1)} %get-tuple-element.25.x_ref, f32[232,128]{1,0:T(8,128)S(1)} %collective-permute-done.a_ref, ...), custom_call_target="tpu_custom_call" | custom-call | flops 10000000 | bytes 2000000 | tf_op jit(solution)/shard_map/pallas_call | solution.py:50
  21.3 1.6 %collective-permute-done.2.far_got = f32[328,128]{1,0:T(8,128)S(1)} collective-permute-done((f32[328,128]{1,0:T(8,128)S(1)}, f32[328,128]{1,0:T(8,128)S(1)}, u32[]{:S(2)}, u32[]{:S(2)}) %collective-permute-start.2) | collective-permute-done | bytes 167968 | tf_op jit(solution)/shard_map/ppermute | solution.py:751
  22.9 0.0 collective-permute-done.3.near_got
  23.0 4.0 %shard_map.157 = (f32[10,64,128]{2,1,0:T(8,128)}, f32[10,64,128]{2,1,0:T(8,128)}, f32[10,64,128]{2,1,0:T(8,128)}, f32[10,64,128]{2,1,0:T(8,128)}, f32[64,128]{1,...) custom-call(f32[64,64,128]{2,1,0:T(8,128)S(1)} %get-tuple-element.25.x_ref, f32[232,128]{1,0:T(8,128)S(1)} %collective-permute-done.a_ref, ...), custom_call_target="tpu_custom_call" | custom-call | flops 50000000 | bytes 2000000 | tf_op jit(solution)/shard_map/pallas_call | solution.py:50
  (1 shorter events, 0.0 us)
Async XLA Ops:
  2.7 12.4 %collective-permute-start = (f32[232,128]{1,0:T(8,128)S(1)}, f32[232,128]{1,0:T(8,128)S(1)}, u32[]{:S(2)}, u32[]{:S(2)}) collective-permute-start(f32[232,128]{1,0:T(8,128)S(1)} %get-tuple-element.26), channel_id=1, source_target_pairs={{0,1},{16,17},{32,33},{48,49},{64,65},{80,81},{96,97},{112,113},{1... | collective-permute-start | bytes 356360 | tf_op jit(solution)/shard_map/ppermute | solution.py:744
  3.6 12.7 %collective-permute-start.1 = (f32[232,128]{1,0:T(8,128)S(1)}, f32[232,128]{1,0:T(8,128)S(1)}, u32[]{:S(2)}, u32[]{:S(2)}) collective-permute-start(f32[232,128]{1,0:T(8,128)S(1)} %get-tuple-element.27), channel_id=1, source_target_pairs={{1,2},{17,18},{33,34},{49,50},{65,66},{81,82},{97,98},{113,114},{1... | collective-permute-start | bytes 356360 | tf_op jit(solution)/shard_map/ppermute | solution.py:743
  16.3 6.7 %collective-permute-start.2 = (f32[328,128]{1,0:T(8,128)S(1)}, f32[328,128]{1,0:T(8,128)S(1)}, u32[]{:S(2)}, u32[]{:S(2)}) collective-permute-start(f32[328,128]{1,0:T(8,128)S(1)} %get-tuple-element.30.far_mine), channel_id=1, source_target_pairs={{16,32},{32,16},{48,64},{64,48},{80,96},{96,80},{112,128},{128,112... | collective-permute-start | bytes 503816 | tf_op jit(solution)/shard_map/ppermute | solution.py:751
  19.9 3.1 %collective-permute-start.3 = (f32[328,128]{1,0:T(8,128)S(1)}, f32[328,128]{1,0:T(8,128)S(1)}, u32[]{:S(2)}, u32[]{:S(2)}) collective-permute-start(f32[328,128]{1,0:T(8,128)S(1)} %get-tuple-element.31.near_mine), channel_id=1, source_target_pairs={{0,16},{16,0},{32,48},{48,32},{64,80},{80,64},{96,112},{112,96},{1... | collective-permute-start | bytes 503816 | tf_op jit(solution)/shard_map/ppermute | solution.py:752

commit v7 on v6

--- a/solution.py
+++ b/solution.py
@@ -683,24 +683,23 @@
         second.append(pltpu.make_async_copy(flats.at[n], dst, sem.at[2 + n]))
         second[-1].start()
 
-    def flow_tile(rows, fixed, refs, src):
-        gain = (own[1, fixed, :] - mu[fixed, :], own[2, fixed, :] - mv[fixed, :])
-        for k in range(LEVELS):
-            wet = x_ref[WET + k, rows, :]
-            for n, (ref, out) in enumerate(zip(refs, (u_new, v_new))):
-                out[k, rows, :] = ref[k, src, :] + mend(n, k, fixed) + wet * gain[n]
-
-    def flow_loop(i, carry):
-        rows, fixed = tile_of(i)
-        flow_tile(rows, fixed, (us, vs), rows)
-        return carry
-
-    lax.fori_loop(1, ROWS // 8 - 1, flow_loop, 0)
-    for n, i in enumerate((0, ROWS // 8 - 1)):
-        flow_tile(slice(8 * i, 8 * i + 8), slice(8 * i + TOP, 8 * i + TOP + 8), (us2, vs2), slice(8 * n, 8 * n + 8))
-    last = [pltpu.make_async_copy(src, dst, sem.at[5 + n]) for n, (src, dst) in enumerate(((u_new, u_out), (v_new, v_out)))]
-    for copy in last:
-        copy.start()
+    last = []
+    for n, (base, edge_base, mean, out, dst) in enumerate(((us, us2, mu, u_new, u_out), (vs, vs2, mv, v_new, v_out))):
+        def flow_tile(rows, fixed, ref, src):
+            gain = own[1 + n, fixed, :] - mean[fixed, :]
+            for k in range(LEVELS):
+                out[k, rows, :] = ref[k, src, :] + mend(n, k, fixed) + x_ref[WET + k, rows, :] * gain
+
+        def flow_loop(i, carry):
+            rows, fixed = tile_of(i)
+            flow_tile(rows, fixed, base, rows)
+            return carry
+
+        lax.fori_loop(1, ROWS // 8 - 1, flow_loop, 0)
+        for m, i in enumerate((0, ROWS // 8 - 1)):
+            flow_tile(slice(8 * i, 8 * i + 8), slice(8 * i + TOP, 8 * i + TOP + 8), edge_base, slice(8 * m, 8 * m + 8))
+        last.append(pltpu.make_async_copy(out, dst, sem.at[5 + n]))
+        last[-1].start()
     for copy in first + second + last:
         copy.wait()
 

time: 27.1 us -> 27.4 us (1.011)
    pallas_call x5, Pallas kernels: 12.2 us -> 12.4 us  [call(): pl.pallas_call(kernel, out_shape=[jax.ShapeDtypeStruct(s, F32) for s in o...]
where the time goes in v7:
time: 27.4 us; the launch traced here: 27.2 us
  Pallas kernels  12.4 us (45%)
  starting transfers between devices  11.3 us (41%)
  waiting for transfers between devices  2.75 us (10%)
  between operations  0.68 us (2%)
    pallas_call x5, Pallas kernels, call(): pl.pallas_call(kernel, out_shape=[jax.ShapeDtypeStruct(s, F32) for s in o...  12.4 us
    ppermute x1, starting transfers between devices, local(): b = lax.ppermute(b, ('lon', 'lat'), colour(1, lats, lons))  6.91 us
    ppermute x1, starting transfers between devices, local(): far_got = lax.ppermute(far, 'lon', partners(1, lons))  3.61 us
    ppermute x1, waiting for transfers between devices, local(): far_got = lax.ppermute(far, 'lon', partners(1, lons))  1.64 us
    ppermute x1, waiting for transfers between devices, local(): b = lax.ppermute(b, ('lon', 'lat'), colour(1, lats, lons))  1.1 us
    ppermute x1, starting transfers between devices, local(): a = lax.ppermute(a, ('lon', 'lat'), colour(0, lats, lons))  0.83 us
  transfers between devices with their start and end apart: 4, of which 2 were waited for; matrix products, arithmetic and copies ran while one was open for 0% of the time, Pallas kernels for 22%

profile of v7, /device:TPU:30, one launch (start us, length us, event | category | flops | bytes accessed | tf_op | source)
XLA Modules:
  0.0 27.2 jit_solution(13059488576038936232)
XLA Ops:
  0.6 2.1 %shard_map.154 = (f32[232,128]{1,0:T(8,128)S(1)}, f32[232,128]{1,0:T(8,128)S(1)}) custom-call(f32[10,64,128]{2,1,0:T(8,128)} %u.3, f32[10,64,128]{2,1,0:T(8,128)} %v.3, f32[10,64,128]{2,1,0:T(8,128)} %t.3, f32[10,64,128]{2,1,0:T(8,128)} %s.3, s32[10,64,128]{2,1,0:T(8,128)} %w.3, s32[64,128]{1,0:T(8,128)} %bottom.3, f32[64,128]{1,0:T(8,128)} %eta.3, ...), custom_call_target="tpu_custom_call" | custom-call | flops 1000000 | bytes 2000000 | tf_op jit(solution)/shard_map/pallas_call | solution.py:50
  2.7 0.8 %collective-permute-start = (f32[232,128]{1,0:T(8,128)S(1)}, f32[232,128]{1,0:T(8,128)S(1)}, u32[]{:S(2)}, u32[]{:S(2)}) collective-permute-start(f32[232,128]{1,0:T(8,128)S(1)} %get-tuple-element.26), channel_id=1, source_target_pairs={{0,1},{16,17},{32,33},{48,49},{64,65},{80,81},{96,97},{112,113},{1... | collective-permute-start | bytes 356360 | tf_op jit(solution)/shard_map/ppermute | solution.py:743
  3.6 6.9 %collective-permute-start.1 = (f32[232,128]{1,0:T(8,128)S(1)}, f32[232,128]{1,0:T(8,128)S(1)}, u32[]{:S(2)}, u32[]{:S(2)}) collective-permute-start(f32[232,128]{1,0:T(8,128)S(1)} %get-tuple-element.27), channel_id=1, source_target_pairs={{1,2},{17,18},{33,34},{49,50},{65,66},{81,82},{97,98},{113,114},{1... | collective-permute-start | bytes 356360 | tf_op jit(solution)/shard_map/ppermute | solution.py:742
  10.5 4.7 %shard_map.153 = (f32[64,64,128]{2,1,0:T(8,128)S(1)}, f32[4,64,128]{2,1,0:T(8,128)S(1)}, f32[4,64,128]{2,1,0:T(8,128)S(1)}, f32[10,64,128]{2,1,0:T(8,128)S(1)}, ...) custom-call(f32[10,64,128]{2,1,0:T(8,128)} %u.3, ...), custom_call_target="tpu_custom_call" | custom-call | flops 20000000 | bytes 2000000 | tf_op jit(solution)/shard_map/pallas_call | solution.py:50
  15.1 0.0 collective-permute-done.a_ref
  15.1 1.1 %collective-permute-done.1.b_ref = f32[232,128]{1,0:T(8,128)S(1)} collective-permute-done((f32[232,128]{1,0:T(8,128)S(1)}, f32[232,128]{1,0:T(8,128)S(1)}, u32[]{:S(2)}, u32[]{:S(2)}) %collective-permute-start.1) | collective-permute-done | bytes 118816 | tf_op jit(solution)/shard_map/ppermute | solution.py:742
  16.3 3.6 %collective-permute-start.2 = (f32[328,128]{1,0:T(8,128)S(1)}, f32[328,128]{1,0:T(8,128)S(1)}, u32[]{:S(2)}, u32[]{:S(2)}) collective-permute-start(f32[328,128]{1,0:T(8,128)S(1)} %get-tuple-element.30.far_mine), channel_id=1, source_target_pairs={{16,32},{32,16},{48,64},{64,48},{80,96},{96,80},{112,128},{128,112... | collective-permute-start | bytes 503816 | tf_op jit(solution)/shard_map/ppermute | solution.py:750
  19.9 0.0 collective-permute-start.3
  19.9 1.4 %shard_map.156 = (f32[10,16,128]{2,1,0:T(8,128)S(1)}, f32[10,16,128]{2,1,0:T(8,128)S(1)}, f32[10,16,128]{2,1,0:T(8,128)S(1)}, f32[10,16,128]{2,1,0:T(8,128)S(1)}, f32[5,32,128]{2,1,0:T(8,128)S(1)}) custom-call(f32[64,64,128]{2,1,0:T(8,128)S(1)} %get-tuple-element.25.x_ref, f32[232,128]{1,0:T(8,128)S(1)} %collective-permute-done.a_ref, ...), custom_call_target="tpu_custom_call" | custom-call | flops 10000000 | bytes 2000000 | tf_op jit(solution)/shard_map/pallas_call | solution.py:50
  21.3 1.6 %collective-permute-done.2.far_got = f32[328,128]{1,0:T(8,128)S(1)} collective-permute-done((f32[328,128]{1,0:T(8,128)S(1)}, f32[328,128]{1,0:T(8,128)S(1)}, u32[]{:S(2)}, u32[]{:S(2)}) %collective-permute-start.2) | collective-permute-done | bytes 167968 | tf_op jit(solution)/shard_map/ppermute | solution.py:750
  22.9 0.0 collective-permute-done.3.near_got
  23.0 4.3 %shard_map.157 = (f32[10,64,128]{2,1,0:T(8,128)}, f32[10,64,128]{2,1,0:T(8,128)}, f32[10,64,128]{2,1,0:T(8,128)}, f32[10,64,128]{2,1,0:T(8,128)}, f32[64,128]{1,...) custom-call(f32[64,64,128]{2,1,0:T(8,128)S(1)} %get-tuple-element.25.x_ref, f32[232,128]{1,0:T(8,128)S(1)} %collective-permute-done.a_ref, ...), custom_call_target="tpu_custom_call" | custom-call | flops 50000000 | bytes 2000000 | tf_op jit(solution)/shard_map/pallas_call | solution.py:50
  (1 shorter events, 0.0 us)
Async XLA Ops:
  2.7 12.4 %collective-permute-start = (f32[232,128]{1,0:T(8,128)S(1)}, f32[232,128]{1,0:T(8,128)S(1)}, u32[]{:S(2)}, u32[]{:S(2)}) collective-permute-start(f32[232,128]{1,0:T(8,128)S(1)} %get-tuple-element.26), channel_id=1, source_target_pairs={{0,1},{16,17},{32,33},{48,49},{64,65},{80,81},{96,97},{112,113},{1... | collective-permute-start | bytes 356360 | tf_op jit(solution)/shard_map/ppermute | solution.py:743
  3.6 12.7 %collective-permute-start.1 = (f32[232,128]{1,0:T(8,128)S(1)}, f32[232,128]{1,0:T(8,128)S(1)}, u32[]{:S(2)}, u32[]{:S(2)}) collective-permute-start(f32[232,128]{1,0:T(8,128)S(1)} %get-tuple-element.27), channel_id=1, source_target_pairs={{1,2},{17,18},{33,34},{49,50},{65,66},{81,82},{97,98},{113,114},{1... | collective-permute-start | bytes 356360 | tf_op jit(solution)/shard_map/ppermute | solution.py:742
  16.3 6.7 %collective-permute-start.2 = (f32[328,128]{1,0:T(8,128)S(1)}, f32[328,128]{1,0:T(8,128)S(1)}, u32[]{:S(2)}, u32[]{:S(2)}) collective-permute-start(f32[328,128]{1,0:T(8,128)S(1)} %get-tuple-element.30.far_mine), channel_id=1, source_target_pairs={{16,32},{32,16},{48,64},{64,48},{80,96},{96,80},{112,128},{128,112... | collective-permute-start | bytes 503816 | tf_op jit(solution)/shard_map/ppermute | solution.py:750
  19.9 3.1 %collective-permute-start.3 = (f32[328,128]{1,0:T(8,128)S(1)}, f32[328,128]{1,0:T(8,128)S(1)}, u32[]{:S(2)}, u32[]{:S(2)}) collective-permute-start(f32[328,128]{1,0:T(8,128)S(1)} %get-tuple-element.31.near_mine), channel_id=1, source_target_pairs={{0,16},{16,0},{32,48},{48,32},{64,80},{80,64},{96,112},{112,96},{1... | collective-permute-start | bytes 503816 | tf_op jit(solution)/shard_map/ppermute | solution.py:751
